TPU v7x, 256 devices: a whole 4x4x8 slice. The times are simulated.
256 devices in a mesh: leaf: 32 (over x, y, core), mp: 8 (over z).
Axes of the slice: x: 4, y: 4, z: 8, core: 2. Of those that a mesh axis runs over, the one named last changes fastest.
Arguments:
- activations: bfloat16 [8192, 4096], P('leaf', 'mp'), may hold values from -6 to 6
- w_query: bfloat16 [4096, 2048], P(None, 'mp'), may hold values from -0.0625 to 0.0625
- w_key: bfloat16 [4096, 2048], P(None, 'mp'), may hold values from -0.0625 to 0.0625
- w_value: bfloat16 [4096, 2048], P(None, 'mp'), may hold values from -0.09375 to 0.09375
- w_out: bfloat16 [2048, 4096], P('mp'), may hold values from -0.70710678 to 0.70710678
- norm_gain: float32 [4096], P('mp'), may hold values from 0.1 to 1.9
- key_cache: bfloat16 [256, 256, 2048], P('leaf', None, 'mp'), may hold values from -6 to 6
- value_cache: bfloat16 [256, 256, 2048], P('leaf', None, 'mp'), may hold values from -6 to 6
- parent: int32 [256], replicated, may hold values from 0 to 255, as said below
- node_len: int32 [256], replicated, may hold values from 1 to 256, as said below
- req_leaf: int32 [128], replicated, may hold values from 0 to 255, as said below
Outputs:
- layer_out: bfloat16 [8192, 4096], P('leaf', 'mp')
Inputs may be any that keep to these rules, and one draw needn't show every extreme that they name: Exactly 4 nodes are their own parent (the roots); node n's cache is held by leaf index n // 8. Every request's leaf, its parent and that parent's parent are three distinct nodes, the last a root; no request's middle or leaf node is held by a leaf index that holds a root. `node_len`: every root has 256 live rows. `req_leaf`: over the 4 requests of one leaf index, the nodes of their paths counted with repetition lie at most 2 on any one holder, and their middle and leaf nodes at most 2; both bounds are reached on some holder for every leaf index.
All inputs are finite; a program needn't handle non-finite values.
Results may differ from a plain program's by a relative error of at most 0.03.
Values may be sent and summed in bfloat16 or wider, within the bound.
A program may use at most 128 MiB of HBM per device.

v0:
```python
import math

import jax
import jax.numpy as jnp
from jax import lax
from jax.sharding import PartitionSpec as P

D = 4096
HD = 128
TENANTS = 4
NODE_DEV = 8
REQ_LEN = 64
REQ_DEV = 4


rope_base = 500000.0
mask_value = -1e30
norm_eps = 1e-06


def rotate(values, positions):
    half_width = values.shape[-1] // 2
    inverse_freq = jnp.exp(
        jnp.arange(half_width, dtype=jnp.float32) * (-2.0 * math.log(rope_base) / values.shape[-1])
    )
    angles = positions.astype(jnp.float32)[:, None] * inverse_freq[None, :]
    cosine = jnp.cos(angles)[:, None, :]
    sine_part = jnp.sin(angles)[:, None, :]
    front_half = values[..., :half_width]
    back_half = values[..., half_width:]
    return jnp.concatenate(
        [front_half * cosine - back_half * sine_part, back_half * cosine + front_half * sine_part],
        axis=-1,
    )


def route_table(sender_nodes, leaf_count, capacity):
    holders = sender_nodes // NODE_DEV
    item_count = sender_nodes.shape[0]
    earlier = jnp.arange(item_count)[:, None] > jnp.arange(item_count)[None, :]
    same_holder = holders[:, None] == holders[None, :]
    ranks = jnp.sum(earlier & same_holder, axis=1)
    slot_table = (
        jnp.full((leaf_count, capacity), -1, jnp.int32).at[holders, ranks].set(sender_nodes)
    )
    return (holders, ranks, slot_table)


def node_attention(queries, keys, values, lengths, heads_local):
    blocks, row_total, width = queries.shape
    head_dim = width // heads_local
    query_heads = queries.reshape(blocks, row_total, heads_local, head_dim)
    key_heads = keys.reshape(blocks, keys.shape[1], heads_local, head_dim)
    value_heads = values.reshape(blocks, values.shape[1], heads_local, head_dim)
    scores = jnp.einsum(
        "nqhd,nkhd->nhqk", query_heads, key_heads, preferred_element_type=jnp.float32
    ) * head_dim ** (-0.5)
    live_mask = jnp.arange(keys.shape[1])[None, :] < lengths[:, None]
    scores = jnp.where(live_mask[:, None, None, :], scores, mask_value)
    highest = jnp.max(scores, axis=-1)
    weights = jnp.exp(scores - highest[..., None])
    totals = jnp.sum(weights, axis=-1)
    mixture = jnp.einsum(
        "nhqk,nkhd->nqhd",
        weights.astype(jnp.bfloat16),
        value_heads,
        preferred_element_type=jnp.float32,
    )
    result = (
        (mixture / jnp.transpose(totals, (0, 2, 1))[..., None])
        .astype(jnp.bfloat16)
        .reshape(blocks, row_total, width)
    )
    return (result, jnp.transpose(highest + jnp.log(totals), (0, 2, 1)))


def self_attention(queries, keys, values):
    head_dim = queries.shape[-1]
    row_total = queries.shape[1]
    scores = jnp.einsum(
        "rqhd,rkhd->rhqk", queries, keys, preferred_element_type=jnp.float32
    ) * head_dim ** (-0.5)
    causal = jnp.arange(row_total)[:, None] >= jnp.arange(row_total)[None, :]
    scores = jnp.where(causal[None, None], scores, mask_value)
    highest = jnp.max(scores, axis=-1)
    weights = jnp.exp(scores - highest[..., None])
    totals = jnp.sum(weights, axis=-1)
    mixture = jnp.einsum(
        "rhqk,rkhd->rqhd", weights.astype(jnp.bfloat16), values, preferred_element_type=jnp.float32
    )
    return (
        mixture / jnp.transpose(totals, (0, 2, 1))[..., None],
        jnp.transpose(highest + jnp.log(totals), (0, 2, 1)),
    )


def on_device(
    activations,
    w_query,
    w_key,
    w_value,
    w_out,
    norm_gain,
    key_cache,
    value_cache,
    parent,
    node_len,
    req_leaf,
):
    leaf_count = lax.axis_size("leaf")
    device = lax.axis_index("leaf")
    tok_rows = activations.shape[0]
    width_local = w_query.shape[1]
    heads_local = width_local // HD
    spread = leaf_count - TENANTS
    node_slots = 2 * ((REQ_DEV + spread - 1) // spread)
    all_slots = max(REQ_DEV // TENANTS, node_slots)
    columns = lax.all_gather(activations, "mp", axis=1, tiled=True)
    query_f, key_f, value_f = tuple(
        (
            jnp.dot(columns, matrix, preferred_element_type=jnp.float32)
            for matrix in (w_query, w_key, w_value)
        )
    )
    middle_all = parent[req_leaf]
    root_all = parent[middle_all]
    prefix = node_len[root_all] + node_len[middle_all] + node_len[req_leaf]
    mine_prefix = lax.dynamic_slice_in_dim(prefix, device * REQ_DEV, REQ_DEV)
    position = (mine_prefix[:, None] + jnp.arange(REQ_LEN, dtype=jnp.int32)[None, :]).reshape(
        tok_rows
    )
    queries = rotate(query_f.reshape(tok_rows, heads_local, HD), position).astype(jnp.bfloat16)
    keys = rotate(key_f.reshape(tok_rows, heads_local, HD), position).astype(jnp.bfloat16)
    values = value_f.astype(jnp.bfloat16)
    q_blocks = queries.reshape(REQ_DEV, REQ_LEN, width_local)
    self_out, self_lse = self_attention(
        queries.reshape(REQ_DEV, REQ_LEN, heads_local, HD),
        keys.reshape(REQ_DEV, REQ_LEN, heads_local, HD),
        values.reshape(REQ_DEV, REQ_LEN, heads_local, HD),
    )
    levels_all = jnp.stack([root_all, middle_all, req_leaf], axis=0).reshape(3, leaf_count, REQ_DEV)
    level_count = levels_all.shape[0]
    per_sender = jnp.transpose(levels_all, (1, 0, 2)).reshape(leaf_count, level_count * REQ_DEV)
    holders_all, ranks_all, tables = jax.vmap(
        lambda sender_nodes: route_table(sender_nodes, leaf_count, all_slots)
    )(per_sender)
    my_holder = holders_all[device]
    my_rank = ranks_all[device]
    item_request = jnp.arange(level_count * REQ_DEV) % REQ_DEV
    outgoing = (
        jnp.zeros((leaf_count, all_slots, REQ_LEN, width_local), jnp.bfloat16)
        .at[my_holder, my_rank]
        .set(q_blocks[item_request])
    )
    arrived = lax.all_to_all(outgoing, "leaf", split_axis=0, concat_axis=0, tiled=True)
    slot_nodes = tables[:, device].reshape(-1)
    filled = slot_nodes >= 0
    local_slot = jnp.where(filled, slot_nodes - device * NODE_DEV, 0)
    lengths = jnp.where(filled, node_len[jnp.maximum(slot_nodes, 0)], 0)
    node_out, node_lse = node_attention(
        arrived.reshape(leaf_count * all_slots, REQ_LEN, width_local),
        key_cache[local_slot],
        value_cache[local_slot],
        lengths,
        heads_local,
    )
    back_out = lax.all_to_all(
        node_out.reshape(leaf_count, all_slots, REQ_LEN, width_local),
        "leaf",
        split_axis=0,
        concat_axis=0,
        tiled=True,
    )
    back_lse = lax.all_to_all(
        node_lse.reshape(leaf_count, all_slots, REQ_LEN, heads_local).astype(jnp.bfloat16),
        "leaf",
        split_axis=0,
        concat_axis=0,
        tiled=True,
    ).astype(jnp.float32)
    got_out = back_out[my_holder, my_rank].reshape(level_count, REQ_DEV, REQ_LEN, width_local)
    got_lse = back_lse[my_holder, my_rank].reshape(level_count, REQ_DEV, REQ_LEN, heads_local)
    partial_out = jnp.concatenate(
        [got_out.reshape(3, REQ_DEV, REQ_LEN, heads_local, HD).astype(jnp.float32), self_out[None]],
        axis=0,
    )
    partial_lse = jnp.concatenate([got_lse, self_lse[None]], axis=0)
    highest = jnp.max(partial_lse, axis=0)
    factor = jnp.exp(partial_lse - highest[None])
    merged = jnp.sum(factor[..., None] * partial_out, axis=0) / jnp.sum(factor, axis=0)[..., None]
    attn = merged.astype(jnp.bfloat16).reshape(tok_rows, width_local)
    partial_value = jnp.dot(attn, w_out, preferred_element_type=jnp.float32)
    projected = lax.psum_scatter(
        partial_value.astype(jnp.bfloat16), "mp", scatter_dimension=1, tiled=True
    ).astype(jnp.float32)
    squares = lax.psum(jnp.sum(projected * projected, axis=1), "mp")
    row_scale = lax.rsqrt(squares / D + norm_eps)
    return (
        activations.astype(jnp.float32) + norm_gain[None, :] * projected * row_scale[:, None]
    ).astype(jnp.bfloat16)


def solution(mesh):
    in_specs = (
        P("leaf", "mp"),
        P(None, "mp"),
        P(None, "mp"),
        P(None, "mp"),
        P("mp", None),
        P("mp"),
        P("leaf", None, "mp"),
        P("leaf", None, "mp"),
        P(),
        P(),
        P(),
    )
    out_specs = P("leaf", "mp")
    return jax.shard_map(
        on_device, mesh=mesh, in_specs=in_specs, out_specs=out_specs, check_vma=False
    )
```

profile of v0, /device:TPU:6, one launch (start us, length us, event | category | flops | bytes accessed | tf_op | source)
XLA Modules:
  0.0 255.0 jit_solution(10342015116051803166)
XLA Ops:
  6.5 0.7 all-gather.2.cloned.1.call-update
  7.3 0.7 compare_select_fusion.8
  7.9 1.6 gather_fusion.5
  9.6 1.6 gather_fusion
  11.2 1.6 gather_fusion.1
  12.9 1.6 gather_fusion.4
  14.5 0.7 stack.14
  15.5 1.6 gather_fusion.3
  18.2 0.3 multiply_cosine_fusion
  18.5 34.4 %all-gather.2.cloned.1.call-done = bf16[256,4096]{1,0:T(8,128)(2,1)} async-done(((bf16[256,512]{1,0:T(8,128)(2,1)}), bf16[256,4096]{1,0:T(8,128)(2,1)}) %all-gather.2.cloned.1.call-update) | async-done | bytes 2097168 | tf_op jit(solution)/shard_map/all_gather | solution.py:118
  52.9 3.3 %fusion.69 = f32[256,256]{0,1:T(8,128)S(1)} fusion(bf16[256,4096]{1,0:T(8,128)(2,1)} %all-gather.2.cloned.1.call-done, bf16[4096,256]{1,0:T(8,128)(2,1)} %param.13), kind=kOutput, calls=%fused_computation.148 | convolution fusion | flops 536870912 | bytes 4456448 | tf_op jit(solution)/shard_map/dot_general | solution.py:121
  56.4 1.0 fusion.68
  57.7 0.6 gather_fusion.6
  58.3 1.6 broadcast_in_dim.33
  59.9 2.5 scatter_fusion
  62.4 7.5 %all-to-all-start = ((bf16[32,2,64,256]{3,2,1,0:T(8,128)(2,1)}), bf16[32,2,64,256]{3,2,1,0:T(8,128)(2,1)}, u32[]{:S(2)}, u32[]{:S(2)}) async-start(bf16[32,2,64,256]{3,2,1,0:T(8,128)(2,1)} %scatter_fusion), calls=%async_computation | async-start | bytes 4194304 | tf_op jit(solution)/shard_map/all_to_all | solution.py:155
  70.4 24.3 %scatter_fusion.1 = s32[32,32,2]{1,0,2:T(8,128)S(1)} fusion(s32[32,32,2]{1,0,2:T(8,128)S(1)} %broadcast_in_dim.30, s32[384]{0:T(512)S(1)} %reshape.587, s32[384]{0:T(512)S(1)} %reshape.589), kind=kCustom, calls=%fused_computation.12 | custom fusion | bytes 9216 | tf_op jit(solution)/shard_map/vmap()/scatter | solution.py:44
  94.9 0.3 copy.152
  95.3 0.3 copy.153
  95.8 0.8 gather_fusion.2
  96.5 0.3 copy.155
  97.0 5.3 %gather_fusion.7 = bf16[64,256,256]{2,1,0:T(8,128)(2,1)} fusion(bf16[8,256,256]{2,1,0:T(8,128)(2,1)S(1)} %copy-done.2, s32[1024]{0:T(1024)S(1)} %pad_clamp_fusion), kind=kCustom, calls=%fused_computation.7 | custom fusion | bytes 16777472 | tf_op jit(solution)/shard_map/gather | solution.py:162
  102.3 6.5 %gather_fusion.9 = bf16[64,256,256]{2,1,0:T(8,128)(2,1)} fusion(bf16[8,256,256]{2,1,0:T(8,128)(2,1)} %param.18, s32[1024]{0:T(1024)S(1)} %pad_clamp_fusion), kind=kCustom, calls=%fused_computation.9 | custom fusion | bytes 16777472 | tf_op jit(solution)/shard_map/gather | solution.py:163
  108.9 4.0 %reshape_reshape.7 = bf16[64,64,2,128]{3,2,1,0:T(2,128)(2,1)} reshape(bf16[32,2,64,256]{3,2,1,0:T(8,128)(2,1)} %all-to-all-done) | data formatting | bytes 4194304 | tf_op jit(solution)/shard_map/reshape;reshape | solution.py:52
  112.9 7.2 %fusion.6 = (f32[64,2,64]{2,1,0:T(2,128)S(1)}, f32[64,2,64,256]{3,2,1,0:T(8,128)S(1)}) fusion(pred[64,256]{1,0:T(8,128)(4,1)S(1)} %iota_compare_fusion, bf16[64,64,2,128]{3,2,1,0:T(2,128)(2,1)} %reshape_reshape.7, bf16[64,256,256]{2,1,0:T(8,128)(2,1)} %gather_fusion.7), kind=kOutput, calls=%fused_computation.21 | convolution fusion | flops 543154176 | bytes 18923520 | tf_op jit(solution)/shard_map/nqhd,nkhd->nhqk/dot_general | solution.py:55
  120.1 3.6 %fusion.8 = f32[64,2,64]{2,1,0:T(2,128)S(1)} fusion(f32[64,2,64,256]{3,2,1,0:T(8,128)S(1)} %get-tuple-element.25, f32[64,2,64]{2,1,0:T(2,128)S(1)} %get-tuple-element.24, pred[64,256]{1,0:T(8,128)(4,1)S(1)} %iota_compare_fusion), kind=kLoop, calls=%fused_computation.23 | loop fusion | flops 8380416 | bytes 8470528 | tf_op jit(solution)/shard_map/reduce_sum | solution.py:62
  123.7 0.7 reshape.599
  124.4 7.4 %all-to-all-start.1 = ((bf16[32,2,128]{2,1,0:T(2,128)(2,1)}), bf16[32,2,128]{2,1,0:T(2,128)(2,1)S(1)}, u32[]{:S(2)}, u32[]{:S(2)}) async-start(bf16[32,2,128]{2,1,0:T(2,128)(2,1)} %reshape.599), calls=%async_computation.1 | async-start | bytes 32768 | tf_op jit(solution)/shard_map/all_to_all | solution.py:174
  131.8 7.5 %fusion.10 = bf16[64,64,2,128]{3,1,2,0:T(8,128)(2,1)S(1)} fusion(f32[64,64,2]{1,2,0:T(2,128)S(1)} %bitcast.135, f32[64,2,64,256]{3,2,1,0:T(8,128)} %copy-done.3, f32[64,2,64]{2,1,0:T(2,128)S(1)} %get-tuple-element.24, pred[64,256]{1,0:T(8,128)(4,1)S(1)} %iota_compare_fusion, bf16[64,256,256]{2,1,0:T(8,128)(2,1)} %gather_fusion.9), kind=kOutput, calls=%fused_computation.26 | convolution fusion | flops 547356672 | bytes 18956288 | tf_op jit(solution)/shard_map/nhqk,nkhd->nqhd/dot_general | solution.py:63
  139.3 3.5 %copy.167 = bf16[64,64,2,128]{3,2,1,0:T(2,128)(2,1)} copy(bf16[64,64,2,128]{3,1,2,0:T(8,128)(2,1)S(1)} %fusion.10) | data formatting | bytes 4194304 | tf_op jit(solution)/shard_map/convert_element_type | solution.py:71
  142.8 4.4 %reshape_reshape.8 = bf16[32,2,64,256]{3,2,1,0:T(8,128)(2,1)} reshape(bf16[64,64,2,128]{3,2,1,0:T(2,128)(2,1)} %copy.167) | data formatting | bytes 4194304 | tf_op jit(solution)/shard_map/reshape;reshape | solution.py:168
  147.2 7.4 %all-to-all-start.2 = ((bf16[32,2,64,256]{3,2,1,0:T(8,128)(2,1)}), bf16[32,2,64,256]{3,2,1,0:T(8,128)(2,1)}, u32[]{:S(2)}, u32[]{:S(2)}) async-start(bf16[32,2,64,256]{3,2,1,0:T(8,128)(2,1)} %reshape_reshape.8), calls=%async_computation.2 | async-start | bytes 4194304 | tf_op jit(solution)/shard_map/all_to_all | solution.py:167
  155.8 2.9 %convolution_convert_fusion.1 = bf16[256,256]{1,0:T(8,128)(2,1)S(1)} fusion(bf16[256,4096]{1,0:T(8,128)(2,1)} %all-gather.2.cloned.1.call-done, bf16[4096,256]{1,0:T(8,128)(2,1)} %param.14), kind=kOutput, calls=%fused_computation.37 | convolution fusion | flops 536936448 | bytes 4325376 | tf_op jit(solution)/shard_map/dot_general | solution.py:121
  158.8 0.3 fusion.67
  159.2 0.2 fusion.18
  159.4 0.9 copy.170
  160.5 0.7 gather_fusion.8
  161.2 0.2 copy.165
  161.6 19.5 %all-to-all-done.2 = bf16[32,2,64,256]{3,2,1,0:T(8,128)(2,1)} async-done(((bf16[32,2,64,256]{3,2,1,0:T(8,128)(2,1)}), bf16[32,2,64,256]{3,2,1,0:T(8,128)(2,1)}, u32[]{:S(2)}, u32[]{:S(2)}) %all-to-all-start.2) | async-done | bytes 2097184 | tf_op jit(solution)/shard_map/all_to_all | solution.py:167
  181.1 3.0 %gather_fusion.10 = bf16[12,64,256]{2,1,0:T(8,128)(2,1)} fusion(bf16[32,2,64,256]{3,2,1,0:T(8,128)(2,1)} %all-to-all-done.2, s32[12]{0:T(128)S(1)} %get-tuple-element.20), kind=kCustom, calls=%fused_computation.10 | custom fusion | bytes 786528 | tf_op jit(solution)/shard_map/gather | solution.py:181
  184.1 1.4 reshape.496
  185.4 2.3 fusion.23
  187.8 0.3 divide_convert_fusion
  188.1 2.1 convolution_convert_fusion
  190.2 39.9 %reduce-scatter.2.cloned.1.call-done = bf16[256,512]{1,0:T(8,128)(2,1)} async-done(((bf16[256,4096]{1,0:T(8,128)(2,1)}), bf16[256,512]{1,0:T(8,128)(2,1)}) %reduce-scatter.2.cloned.1.call-update) | async-done | bytes 262160 | tf_op jit(solution)/shard_map/reduce_scatter | solution.py:193
  230.1 1.1 fusion.27
  231.1 15.2 %psum.7 = f32[256]{0:T(256)S(1)} all-reduce(f32[256]{0:T(256)S(1)} %fusion.27), channel_id=1, replica_groups=mesh['leaf'=32,'mp'=8] {'mp'}, use_global_device_ids=true, to_apply=%region_12.13 | all-reduce | flops 256 | bytes 2048 | tf_op jit(solution)/shard_map/psum | solution.py:196
  246.4 1.8 fusion.26
  (87 shorter events, 4.3 us)
Async XLA Ops:
  6.5 181.6 %copy-start = (bf16[256,4096]{1,0:T(8,128)(2,1)S(1)}, bf16[256,4096]{1,0:T(8,128)(2,1)}, u32[]{:S(2)}) copy-start(bf16[256,4096]{1,0:T(8,128)(2,1)} %param.15) | copy-start | bytes 6291460
  6.5 46.4 %all-gather.2.cloned.1.call-start = ((), (), s32[]{:S(2)}) async-start(), calls=%async_computation.4 | async-start | bytes 2359296 | tf_op jit(solution)/shard_map/all_gather | solution.py:118
  52.9 3.3 %copy-start.4 = (bf16[256,4096]{1,0:T(8,128)(2,1)S(1)}, bf16[256,4096]{1,0:T(8,128)(2,1)}, u32[]{:S(2)}) copy-start(bf16[256,4096]{1,0:T(8,128)(2,1)} %all-gather.2.cloned.1.call-done) | copy-start | bytes 6291460
  52.9 3.5 %copy-start.5 = (bf16[4096,256]{1,0:T(8,128)(2,1)S(1)}, bf16[4096,256]{1,0:T(8,128)(2,1)}, u32[]{:S(2)}) copy-start(bf16[4096,256]{1,0:T(8,128)(2,1)} %param.12) | copy-start | bytes 6291460
  62.4 46.5 %all-to-all-start = ((bf16[32,2,64,256]{3,2,1,0:T(8,128)(2,1)}), bf16[32,2,64,256]{3,2,1,0:T(8,128)(2,1)}, u32[]{:S(2)}, u32[]{:S(2)}) async-start(bf16[32,2,64,256]{3,2,1,0:T(8,128)(2,1)} %scatter_fusion), calls=%async_computation | async-start | bytes 4194304 | tf_op jit(solution)/shard_map/all_to_all | solution.py:155
  70.4 25.3 %copy-start.1 = (s32[256]{0:T(256)S(1)}, s32[256]{0:T(256)}, u32[]{:S(2)}) copy-start(s32[256]{0:T(256)} %param.20) | copy-start | bytes 3076
  70.4 26.6 %copy-start.2 = (bf16[8,256,256]{2,1,0:T(8,128)(2,1)S(1)}, bf16[8,256,256]{2,1,0:T(8,128)(2,1)}, u32[]{:S(2)}) copy-start(bf16[8,256,256]{2,1,0:T(8,128)(2,1)} %param.17) | copy-start | bytes 3145732
  120.1 3.6 %copy-start.3 = (f32[64,2,64,256]{3,2,1,0:T(8,128)}, f32[64,2,64,256]{3,2,1,0:T(8,128)S(1)}, u32[]{:S(2)}) copy-start(f32[64,2,64,256]{3,2,1,0:T(8,128)S(1)} %get-tuple-element.25) | copy-start | bytes 25165828
  124.4 22.8 %all-to-all-start.1 = ((bf16[32,2,128]{2,1,0:T(2,128)(2,1)}), bf16[32,2,128]{2,1,0:T(2,128)(2,1)S(1)}, u32[]{:S(2)}, u32[]{:S(2)}) async-start(bf16[32,2,128]{2,1,0:T(2,128)(2,1)} %reshape.599), calls=%async_computation.1 | async-start | bytes 32768 | tf_op jit(solution)/shard_map/all_to_all | solution.py:174
  147.2 33.8 %all-to-all-start.2 = ((bf16[32,2,64,256]{3,2,1,0:T(8,128)(2,1)}), bf16[32,2,64,256]{3,2,1,0:T(8,128)(2,1)}, u32[]{:S(2)}, u32[]{:S(2)}) async-start(bf16[32,2,64,256]{3,2,1,0:T(8,128)(2,1)} %reshape_reshape.8), calls=%async_computation.2 | async-start | bytes 4194304 | tf_op jit(solution)/shard_map/all_to_all | solution.py:167
  154.7 75.4 %reduce-scatter.2.cloned.1.call-start = ((), (), s32[]{:S(2)}) async-start(), calls=%async_computation.5 | async-start | bytes 2359296 | tf_op jit(solution)/shard_map/reduce_scatter | solution.py:193
  185.4 60.9 %copy-start.7 = (f32[512]{0:T(512)S(1)}, f32[512]{0:T(512)}, u32[]{:S(2)}) copy-start(f32[512]{0:T(512)} %param.16) | copy-start | bytes 6148
  187.7 58.6 %copy-start.6 = (bf16[256,512]{1,0:T(8,128)(2,1)S(1)}, bf16[256,512]{1,0:T(8,128)(2,1)}, u32[]{:S(2)}) copy-start(bf16[256,512]{1,0:T(8,128)(2,1)} %param.11) | copy-start | bytes 786436
Sparse Core Ops, SparseCore 0:
  9.1 43.7 all-gather.1
  190.3 39.6 reduce-scatter.1
where the time goes:
time: 256 us; the launch traced here: 255 us
  waiting for transfers between devices  94.5 us (37%)
  local copies, waits for them, and re-layouts  73.6 us (29%)
  matrix products  24.5 us (10%)
  starting transfers between devices  22.4 us (9%)
  blocking collectives  15.2 us (6%)
  between operations  13.9 us (5%)
  other arithmetic  10.8 us (4%)
    reduce_scatter x1, waiting for transfers between devices, on_device(): lax.psum_scatter(partial_value.astype(jnp.bfloat16), 'mp', scatter_dimens...  39.9 us
    all_gather x1, waiting for transfers between devices, on_device(): columns = lax.all_gather(activations, 'mp', axis=1, tiled=True)  34.4 us
    scatter x3, local copies, waits for them, and re-layouts, route_table(): jnp.full((leaf_count, capacity), -1, jnp.int32).at[holders, ranks]  24.5 us
    all_to_all x1, waiting for transfers between devices, on_device(): lax.all_to_all(node_out.reshape(leaf_count, all_slots, REQ_LEN, width_loc...  19.5 us
    psum x1, blocking collectives, on_device(): squares = lax.psum(jnp.sum(projected * projected, axis=1), 'mp')  15.2 us
    dot_general x1, matrix products, node_attention(): jnp.einsum('nhqk,nkhd->nqhd', weights.astype(jnp.bfloat16), value_heads,...  7.53 us
    all_to_all x1, starting transfers between devices, on_device(): lax.all_to_all(outgoing, 'leaf', split_axis=0, concat_axis=0, tiled=True)  7.52 us
    all_to_all x1, starting transfers between devices, on_device(): lax.all_to_all(node_out.reshape(leaf_count, all_slots, REQ_LEN, width_loc...  7.44 us
  transfers between devices with their start and end apart: 5, of which 3 were waited for; matrix products, arithmetic and copies ran while one was open for 28% of the time, Pallas kernels for 0%

commit v1 on v0

--- a/solution.py
+++ b/solution.py
@@ -34,16 +34,9 @@
     )
 
 
-def route_table(sender_nodes, leaf_count, capacity):
-    holders = sender_nodes // NODE_DEV
-    item_count = sender_nodes.shape[0]
-    earlier = jnp.arange(item_count)[:, None] > jnp.arange(item_count)[None, :]
-    same_holder = holders[:, None] == holders[None, :]
-    ranks = jnp.sum(earlier & same_holder, axis=1)
-    slot_table = (
-        jnp.full((leaf_count, capacity), -1, jnp.int32).at[holders, ranks].set(sender_nodes)
-    )
-    return (holders, ranks, slot_table)
+def lookup(table, index):
+    hit = index[..., None] == jnp.arange(table.shape[0], dtype=index.dtype)
+    return jnp.sum(jnp.where(hit, table, 0), axis=-1).astype(table.dtype)
 
 
 def node_attention(queries, keys, values, lengths, heads_local):
@@ -115,6 +108,7 @@
     spread = leaf_count - TENANTS
     node_slots = 2 * ((REQ_DEV + spread - 1) // spread)
     all_slots = max(REQ_DEV // TENANTS, node_slots)
+    block = REQ_LEN * width_local
     columns = lax.all_gather(activations, "mp", axis=1, tiled=True)
     query_f, key_f, value_f = tuple(
         (
@@ -122,9 +116,10 @@
             for matrix in (w_query, w_key, w_value)
         )
     )
-    middle_all = parent[req_leaf]
-    root_all = parent[middle_all]
-    prefix = node_len[root_all] + node_len[middle_all] + node_len[req_leaf]
+    middle_all = lookup(parent, req_leaf)
+    root_all = lookup(parent, middle_all)
+    len_of = lambda nodes: lookup(node_len, nodes)
+    prefix = len_of(root_all) + len_of(middle_all) + len_of(req_leaf)
     mine_prefix = lax.dynamic_slice_in_dim(prefix, device * REQ_DEV, REQ_DEV)
     position = (mine_prefix[:, None] + jnp.arange(REQ_LEN, dtype=jnp.int32)[None, :]).reshape(
         tok_rows
@@ -132,7 +127,7 @@
     queries = rotate(query_f.reshape(tok_rows, heads_local, HD), position).astype(jnp.bfloat16)
     keys = rotate(key_f.reshape(tok_rows, heads_local, HD), position).astype(jnp.bfloat16)
     values = value_f.astype(jnp.bfloat16)
-    q_blocks = queries.reshape(REQ_DEV, REQ_LEN, width_local)
+    q_blocks = queries.reshape(REQ_DEV, block)
     self_out, self_lse = self_attention(
         queries.reshape(REQ_DEV, REQ_LEN, heads_local, HD),
         keys.reshape(REQ_DEV, REQ_LEN, heads_local, HD),
@@ -140,23 +135,33 @@
     )
     levels_all = jnp.stack([root_all, middle_all, req_leaf], axis=0).reshape(3, leaf_count, REQ_DEV)
     level_count = levels_all.shape[0]
-    per_sender = jnp.transpose(levels_all, (1, 0, 2)).reshape(leaf_count, level_count * REQ_DEV)
-    holders_all, ranks_all, tables = jax.vmap(
-        lambda sender_nodes: route_table(sender_nodes, leaf_count, all_slots)
-    )(per_sender)
-    my_holder = holders_all[device]
-    my_rank = ranks_all[device]
-    item_request = jnp.arange(level_count * REQ_DEV) % REQ_DEV
-    outgoing = (
-        jnp.zeros((leaf_count, all_slots, REQ_LEN, width_local), jnp.bfloat16)
-        .at[my_holder, my_rank]
-        .set(q_blocks[item_request])
-    )
+    items = level_count * REQ_DEV
+    per_sender = jnp.transpose(levels_all, (1, 0, 2)).reshape(leaf_count, items)
+    holders = per_sender // NODE_DEV
+    earlier = jnp.arange(items)[:, None] > jnp.arange(items)[None, :]
+    ranks = jnp.sum(
+        earlier[None] & (holders[:, :, None] == holders[:, None, :]), axis=2
+    ).astype(jnp.int32)
+    slot_ids = jnp.arange(all_slots, dtype=jnp.int32)
+    my_holders = lax.dynamic_index_in_dim(holders, device, 0, keepdims=False)
+    my_ranks = lax.dynamic_index_in_dim(ranks, device, 0, keepdims=False)
+    send_hit = (
+        (my_holders[None, None, :] == jnp.arange(leaf_count, dtype=jnp.int32)[:, None, None])
+        & (my_ranks[None, None, :] == slot_ids[None, :, None])
+    )
+    send_item = jnp.sum(jnp.where(send_hit, jnp.arange(items, dtype=jnp.int32), 0), axis=2)
+    send_valid = jnp.any(send_hit, axis=2)
+    outgoing = jnp.where(
+        send_valid.reshape(-1)[:, None],
+        jnp.take(q_blocks, (send_item % REQ_DEV).reshape(-1), axis=0),
+        jnp.zeros((), jnp.bfloat16),
+    ).reshape(leaf_count, all_slots * block)
     arrived = lax.all_to_all(outgoing, "leaf", split_axis=0, concat_axis=0, tiled=True)
-    slot_nodes = tables[:, device].reshape(-1)
-    filled = slot_nodes >= 0
+    recv_hit = (holders[:, None, :] == device) & (ranks[:, None, :] == slot_ids[None, :, None])
+    slot_nodes = jnp.sum(jnp.where(recv_hit, per_sender[:, None, :], 0), axis=2).reshape(-1)
+    filled = jnp.any(recv_hit, axis=2).reshape(-1)
     local_slot = jnp.where(filled, slot_nodes - device * NODE_DEV, 0)
-    lengths = jnp.where(filled, node_len[jnp.maximum(slot_nodes, 0)], 0)
+    lengths = jnp.where(filled, len_of(slot_nodes), 0)
     node_out, node_lse = node_attention(
         arrived.reshape(leaf_count * all_slots, REQ_LEN, width_local),
         key_cache[local_slot],
@@ -164,26 +169,33 @@
         lengths,
         heads_local,
     )
-    back_out = lax.all_to_all(
-        node_out.reshape(leaf_count, all_slots, REQ_LEN, width_local),
+    flat_lse = node_lse.reshape(leaf_count * all_slots, REQ_LEN * heads_local)
+    lse_high = lax.reduce_precision(flat_lse, exponent_bits=8, mantissa_bits=7)
+    lse_low = (flat_lse - lse_high).astype(jnp.bfloat16)
+    payload = jnp.concatenate(
+        [
+            node_out.reshape(leaf_count * all_slots, block),
+            lse_high.astype(jnp.bfloat16),
+            lse_low,
+        ],
+        axis=1,
+    )
+    piece = payload.shape[1]
+    back = lax.all_to_all(
+        payload.reshape(leaf_count, all_slots * piece),
         "leaf",
         split_axis=0,
         concat_axis=0,
         tiled=True,
-    )
-    back_lse = lax.all_to_all(
-        node_lse.reshape(leaf_count, all_slots, REQ_LEN, heads_local).astype(jnp.bfloat16),
-        "leaf",
-        split_axis=0,
-        concat_axis=0,
-        tiled=True,
-    ).astype(jnp.float32)
-    got_out = back_out[my_holder, my_rank].reshape(level_count, REQ_DEV, REQ_LEN, width_local)
-    got_lse = back_lse[my_holder, my_rank].reshape(level_count, REQ_DEV, REQ_LEN, heads_local)
-    partial_out = jnp.concatenate(
-        [got_out.reshape(3, REQ_DEV, REQ_LEN, heads_local, HD).astype(jnp.float32), self_out[None]],
-        axis=0,
-    )
+    ).reshape(leaf_count * all_slots, piece)
+    got = jnp.take(back, my_holders * all_slots + my_ranks, axis=0)
+    got_out = got[:, :block].reshape(level_count, REQ_DEV, REQ_LEN, heads_local, HD)
+    lse_width = REQ_LEN * heads_local
+    got_lse = (
+        got[:, block : block + lse_width].astype(jnp.float32)
+        + got[:, block + lse_width :].astype(jnp.float32)
+    ).reshape(level_count, REQ_DEV, REQ_LEN, heads_local)
+    partial_out = jnp.concatenate([got_out.astype(jnp.float32), self_out[None]], axis=0)
     partial_lse = jnp.concatenate([got_lse, self_lse[None]], axis=0)
     highest = jnp.max(partial_lse, axis=0)
     factor = jnp.exp(partial_lse - highest[None])
@@ -193,7 +205,9 @@
     projected = lax.psum_scatter(
         partial_value.astype(jnp.bfloat16), "mp", scatter_dimension=1, tiled=True
     ).astype(jnp.float32)
-    squares = lax.psum(jnp.sum(projected * projected, axis=1), "mp")
+    squares = jnp.sum(
+        lax.all_gather(jnp.sum(projected * projected, axis=1), "mp", axis=0), axis=0
+    )
     row_scale = lax.rsqrt(squares / D + norm_eps)
     return (
         activations.astype(jnp.float32) + norm_gain[None, :] * projected * row_scale[:, None]

time: 256 us -> 336 us (1.31)
  other arithmetic: 10.8 us -> 69.1 us
  local copies, waits for them, and re-layouts: 73.6 us -> 97.4 us
  starting transfers between devices: 22.4 us -> 15.2 us
  waiting for transfers between devices: 94.5 us -> 98.7 us
    all_to_all x0 -> x3, other arithmetic: none -> 42.3 us  [the longest x2 28.5 us: on_device(): lax.all_to_all(payload.reshape(leaf_count, all_slots * piece), 'leaf', sp...]
    unnamed x18 -> x34, local copies, waits for them, and re-layouts: 0.98 us -> 29.9 us
    scatter x4 -> x0, local copies, waits for them, and re-layouts: 27.1 us -> none  [the longest x3 24.5 us: route_table(): jnp.full((leaf_count, capacity), -1, jnp.int32).at[holders, ranks]]
    psum x1 -> x0, blocking collectives: 15.2 us -> none  [on_device(): squares = lax.psum(jnp.sum(projected * projected, axis=1), 'mp')]
    all_gather x0 -> x1, blocking collectives: none -> 14.6 us  [on_device(): lax.all_gather(jnp.sum(projected * projected, axis=1), 'mp', axis=0)]
    all_to_all x1, waiting for transfers between devices: 0.01 us -> 13.9 us  [on_device(): lax.all_to_all(outgoing, 'leaf', split_axis=0, concat_axis=0, tiled=True)]
    broadcast_in_dim x2 -> x4, local copies, waits for them, and re-layouts: 1.59 us -> 14.9 us  [the longest x2 7.86 us: on_device(): jnp.take(q_blocks, (send_item % REQ_DEV).reshape(-1), axis=0)]
    all_gather x1, waiting for transfers between devices: 34.4 us -> 23.5 us  [on_device(): columns = lax.all_gather(activations, 'mp', axis=1, tiled=True)]
  transfers between devices with their start and end apart: 5 -> 4, of which waited for: 3 -> 4; matrix products, arithmetic and copies ran while one was open for 28% -> 12% of each run, Pallas kernels for 0% -> 0%
where the time goes in v1:
time: 336 us; the launch traced here: 334 us
  waiting for transfers between devices  98.7 us (29%)
  local copies, waits for them, and re-layouts  97.4 us (29%)
  other arithmetic  69.1 us (21%)
  matrix products  24.7 us (7%)
  starting transfers between devices  15.2 us (5%)
  blocking collectives  14.6 us (4%)
  between operations  14 us (4%)
    reduce_scatter x1, waiting for transfers between devices, on_device(): lax.psum_scatter(partial_value.astype(jnp.bfloat16), 'mp', scatter_dimens...  39.6 us
    unnamed x34, local copies, waits for them, and re-layouts  29.9 us
    all_to_all x2, other arithmetic, on_device(): lax.all_to_all(payload.reshape(leaf_count, all_slots * piece), 'leaf', sp...  28.5 us
    all_gather x1, waiting for transfers between devices, on_device(): columns = lax.all_gather(activations, 'mp', axis=1, tiled=True)  23.5 us
    all_to_all x1, waiting for transfers between devices, on_device(): lax.all_to_all(payload.reshape(leaf_count, all_slots * piece), 'leaf', sp...  21 us
    all_gather x1, blocking collectives, on_device(): lax.all_gather(jnp.sum(projected * projected, axis=1), 'mp', axis=0)  14.6 us
    all_to_all x1, waiting for transfers between devices, on_device(): lax.all_to_all(outgoing, 'leaf', split_axis=0, concat_axis=0, tiled=True)  13.9 us
    all_to_all x1, other arithmetic, on_device(): lax.all_to_all(outgoing, 'leaf', split_axis=0, concat_axis=0, tiled=True)  13.8 us
  transfers between devices with their start and end apart: 4, of which 4 were waited for; matrix products, arithmetic and copies ran while one was open for 12% of the time, Pallas kernels for 0%

profile of v1, /device:TPU:6, one launch (start us, length us, event | category | flops | bytes accessed | tf_op | source)
XLA Modules:
  0.0 333.7 jit_solution(5762768848607387060)
XLA Ops:
  7.3 0.8 stack.14
  8.0 0.9 select_reduce_fusion.4
  9.0 0.9 select_reduce_fusion.3
  10.0 0.9 select_reduce_fusion.1
  11.5 0.8 add_reduce_fusion
  13.1 2.5 broadcast_in_dim.178
  15.6 4.5 %broadcast_in_dim.179 = pred[32,1,32768]{2,0,1:T(8,128)(4,1)S(1)} reshape(pred[32,2,16384]{2,1,0:T(4,128)(4,1)} %broadcast_in_dim.178) | data formatting | bytes 2097152 | tf_op jit(solution)/shard_map/jit(_where)/broadcast_in_dim | solution.py:154
  20.4 2.5 broadcast_in_dim.181
  22.9 5.4 %broadcast_in_dim.182 = pred[32,1,32768]{2,0,1:T(8,128)(4,1)} reshape(pred[32,2,16384]{2,1,0:T(4,128)(4,1)} %broadcast_in_dim.181) | data formatting | bytes 2097152 | tf_op jit(solution)/shard_map/jit(_take)/broadcast_in_dim | solution.py:156
  29.5 23.5 %all-gather.4.cloned.1.call-done = bf16[256,4096]{1,0:T(8,128)(2,1)} async-done(((bf16[256,512]{1,0:T(8,128)(2,1)}), bf16[256,4096]{1,0:T(8,128)(2,1)}) %all-gather.4.cloned.1.call-update) | async-done | bytes 2097168 | tf_op jit(solution)/shard_map/all_gather | solution.py:112
  53.0 3.3 fusion.61
  56.5 1.0 fusion.60
  58.4 3.3 gather_fusion.1
  61.6 4.1 %gather.18 = bf16[32,1,32768]{2,0,1:T(8,128)(2,1)} reshape(bf16[64,16384]{1,0:T(8,128)(2,1)} %gather_fusion.1) | data formatting | bytes 4194304 | tf_op jit(solution)/shard_map/jit(_take)/gather | solution.py:156
  65.8 3.6 %select_select_fusion = bf16[32,1,32768]{2,0,1:T(8,128)(2,1)} fusion(pred[32,1,32768]{2,0,1:T(8,128)(4,1)S(1)} %broadcast_in_dim.179, pred[32,1,32768]{2,0,1:T(8,128)(4,1)} %broadcast_in_dim.182, bf16[32,1,32768]{2,0,1:T(8,128)(2,1)} %gather.18), kind=kLoop, calls=%fused_computation.24 | loop fusion | flops 2097152 | bytes 6291456 | tf_op jit(solution)/shard_map/jit(_where)/select_n | solution.py:154
  70.0 4.5 %reduce.11 = bf16[32,32768]{1,0:T(8,128)(2,1)} reduce(bf16[32,1,32768]{2,0,1:T(8,128)(2,1)} %select_select_fusion, bf16[]{:T(256)} %broadcast.415), dimensions={1}, to_apply=%copy.217.reduce_sub_computation | reduce | bytes 4194306 | tf_op jit(solution)/shard_map/jit(_where)/select_n | solution.py:154
  74.5 4.5 %reshape.566 = bf16[32,2,16384]{2,1,0:T(2,128)(2,1)} reshape(bf16[32,32768]{1,0:T(8,128)(2,1)} %reduce.11) | data formatting | bytes 4194304
  79.0 7.7 %all-to-all-start = ((bf16[32,2,16384]{2,1,0:T(2,128)(2,1)}), bf16[32,2,16384]{2,1,0:T(2,128)(2,1)}, u32[]{:S(2)}, u32[]{:S(2)}) async-start(bf16[32,2,16384]{2,1,0:T(2,128)(2,1)} %reshape.566), calls=%async_computation | async-start | bytes 4194304 | tf_op jit(solution)/shard_map/all_to_all | solution.py:159
  87.1 5.3 %gather_fusion.2 = bf16[64,256,256]{2,1,0:T(8,128)(2,1)} fusion(bf16[8,256,256]{2,1,0:T(8,128)(2,1)S(1)} %copy-done.1, s32[1024]{0:T(1024)S(1)} %pad_clamp_fusion.1), kind=kCustom, calls=%fused_computation.2 | custom fusion | bytes 16777472 | tf_op jit(solution)/shard_map/gather | solution.py:167
  92.4 6.5 %gather_fusion = bf16[64,256,256]{2,1,0:T(8,128)(2,1)} fusion(bf16[8,256,256]{2,1,0:T(8,128)(2,1)} %param.18, s32[1024]{0:T(1024)S(1)} %pad_clamp_fusion.1), kind=kCustom, calls=%fused_computation | custom fusion | bytes 16777472 | tf_op jit(solution)/shard_map/gather | solution.py:168
  99.2 13.9 %all-to-all-done = bf16[32,2,16384]{2,1,0:T(2,128)(2,1)} async-done(((bf16[32,2,16384]{2,1,0:T(2,128)(2,1)}), bf16[32,2,16384]{2,1,0:T(2,128)(2,1)}, u32[]{:S(2)}, u32[]{:S(2)}) %all-to-all-start) | async-done | bytes 2097184 | tf_op jit(solution)/shard_map/all_to_all | solution.py:159
  113.1 10.5 %reshape.567 = bf16[32,1,32768]{2,1,0:T(2,128)(2,1)} reshape(bf16[32,2,16384]{2,1,0:T(2,128)(2,1)} %all-to-all-done) | data formatting | bytes 4194304
  123.6 13.8 %reduce.5 = bf16[32,32768]{1,0:T(8,128)(2,1)} reduce(bf16[32,1,32768]{2,1,0:T(2,128)(2,1)} %reshape.567, bf16[]{:T(256)} %constant.103), dimensions={1}, to_apply=%all_to_all.10.reduce_sub_computation | reduce | bytes 4194306 | tf_op jit(solution)/shard_map/all_to_all | solution.py:159
  137.4 4.5 %reshape_reshape.6 = bf16[64,64,2,128]{3,2,1,0:T(2,128)(2,1)} reshape(bf16[32,32768]{1,0:T(8,128)(2,1)} %reduce.5) | data formatting | bytes 4194304 | tf_op jit(solution)/shard_map/reshape;reshape | solution.py:45
  141.9 7.2 %fusion.6 = (f32[64,2,64]{2,1,0:T(2,128)S(1)}, f32[64,2,64,256]{3,2,1,0:T(8,128)S(1)}) fusion(pred[64,256]{1,0:T(8,128)(4,1)S(1)} %iota_compare_fusion.4, bf16[64,64,2,128]{3,2,1,0:T(2,128)(2,1)} %reshape_reshape.6, bf16[64,256,256]{2,1,0:T(8,128)(2,1)} %gather_fusion.2), kind=kOutput, calls=%fused_computation.12 | convolution fusion | flops 543154176 | bytes 18923520 | tf_op jit(solution)/shard_map/nqhd,nkhd->nhqk/dot_general | solution.py:48
  149.1 3.6 %fusion.7 = f32[64,2,64]{2,1,0:T(2,128)S(1)} fusion(f32[64,2,64,256]{3,2,1,0:T(8,128)S(1)} %get-tuple-element.30, f32[64,2,64]{2,1,0:T(2,128)S(1)} %get-tuple-element.29, pred[64,256]{1,0:T(8,128)(4,1)S(1)} %iota_compare_fusion.4), kind=kLoop, calls=%fused_computation.13 | loop fusion | flops 8380416 | bytes 8470528 | tf_op jit(solution)/shard_map/reduce_sum | solution.py:55
  153.0 7.7 %fusion.10 = bf16[64,64,2,128]{3,1,2,0:T(8,128)(2,1)S(1)} fusion(f32[64,64,2]{1,2,0:T(2,128)S(1)} %copy.222, f32[64,2,64,256]{3,2,1,0:T(8,128)} %copy-done.2, f32[64,2,64]{2,1,0:T(2,128)S(1)} %get-tuple-element.29, pred[64,256]{1,0:T(8,128)(4,1)S(1)} %iota_compare_fusion.4, bf16[64,256,256]{2,1,0:T(8,128)(2,1)} %gather_fusion), kind=kOutput, calls=%fused_computation.17 | convolution fusion | flops 547356672 | bytes 18956288 | tf_op jit(solution)/shard_map/nhqk,nkhd->nqhd/dot_general | solution.py:56
  160.7 3.5 %copy.223 = bf16[64,64,2,128]{3,2,1,0:T(2,128)(2,1)} copy(bf16[64,64,2,128]{3,1,2,0:T(8,128)(2,1)S(1)} %fusion.10) | data formatting | bytes 4194304 | tf_op jit(solution)/shard_map/convert_element_type | solution.py:64
  164.2 4.5 %reshape_reshape.7 = bf16[64,16384]{1,0:T(8,128)(2,1)} reshape(bf16[64,64,2,128]{3,2,1,0:T(2,128)(2,1)} %copy.223) | data formatting | bytes 4194304 | tf_op jit(solution)/shard_map/reshape;reshape | solution.py:177
  168.7 3.1 pad_maximum_fusion
  171.7 6.2 %all_to_all.13 = bf16[32,1,33280]{2,1,0:T(2,128)(2,1)} reshape(bf16[64,16640]{1,0:T(8,128)(2,1)} %pad_maximum_fusion) | data formatting | bytes 4259840 | tf_op jit(solution)/shard_map/all_to_all | solution.py:184
  177.9 14.6 %reduce.12 = bf16[32,33280]{1,0:T(8,128)(2,1)} reduce(bf16[32,1,33280]{2,1,0:T(2,128)(2,1)} %all_to_all.13, bf16[]{:T(256)} %broadcast.415), dimensions={1}, to_apply=%all_to_all.13.reduce_sub_computation | reduce | bytes 4259842 | tf_op jit(solution)/shard_map/all_to_all | solution.py:184
  192.5 4.0 %reshape.568 = bf16[32,2,16640]{2,1,0:T(2,128)(2,1)} reshape(bf16[32,33280]{1,0:T(8,128)(2,1)} %reduce.12) | data formatting | bytes 4259840
  196.5 7.4 %all-to-all-start.1 = ((bf16[32,2,16640]{2,1,0:T(2,128)(2,1)}), bf16[32,2,16640]{2,1,0:T(2,128)(2,1)}, u32[]{:S(2)}, u32[]{:S(2)}) async-start(bf16[32,2,16640]{2,1,0:T(2,128)(2,1)} %reshape.568), calls=%async_computation.1 | async-start | bytes 4259840 | tf_op jit(solution)/shard_map/all_to_all | solution.py:184
  205.2 2.9 convolution_convert_fusion.1
  208.8 0.9 copy.241
  209.7 21.0 %all-to-all-done.1 = bf16[32,2,16640]{2,1,0:T(2,128)(2,1)} async-done(((bf16[32,2,16640]{2,1,0:T(2,128)(2,1)}), bf16[32,2,16640]{2,1,0:T(2,128)(2,1)}, u32[]{:S(2)}, u32[]{:S(2)}) %all-to-all-start.1) | async-done | bytes 2129952 | tf_op jit(solution)/shard_map/all_to_all | solution.py:184
  230.7 10.3 %reshape.569 = bf16[32,1,33280]{2,1,0:T(2,128)(2,1)} reshape(bf16[32,2,16640]{2,1,0:T(2,128)(2,1)} %all-to-all-done.1) | data formatting | bytes 4259840
  241.0 13.9 %reduce.6 = bf16[32,33280]{1,0:T(8,128)(2,1)} reduce(bf16[32,1,33280]{2,1,0:T(2,128)(2,1)} %reshape.569, bf16[]{:T(256)} %constant.103), dimensions={1}, to_apply=%all_to_all.12.reduce_sub_computation | reduce | bytes 4259842 | tf_op jit(solution)/shard_map/all_to_all | solution.py:184
  254.9 4.1 %reshape.521 = bf16[64,16640]{1,0:T(8,128)(2,1)} reshape(bf16[32,33280]{1,0:T(8,128)(2,1)} %reduce.6) | data formatting | bytes 4259840 | tf_op jit(solution)/shard_map/reshape | solution.py:190
  259.1 3.0 gather_fusion.3
  262.3 1.5 reshape.524
  265.0 2.3 fusion.23
  267.7 2.1 convolution_convert_fusion
  269.8 39.6 %reduce-scatter.2.cloned.1.call-done = bf16[256,512]{1,0:T(8,128)(2,1)} async-done(((bf16[256,4096]{1,0:T(8,128)(2,1)}), bf16[256,512]{1,0:T(8,128)(2,1)}) %reduce-scatter.2.cloned.1.call-update) | async-done | bytes 262160 | tf_op jit(solution)/shard_map/reduce_scatter | solution.py:205
  309.4 1.1 fusion.27
  310.4 14.6 %all-gather.1 = f32[8,1,256]{2,1,0:T(1,128)S(1)} all-gather(f32[1,1,256]{2,1,0:T(1,128)S(1)} %bitcast.92), channel_id=2, replica_groups=mesh['leaf'=32,'mp'=8] {'mp'}, dimensions={0}, use_global_device_ids=true | all-gather | bytes 9216 | tf_op jit(solution)/shard_map/all_gather | solution.py:209
  325.1 1.8 fusion.26
  (118 shorter events, 9.8 us)
Async XLA Ops:
  6.5 261.1 %copy-start = (bf16[256,4096]{1,0:T(8,128)(2,1)S(1)}, bf16[256,4096]{1,0:T(8,128)(2,1)}, u32[]{:S(2)}) copy-start(bf16[256,4096]{1,0:T(8,128)(2,1)} %param.15) | copy-start | bytes 6291460
  6.5 46.5 %all-gather.4.cloned.1.call-start = ((), (), s32[]{:S(2)}) async-start(), calls=%async_computation.3 | async-start | bytes 2359296 | tf_op jit(solution)/shard_map/all_gather | solution.py:112
  12.3 0.5 copy-start.11
  53.0 3.3 copy-start.3
  53.0 3.5 %copy-start.5 = (bf16[4096,256]{1,0:T(8,128)(2,1)S(1)}, bf16[4096,256]{1,0:T(8,128)(2,1)}, u32[]{:S(2)}) copy-start(bf16[4096,256]{1,0:T(8,128)(2,1)} %param.12) | copy-start | bytes 6291460
  79.0 8.2 %copy-start.13 = (s32[64]{0:T(128)S(1)}, s32[64]{0:T(128)}, u32[]{:S(2)}) copy-start(s32[64]{0:T(128)} %get-tuple-element.31) | copy-start | bytes 772
  79.0 8.2 %copy-start.1 = (bf16[8,256,256]{2,1,0:T(8,128)(2,1)S(1)}, bf16[8,256,256]{2,1,0:T(8,128)(2,1)}, u32[]{:S(2)}) copy-start(bf16[8,256,256]{2,1,0:T(8,128)(2,1)} %param.17) | copy-start | bytes 3145732
  79.0 34.1 %all-to-all-start = ((bf16[32,2,16384]{2,1,0:T(2,128)(2,1)}), bf16[32,2,16384]{2,1,0:T(2,128)(2,1)}, u32[]{:S(2)}, u32[]{:S(2)}) async-start(bf16[32,2,16384]{2,1,0:T(2,128)(2,1)} %reshape.566), calls=%async_computation | async-start | bytes 4194304 | tf_op jit(solution)/shard_map/all_to_all | solution.py:159
  92.4 6.5 %copy-start.9 = (s32[256]{0:T(256)S(1)}, s32[256]{0:T(256)}, u32[]{:S(2)}) copy-start(s32[256]{0:T(256)} %param.20) | copy-start | bytes 3076
  149.1 3.6 %copy-start.2 = (f32[64,2,64,256]{3,2,1,0:T(8,128)}, f32[64,2,64,256]{3,2,1,0:T(8,128)S(1)}, u32[]{:S(2)}) copy-start(f32[64,2,64,256]{3,2,1,0:T(8,128)S(1)} %get-tuple-element.30) | copy-start | bytes 25165828
  196.5 7.5 %copy-start.14 = (s32[12]{0:T(128)S(1)}, s32[12]{0:T(128)}, u32[]{:S(2)}) copy-start(s32[12]{0:T(128)} %get-tuple-element.5) | copy-start | bytes 148
  196.5 7.6 %copy-start.12 = (s32[12]{0:T(128)S(1)}, s32[12]{0:T(128)}, u32[]{:S(2)}) copy-start(s32[12]{0:T(128)} %copy-done.11) | copy-start | bytes 148
  196.5 7.8 %copy-start.8 = (bf16[256,2,64]{0,2,1:T(8,128)(2,1)S(1)}, bf16[256,2,64]{0,2,1:T(8,128)(2,1)}, u32[]{:S(2)}) copy-start(bf16[256,2,64]{0,2,1:T(8,128)(2,1)} %get-tuple-element.16) | copy-start | bytes 196612
  196.5 8.1 %copy-start.7 = (bf16[256,2,64]{0,2,1:T(8,128)(2,1)S(1)}, bf16[256,2,64]{0,2,1:T(8,128)(2,1)}, u32[]{:S(2)}) copy-start(bf16[256,2,64]{0,2,1:T(8,128)(2,1)} %get-tuple-element.15) | copy-start | bytes 196612
  196.5 34.2 %all-to-all-start.1 = ((bf16[32,2,16640]{2,1,0:T(2,128)(2,1)}), bf16[32,2,16640]{2,1,0:T(2,128)(2,1)}, u32[]{:S(2)}, u32[]{:S(2)}) async-start(bf16[32,2,16640]{2,1,0:T(2,128)(2,1)} %reshape.568), calls=%async_computation.1 | async-start | bytes 4259840 | tf_op jit(solution)/shard_map/all_to_all | solution.py:184
  203.9 105.4 %reduce-scatter.2.cloned.1.call-start = ((), (), s32[]{:S(2)}) async-start(), calls=%async_computation.4 | async-start | bytes 2359296 | tf_op jit(solution)/shard_map/reduce_scatter | solution.py:205
  263.9 1.1 copy-start.4
  269.7 55.3 %copy-start.6 = (bf16[256,512]{1,0:T(8,128)(2,1)S(1)}, bf16[256,512]{1,0:T(8,128)(2,1)}, u32[]{:S(2)}) copy-start(bf16[256,512]{1,0:T(8,128)(2,1)} %param.11) | copy-start | bytes 786436
  269.7 55.3 %copy-start.10 = (f32[512]{0:T(512)S(1)}, f32[512]{0:T(512)}, u32[]{:S(2)}) copy-start(f32[512]{0:T(512)} %param.16) | copy-start | bytes 6148
Sparse Core Ops, SparseCore 0:
  9.1 43.8 all-gather.3
  269.9 39.4 reduce-scatter.1

commit v2 on v1

--- a/solution.py
+++ b/solution.py
@@ -3,6 +3,8 @@
 import jax
 import jax.numpy as jnp
 from jax import lax
+from jax.experimental import pallas as pl
+from jax.experimental.pallas import tpu as pltpu
 from jax.sharding import PartitionSpec as P
 
 D = 4096
@@ -39,32 +41,64 @@
     return jnp.sum(jnp.where(hit, table, 0), axis=-1).astype(table.dtype)
 
 
-def node_attention(queries, keys, values, lengths, heads_local):
-    blocks, row_total, width = queries.shape
-    head_dim = width // heads_local
-    query_heads = queries.reshape(blocks, row_total, heads_local, head_dim)
-    key_heads = keys.reshape(blocks, keys.shape[1], heads_local, head_dim)
-    value_heads = values.reshape(blocks, values.shape[1], heads_local, head_dim)
-    scores = jnp.einsum(
-        "nqhd,nkhd->nhqk", query_heads, key_heads, preferred_element_type=jnp.float32
-    ) * head_dim ** (-0.5)
-    live_mask = jnp.arange(keys.shape[1])[None, :] < lengths[:, None]
-    scores = jnp.where(live_mask[:, None, None, :], scores, mask_value)
-    highest = jnp.max(scores, axis=-1)
-    weights = jnp.exp(scores - highest[..., None])
-    totals = jnp.sum(weights, axis=-1)
-    mixture = jnp.einsum(
-        "nhqk,nkhd->nqhd",
-        weights.astype(jnp.bfloat16),
-        value_heads,
-        preferred_element_type=jnp.float32,
-    )
-    result = (
-        (mixture / jnp.transpose(totals, (0, 2, 1))[..., None])
-        .astype(jnp.bfloat16)
-        .reshape(blocks, row_total, width)
-    )
-    return (result, jnp.transpose(highest + jnp.log(totals), (0, 2, 1)))
+def node_kernel(slot_ref, len_ref, q_ref, k_ref, v_ref, out_ref, lse_ref):
+    slots, rows, width = q_ref.shape
+    cache_rows = k_ref.shape[1]
+    heads = width // HD
+
+    def body(i, carry):
+        node = slot_ref[i]
+        length = len_ref[i]
+
+        @pl.when(length > 0)
+        def _():
+            live = lax.broadcasted_iota(jnp.int32, (rows, cache_rows), 1) < length
+            for h in range(heads):
+                cols = pl.ds(h * HD, HD)
+                q = q_ref[i, :, cols]
+                k = k_ref[node, :, cols]
+                v = v_ref[node, :, cols]
+                s = lax.dot_general(
+                    q, k, (((1,), (1,)), ((), ())), preferred_element_type=jnp.float32
+                ) * HD ** (-0.5)
+                s = jnp.where(live, s, mask_value)
+                m = jnp.max(s, axis=1, keepdims=True)
+                p = jnp.exp(s - m)
+                l = jnp.sum(p, axis=1, keepdims=True)
+                o = jnp.dot(p.astype(jnp.bfloat16), v, preferred_element_type=jnp.float32)
+                out_ref[i, :, cols] = (o / l).astype(out_ref.dtype)
+                lse_ref[i, :, pl.ds(h, 1)] = m + jnp.log(l)
+
+        @pl.when(length == 0)
+        def _():
+            out_ref[i] = jnp.zeros((rows, width), out_ref.dtype)
+            lse_ref[i] = jnp.zeros((rows, heads), lse_ref.dtype)
+
+        return carry
+
+    lax.fori_loop(0, slots, body, 0)
+
+
+def node_attention(queries, key_cache, value_cache, local_slot, lengths, heads_local):
+    slots, rows, width = queries.shape
+    nodes, cache_rows, _ = key_cache.shape
+    vmem = pl.BlockSpec(memory_space=pltpu.VMEM)
+    smem = pl.BlockSpec(memory_space=pltpu.SMEM)
+    flops = 4 * slots * rows * cache_rows * width
+    return pl.pallas_call(
+        node_kernel,
+        out_shape=(
+            jax.ShapeDtypeStruct((slots, rows, width), jnp.bfloat16),
+            jax.ShapeDtypeStruct((slots, rows, heads_local), jnp.float32),
+        ),
+        in_specs=[smem, smem, vmem, vmem, vmem],
+        out_specs=(vmem, vmem),
+        cost_estimate=pl.CostEstimate(
+            flops=flops,
+            transcendentals=slots * rows * cache_rows * heads_local,
+            bytes_accessed=2 * queries.size * 2 + 2 * key_cache.size * 2,
+        ),
+    )(local_slot, lengths, queries, key_cache, value_cache)
 
 
 def self_attention(queries, keys, values):
@@ -151,11 +185,14 @@
     )
     send_item = jnp.sum(jnp.where(send_hit, jnp.arange(items, dtype=jnp.int32), 0), axis=2)
     send_valid = jnp.any(send_hit, axis=2)
-    outgoing = jnp.where(
-        send_valid.reshape(-1)[:, None],
-        jnp.take(q_blocks, (send_item % REQ_DEV).reshape(-1), axis=0),
-        jnp.zeros((), jnp.bfloat16),
-    ).reshape(leaf_count, all_slots * block)
+    pick = (
+        send_valid[:, :, None] & (send_item[:, :, None] % REQ_DEV == jnp.arange(REQ_DEV))
+    ).reshape(leaf_count * all_slots, REQ_DEV)
+    outgoing = (
+        jnp.dot(pick.astype(jnp.bfloat16), q_blocks, preferred_element_type=jnp.float32)
+        .astype(jnp.bfloat16)
+        .reshape(leaf_count, all_slots, REQ_LEN, width_local)
+    )
     arrived = lax.all_to_all(outgoing, "leaf", split_axis=0, concat_axis=0, tiled=True)
     recv_hit = (holders[:, None, :] == device) & (ranks[:, None, :] == slot_ids[None, :, None])
     slot_nodes = jnp.sum(jnp.where(recv_hit, per_sender[:, None, :], 0), axis=2).reshape(-1)
@@ -164,38 +201,45 @@
     lengths = jnp.where(filled, len_of(slot_nodes), 0)
     node_out, node_lse = node_attention(
         arrived.reshape(leaf_count * all_slots, REQ_LEN, width_local),
-        key_cache[local_slot],
-        value_cache[local_slot],
+        key_cache,
+        value_cache,
+        local_slot,
         lengths,
         heads_local,
     )
     flat_lse = node_lse.reshape(leaf_count * all_slots, REQ_LEN * heads_local)
     lse_high = lax.reduce_precision(flat_lse, exponent_bits=8, mantissa_bits=7)
-    lse_low = (flat_lse - lse_high).astype(jnp.bfloat16)
-    payload = jnp.concatenate(
-        [
-            node_out.reshape(leaf_count * all_slots, block),
-            lse_high.astype(jnp.bfloat16),
-            lse_low,
-        ],
-        axis=1,
-    )
-    piece = payload.shape[1]
-    back = lax.all_to_all(
-        payload.reshape(leaf_count, all_slots * piece),
+    lse_low = flat_lse - lse_high
+    lse_pair = jnp.stack([lse_high, lse_low], axis=1).astype(jnp.bfloat16)
+    back_out = lax.all_to_all(
+        node_out.reshape(leaf_count, all_slots, REQ_LEN, width_local),
         "leaf",
         split_axis=0,
         concat_axis=0,
         tiled=True,
-    ).reshape(leaf_count * all_slots, piece)
-    got = jnp.take(back, my_holders * all_slots + my_ranks, axis=0)
-    got_out = got[:, :block].reshape(level_count, REQ_DEV, REQ_LEN, heads_local, HD)
-    lse_width = REQ_LEN * heads_local
-    got_lse = (
-        got[:, block : block + lse_width].astype(jnp.float32)
-        + got[:, block + lse_width :].astype(jnp.float32)
-    ).reshape(level_count, REQ_DEV, REQ_LEN, heads_local)
-    partial_out = jnp.concatenate([got_out.astype(jnp.float32), self_out[None]], axis=0)
+    )
+    back_lse = lax.all_to_all(
+        lse_pair.reshape(leaf_count, all_slots, 2, REQ_LEN * heads_local),
+        "leaf",
+        split_axis=0,
+        concat_axis=0,
+        tiled=True,
+    )
+    take = (
+        (my_holders * all_slots + my_ranks)[:, None]
+        == jnp.arange(leaf_count * all_slots, dtype=jnp.int32)[None, :]
+    ).astype(jnp.bfloat16)
+    got_out = (
+        jnp.dot(take, back_out.reshape(leaf_count * all_slots, block), preferred_element_type=jnp.float32)
+        .reshape(level_count, REQ_DEV, REQ_LEN, heads_local, HD)
+    )
+    got_pair = jnp.dot(
+        take,
+        back_lse.reshape(leaf_count * all_slots, 2 * REQ_LEN * heads_local),
+        preferred_element_type=jnp.float32,
+    ).reshape(items, 2, REQ_LEN * heads_local)
+    got_lse = (got_pair[:, 0] + got_pair[:, 1]).reshape(level_count, REQ_DEV, REQ_LEN, heads_local)
+    partial_out = jnp.concatenate([got_out, self_out[None]], axis=0)
     partial_lse = jnp.concatenate([got_lse, self_lse[None]], axis=0)
     highest = jnp.max(partial_lse, axis=0)
     factor = jnp.exp(partial_lse - highest[None])
@@ -205,9 +249,7 @@
     projected = lax.psum_scatter(
         partial_value.astype(jnp.bfloat16), "mp", scatter_dimension=1, tiled=True
     ).astype(jnp.float32)
-    squares = jnp.sum(
-        lax.all_gather(jnp.sum(projected * projected, axis=1), "mp", axis=0), axis=0
-    )
+    squares = lax.psum(jnp.sum(projected * projected, axis=1), "mp")
     row_scale = lax.rsqrt(squares / D + norm_eps)
     return (
         activations.astype(jnp.float32) + norm_gain[None, :] * projected * row_scale[:, None]

time: 336 us -> 247 us (0.74)
  local copies, waits for them, and re-layouts: 97.4 us -> 18.7 us
  other arithmetic: 69.1 us -> 9.07 us
  waiting for transfers between devices: 98.7 us -> 131 us
  starting transfers between devices: 15.2 us -> 36.9 us
  matrix products: 24.7 us -> 13.6 us
  Pallas kernels: 0 us -> 7.87 us
    all_to_all x3 -> x0, other arithmetic: 42.3 us -> none  [the longest x2 28.5 us: on_device(): lax.all_to_all(payload.reshape(leaf_count, all_slots * piece), 'leaf', sp...]
    unnamed x34 -> x15, local copies, waits for them, and re-layouts: 29.9 us -> 6.34 us
    gather x5 -> x0, local copies, waits for them, and re-layouts: 22.2 us -> none  [the longest x2 7.4 us: on_device(): jnp.take(q_blocks, (send_item % REQ_DEV).reshape(-1), axis=0)]
    all_to_all x1 -> x2, starting transfers between devices: 7.44 us -> 29 us  [the longest x1 22.4 us: on_device(): lax.all_to_all(lse_pair.reshape(leaf_count, all_slots, 2, REQ_LEN * heads...]
    all_gather x1, waiting for transfers between devices: 23.5 us -> 40.1 us  [on_device(): columns = lax.all_gather(activations, 'mp', axis=1, tiled=True)]
    broadcast_in_dim x5 -> x0, local copies, waits for them, and re-layouts: 15.8 us -> none  [the longest x2 7.86 us: on_device(): jnp.take(q_blocks, (send_item % REQ_DEV).reshape(-1), axis=0)]
    psum x0 -> x1, blocking collectives: none -> 15.6 us  [on_device(): squares = lax.psum(jnp.sum(projected * projected, axis=1), 'mp')]
    all_gather x1 -> x0, blocking collectives: 14.6 us -> none  [on_device(): lax.all_gather(jnp.sum(projected * projected, axis=1), 'mp', axis=0)]
  transfers between devices with their start and end apart: 4 -> 5, of which waited for: 4 -> 5; matrix products, arithmetic and copies ran while one was open for 12% -> 5% of each run, Pallas kernels for 0% -> 0%
where the time goes in v2:
time: 247 us; the launch traced here: 246 us
  waiting for transfers between devices  131 us (53%)
  starting transfers between devices  36.9 us (15%)
  local copies, waits for them, and re-layouts  18.7 us (8%)
  blocking collectives  15.6 us (6%)
  between operations  13.8 us (6%)
  matrix products  13.6 us (6%)
  other arithmetic  9.07 us (4%)
  Pallas kernels  7.87 us (3%)
    all_gather x1, waiting for transfers between devices, on_device(): columns = lax.all_gather(activations, 'mp', axis=1, tiled=True)  40.1 us
    reduce_scatter x1, waiting for transfers between devices, on_device(): lax.psum_scatter(partial_value.astype(jnp.bfloat16), 'mp', scatter_dimens...  39.5 us
    all_to_all x1, waiting for transfers between devices, on_device(): lax.all_to_all(outgoing, 'leaf', split_axis=0, concat_axis=0, tiled=True)  25.2 us
    all_to_all x1, starting transfers between devices, on_device(): lax.all_to_all(lse_pair.reshape(leaf_count, all_slots, 2, REQ_LEN * heads...  22.4 us
    all_to_all x1, waiting for transfers between devices, on_device(): lax.all_to_all(node_out.reshape(leaf_count, all_slots, REQ_LEN, width_loc...  20.1 us
    psum x1, blocking collectives, on_device(): squares = lax.psum(jnp.sum(projected * projected, axis=1), 'mp')  15.6 us
    pallas_call x1, Pallas kernels, node_attention(): pl.pallas_call(node_kernel, out_shape=(jax.ShapeDtypeStruct((slots, rows,...  7.87 us
    all_to_all x1, starting transfers between devices, on_device(): lax.all_to_all(outgoing, 'leaf', split_axis=0, concat_axis=0, tiled=True)  7.64 us
  transfers between devices with their start and end apart: 5, of which 5 were waited for; matrix products, arithmetic and copies ran while one was open for 5% of the time, Pallas kernels for 0%

profile of v2, /device:TPU:6, one launch (start us, length us, event | category | flops | bytes accessed | tf_op | source)
XLA Modules:
  0.0 246.4 jit_solution(2637883893534621968)
XLA Ops:
  6.5 0.7 all-gather.2.cloned.1.call-update
  7.3 0.8 stack.19
  8.0 0.9 select_reduce_fusion.4
  9.0 0.9 select_reduce_fusion.3
  10.0 0.9 select_reduce_fusion.1
  11.5 0.2 add_reduce_fusion
  12.6 0.3 multiply_cosine_fusion
  12.9 40.1 %all-gather.2.cloned.1.call-done = bf16[256,4096]{1,0:T(8,128)(2,1)} async-done(((bf16[256,512]{1,0:T(8,128)(2,1)}), bf16[256,4096]{1,0:T(8,128)(2,1)}) %all-gather.2.cloned.1.call-update) | async-done | bytes 2097168 | tf_op jit(solution)/shard_map/all_gather | solution.py:146
  52.9 3.3 %fusion.51 = f32[256,256]{0,1:T(8,128)S(1)} fusion(bf16[256,4096]{1,0:T(8,128)(2,1)} %all-gather.2.cloned.1.call-done, bf16[4096,256]{1,0:T(8,128)(2,1)} %param.13), kind=kOutput, calls=%fused_computation.112 | convolution fusion | flops 536870912 | bytes 4456448 | tf_op jit(solution)/shard_map/dot_general | solution.py:149
  56.3 0.2 copy-done.2
  56.4 1.0 fusion.50
  57.7 0.7 convolution_convert_fusion
  58.4 1.8 copy.178
  60.2 7.6 %all-to-all-start = ((bf16[32,2,64,256]{3,2,1,0:T(8,128)(2,1)}), bf16[32,2,64,256]{3,2,1,0:T(8,128)(2,1)}, u32[]{:S(2)}, u32[]{:S(2)}) async-start(bf16[32,2,64,256]{3,2,1,0:T(8,128)(2,1)} %bitcast.85), calls=%async_computation | async-start | bytes 4194304 | tf_op jit(solution)/shard_map/all_to_all | solution.py:196
  68.4 0.2 select_reduce_fusion.5
  68.6 0.5 broadcast_select_fusion
  69.1 25.2 %all-to-all-done = bf16[32,2,64,256]{3,2,1,0:T(8,128)(2,1)} async-done(((bf16[32,2,64,256]{3,2,1,0:T(8,128)(2,1)}), bf16[32,2,64,256]{3,2,1,0:T(8,128)(2,1)}, u32[]{:S(2)}, u32[]{:S(2)}) %all-to-all-start) | async-done | bytes 2097184 | tf_op jit(solution)/shard_map/all_to_all | solution.py:196
  94.3 7.9 %shard_map.109 = (bf16[64,64,256]{2,1,0:T(8,128)(2,1)}, f32[64,64,2]{2,1,0:T(8,128)}) custom-call(s32[64]{0:T(128)} %get-tuple-element.32.slot_ref, s32[64]{0:T(128)} %get-tuple-element.31.len_ref, bf16[64,64,256]{2,1,0:T(8,128)(2,1)} %bitcast.3.q_ref, bf16[8,256,256]{2,1,0:T(8,128)(2,1)} %k_ref.1, bf16[8,256,256]{2,1,0:T(8,128)(2,1)} %v_ref.1), custom_call_target="tpu_custom_call" | custom-call | flops 1073741824 | bytes 6291456 | tf_op jit(solution)/shard_map/pallas_call | solution.py:88
  102.2 2.8 %reshape.412 = f32[32,2,1,128]{3,1,0,2:T(2,128)S(1)} reshape(f32[64,64,2]{2,1,0:T(8,128)} %get-tuple-element.7) | data formatting | bytes 65536 | tf_op jit(solution)/shard_map/reshape | solution.py:210
  105.1 0.6 copy.152
  105.7 22.4 %all-to-all-start.1 = ((bf16[32,2,2,128]{3,1,2,0:T(2,128)(2,1)}), bf16[32,2,2,128]{3,1,2,0:T(2,128)(2,1)S(1)}, u32[]{:S(2)}, u32[]{:S(2)}) async-start(bf16[32,2,2,128]{3,1,2,0:T(2,128)(2,1)} %copy.152), calls=%async_computation.1 | async-start | bytes 65536 | tf_op jit(solution)/shard_map/all_to_all | solution.py:221
  128.5 5.2 %all-to-all-done.1 = bf16[32,2,2,128]{3,1,2,0:T(2,128)(2,1)S(1)} async-done(((bf16[32,2,2,128]{3,1,2,0:T(2,128)(2,1)}), bf16[32,2,2,128]{3,1,2,0:T(2,128)(2,1)S(1)}, u32[]{:S(2)}, u32[]{:S(2)}) %all-to-all-start.1) | async-done | bytes 32800 | tf_op jit(solution)/shard_map/all_to_all | solution.py:221
  133.7 6.6 %all-to-all-start.2 = ((bf16[32,2,64,256]{3,2,1,0:T(8,128)(2,1)}), bf16[32,2,64,256]{3,2,1,0:T(8,128)(2,1)}, u32[]{:S(2)}, u32[]{:S(2)}) async-start(bf16[32,2,64,256]{3,2,1,0:T(8,128)(2,1)} %bitcast.88), calls=%async_computation.2 | async-start | bytes 4194304 | tf_op jit(solution)/shard_map/all_to_all | solution.py:214
  140.3 0.2 reduce-scatter.2.cloned.1.call-start
  140.6 2.9 %convolution_convert_fusion.2 = bf16[256,256]{1,0:T(8,128)(2,1)S(1)} fusion(bf16[256,4096]{1,0:T(8,128)(2,1)} %all-gather.2.cloned.1.call-done, bf16[4096,256]{1,0:T(8,128)(2,1)} %param.14), kind=kOutput, calls=%fused_computation.7 | convolution fusion | flops 536936448 | bytes 4325376 | tf_op jit(solution)/shard_map/dot_general | solution.py:149
  143.7 0.1 copy.158
  143.9 0.1 copy.159
  144.1 0.1 copy.157
  144.2 0.1 copy.156
  144.4 0.3 fusion.49
  144.9 0.2 fusion.12
  145.1 0.2 fusion.9
  145.4 0.2 fusion.25
  145.7 0.1 add.116
  145.9 0.1 copy.160
  146.0 0.2 reduce_max.26
  146.5 0.2 copy.164
  146.7 20.1 %all-to-all-done.2 = bf16[32,2,64,256]{3,2,1,0:T(8,128)(2,1)} async-done(((bf16[32,2,64,256]{3,2,1,0:T(8,128)(2,1)}), bf16[32,2,64,256]{3,2,1,0:T(8,128)(2,1)}, u32[]{:S(2)}, u32[]{:S(2)}) %all-to-all-start.2) | async-done | bytes 2097184 | tf_op jit(solution)/shard_map/all_to_all | solution.py:214
  166.7 4.2 %copy.180 = bf16[8,8,64,256]{3,1,2,0:T(8,128)(2,1)} copy(bf16[8,8,64,256]{3,2,1,0:T(8,128)(2,1)} %bitcast.34) | data formatting | bytes 4194304
  170.9 4.5 %dot_general.43 = bf16[64,2,128,64]{2,1,0,3:T(2,128)(2,1)} reshape(bf16[16384,64]{0,1:T(8,128)(2,1)} %bitcast.87) | data formatting | bytes 4194304 | tf_op jit(solution)/shard_map/dot_general | solution.py:233
  175.4 2.9 %fusion = f32[3,4,64,2,128]{4,1,3,2,0:T(4,128)S(1)} fusion(bf16[64,2,128,64]{2,1,0,3:T(2,128)(2,1)} %dot_general.43, s32[3,4]{1,0:T(4,128)S(1)} %add.120), kind=kOutput, calls=%fused_computation.2 | convolution fusion | flops 25166592 | bytes 2883632 | tf_op jit(solution)/shard_map/dot_general | solution.py:233
  178.3 0.8 fusion.4
  179.1 0.2 divide_convert_fusion
  179.4 2.1 convolution_convert_fusion.1
  181.5 39.5 %reduce-scatter.2.cloned.1.call-done = bf16[256,512]{1,0:T(8,128)(2,1)} async-done(((bf16[256,4096]{1,0:T(8,128)(2,1)}), bf16[256,512]{1,0:T(8,128)(2,1)}) %reduce-scatter.2.cloned.1.call-update) | async-done | bytes 262160 | tf_op jit(solution)/shard_map/reduce_scatter | solution.py:249
  221.0 1.1 fusion.8
  222.1 15.6 %psum.7 = f32[256]{0:T(256)S(1)} all-reduce(f32[256]{0:T(256)S(1)} %fusion.8), channel_id=1, replica_groups=mesh['leaf'=32,'mp'=8] {'mp'}, use_global_device_ids=true, to_apply=%region_18.19 | all-reduce | flops 256 | bytes 2048 | tf_op jit(solution)/shard_map/psum | solution.py:252
  237.8 1.8 fusion.7
  (70 shorter events, 3.7 us)
Async XLA Ops:
  6.5 172.9 %copy-start = (bf16[256,4096]{1,0:T(8,128)(2,1)S(1)}, bf16[256,4096]{1,0:T(8,128)(2,1)}, u32[]{:S(2)}) copy-start(bf16[256,4096]{1,0:T(8,128)(2,1)} %param.15) | copy-start | bytes 6291460
  6.5 46.4 %all-gather.2.cloned.1.call-start = ((), (), s32[]{:S(2)}) async-start(), calls=%async_computation.4 | async-start | bytes 2359296 | tf_op jit(solution)/shard_map/all_gather | solution.py:146
  52.9 3.3 %copy-start.1 = (bf16[256,4096]{1,0:T(8,128)(2,1)S(1)}, bf16[256,4096]{1,0:T(8,128)(2,1)}, u32[]{:S(2)}) copy-start(bf16[256,4096]{1,0:T(8,128)(2,1)} %all-gather.2.cloned.1.call-done) | copy-start | bytes 6291460
  52.9 3.5 %copy-start.2 = (bf16[4096,256]{1,0:T(8,128)(2,1)S(1)}, bf16[4096,256]{1,0:T(8,128)(2,1)}, u32[]{:S(2)}) copy-start(bf16[4096,256]{1,0:T(8,128)(2,1)} %param.12) | copy-start | bytes 6291460
  60.2 8.1 %copy-start.4 = (s32[256]{0:T(256)S(1)}, s32[256]{0:T(256)}, u32[]{:S(2)}) copy-start(s32[256]{0:T(256)} %param.20) | copy-start | bytes 3076
  60.2 34.0 %all-to-all-start = ((bf16[32,2,64,256]{3,2,1,0:T(8,128)(2,1)}), bf16[32,2,64,256]{3,2,1,0:T(8,128)(2,1)}, u32[]{:S(2)}, u32[]{:S(2)}) async-start(bf16[32,2,64,256]{3,2,1,0:T(8,128)(2,1)} %bitcast.85), calls=%async_computation | async-start | bytes 4194304 | tf_op jit(solution)/shard_map/all_to_all | solution.py:196
  105.7 28.0 %all-to-all-start.1 = ((bf16[32,2,2,128]{3,1,2,0:T(2,128)(2,1)}), bf16[32,2,2,128]{3,1,2,0:T(2,128)(2,1)S(1)}, u32[]{:S(2)}, u32[]{:S(2)}) async-start(bf16[32,2,2,128]{3,1,2,0:T(2,128)(2,1)} %copy.152), calls=%async_computation.1 | async-start | bytes 65536 | tf_op jit(solution)/shard_map/all_to_all | solution.py:221
  133.7 33.0 %all-to-all-start.2 = ((bf16[32,2,64,256]{3,2,1,0:T(8,128)(2,1)}), bf16[32,2,64,256]{3,2,1,0:T(8,128)(2,1)}, u32[]{:S(2)}, u32[]{:S(2)}) async-start(bf16[32,2,64,256]{3,2,1,0:T(8,128)(2,1)} %bitcast.88), calls=%async_computation.2 | async-start | bytes 4194304 | tf_op jit(solution)/shard_map/all_to_all | solution.py:214
  140.3 80.7 %reduce-scatter.2.cloned.1.call-start = ((), (), s32[]{:S(2)}) async-start(), calls=%async_computation.5 | async-start | bytes 2359296 | tf_op jit(solution)/shard_map/reduce_scatter | solution.py:249
  181.5 56.3 %copy-start.3 = (bf16[256,512]{1,0:T(8,128)(2,1)S(1)}, bf16[256,512]{1,0:T(8,128)(2,1)}, u32[]{:S(2)}) copy-start(bf16[256,512]{1,0:T(8,128)(2,1)} %param.11) | copy-start | bytes 786436
  181.5 56.3 %copy-start.5 = (f32[512]{0:T(512)S(1)}, f32[512]{0:T(512)}, u32[]{:S(2)}) copy-start(f32[512]{0:T(512)} %param.16) | copy-start | bytes 6148
Sparse Core Ops, SparseCore 0:
  9.1 43.7 all-gather.1
  181.6 39.3 reduce-scatter.1

commit v3 on v2

--- a/solution.py
+++ b/solution.py
@@ -41,64 +41,163 @@
     return jnp.sum(jnp.where(hit, table, 0), axis=-1).astype(table.dtype)
 
 
-def node_kernel(slot_ref, len_ref, q_ref, k_ref, v_ref, out_ref, lse_ref):
-    slots, rows, width = q_ref.shape
+GROUP = 8
+
+
+def attend(q, k, v, length, rows, cache_rows):
+    live = lax.broadcasted_iota(jnp.int32, (rows, cache_rows), 1) < length
+    s = lax.dot_general(
+        q, k, (((1,), (1,)), ((), ())), preferred_element_type=jnp.float32
+    ) * HD ** (-0.5)
+    s = jnp.where(live, s, mask_value)
+    m = jnp.max(s, axis=1, keepdims=True)
+    p = jnp.exp(s - m)
+    l = jnp.sum(p, axis=1, keepdims=True)
+    o = jnp.dot(p.astype(jnp.bfloat16), v, preferred_element_type=jnp.float32)
+    return o / l, m + jnp.log(l)
+
+
+def node_kernel(
+    slot_ref, len_ref, mode_ref, gnode_ref, glen_ref, q_ref, k_ref, v_ref, out_ref, lse_ref
+):
+    total_rows, width = q_ref.shape
     cache_rows = k_ref.shape[1]
     heads = width // HD
-
-    def body(i, carry):
+    groups = mode_ref.shape[0]
+    span = GROUP * REQ_LEN
+
+    def one_slot(i, carry):
         node = slot_ref[i]
         length = len_ref[i]
+        rows = pl.ds(pl.multiple_of(i * REQ_LEN, REQ_LEN), REQ_LEN)
 
         @pl.when(length > 0)
         def _():
-            live = lax.broadcasted_iota(jnp.int32, (rows, cache_rows), 1) < length
             for h in range(heads):
                 cols = pl.ds(h * HD, HD)
-                q = q_ref[i, :, cols]
-                k = k_ref[node, :, cols]
-                v = v_ref[node, :, cols]
-                s = lax.dot_general(
-                    q, k, (((1,), (1,)), ((), ())), preferred_element_type=jnp.float32
-                ) * HD ** (-0.5)
-                s = jnp.where(live, s, mask_value)
-                m = jnp.max(s, axis=1, keepdims=True)
-                p = jnp.exp(s - m)
-                l = jnp.sum(p, axis=1, keepdims=True)
-                o = jnp.dot(p.astype(jnp.bfloat16), v, preferred_element_type=jnp.float32)
-                out_ref[i, :, cols] = (o / l).astype(out_ref.dtype)
-                lse_ref[i, :, pl.ds(h, 1)] = m + jnp.log(l)
+                o, lse = attend(
+                    q_ref[rows, cols], k_ref[node, :, cols], v_ref[node, :, cols],
+                    length, REQ_LEN, cache_rows,
+                )
+                out_ref[rows, cols] = o.astype(out_ref.dtype)
+                lse_ref[rows, pl.ds(h, 1)] = lse
 
         @pl.when(length == 0)
         def _():
-            out_ref[i] = jnp.zeros((rows, width), out_ref.dtype)
-            lse_ref[i] = jnp.zeros((rows, heads), lse_ref.dtype)
+            out_ref[rows, :] = jnp.zeros((REQ_LEN, width), out_ref.dtype)
+            lse_ref[rows, :] = jnp.zeros((REQ_LEN, heads), lse_ref.dtype)
 
         return carry
 
-    lax.fori_loop(0, slots, body, 0)
+    def one_group(g, carry):
+        mode = mode_ref[g]
+        rows = pl.ds(pl.multiple_of(g * span, span), span)
+
+        @pl.when(mode == 0)
+        def _():
+            out_ref[rows, :] = jnp.zeros((span, width), out_ref.dtype)
+            lse_ref[rows, :] = jnp.zeros((span, heads), lse_ref.dtype)
+
+        @pl.when(mode == 1)
+        def _():
+            node = gnode_ref[g]
+            length = glen_ref[g]
+            for h in range(heads):
+                cols = pl.ds(h * HD, HD)
+                o, lse = attend(
+                    q_ref[rows, cols], k_ref[node, :, cols], v_ref[node, :, cols],
+                    length, span, cache_rows,
+                )
+                out_ref[rows, cols] = o.astype(out_ref.dtype)
+                lse_ref[rows, pl.ds(h, 1)] = lse
+
+        @pl.when(mode == 2)
+        def _():
+            lax.fori_loop(g * GROUP, (g + 1) * GROUP, one_slot, 0)
+
+        return carry
+
+    lax.fori_loop(0, groups, one_group, 0)
 
 
 def node_attention(queries, key_cache, value_cache, local_slot, lengths, heads_local):
     slots, rows, width = queries.shape
     nodes, cache_rows, _ = key_cache.shape
+    groups = slots // GROUP
+    live = (lengths > 0).reshape(groups, GROUP)
+    grouped_node = local_slot.reshape(groups, GROUP)
+    grouped_len = lengths.reshape(groups, GROUP)
+    group_node = jnp.max(jnp.where(live, grouped_node, 0), axis=1)
+    group_len = jnp.max(grouped_len, axis=1)
+    uniform = jnp.all(~live | (grouped_node == group_node[:, None]), axis=1)
+    mode = jnp.where(jnp.any(live, axis=1), jnp.where(uniform, 1, 2), 0).astype(jnp.int32)
     vmem = pl.BlockSpec(memory_space=pltpu.VMEM)
     smem = pl.BlockSpec(memory_space=pltpu.SMEM)
     flops = 4 * slots * rows * cache_rows * width
-    return pl.pallas_call(
+    out, lse = pl.pallas_call(
         node_kernel,
         out_shape=(
-            jax.ShapeDtypeStruct((slots, rows, width), jnp.bfloat16),
-            jax.ShapeDtypeStruct((slots, rows, heads_local), jnp.float32),
+            jax.ShapeDtypeStruct((slots * rows, width), jnp.bfloat16),
+            jax.ShapeDtypeStruct((slots * rows, heads_local), jnp.float32),
         ),
-        in_specs=[smem, smem, vmem, vmem, vmem],
+        in_specs=[smem] * 5 + [vmem] * 3,
         out_specs=(vmem, vmem),
         cost_estimate=pl.CostEstimate(
             flops=flops,
             transcendentals=slots * rows * cache_rows * heads_local,
             bytes_accessed=2 * queries.size * 2 + 2 * key_cache.size * 2,
         ),
-    )(local_slot, lengths, queries, key_cache, value_cache)
+    )(
+        local_slot, lengths, mode, group_node, group_len,
+        queries.reshape(slots * rows, width), key_cache, value_cache,
+    )
+    return out.reshape(slots, rows, width), lse.reshape(slots, rows, heads_local)
+
+
+def sum_kernel(x_ref, out_ref, recv, send_sem, recv_sem):
+    n = recv.shape[0]
+    me = lax.axis_index("mp")
+    barrier = pltpu.get_barrier_semaphore()
+    for d in range(1, n):
+        pl.semaphore_signal(
+            barrier, inc=1, device_id={"mp": lax.rem(me + d, n)},
+            device_id_type=pl.DeviceIdType.MESH,
+        )
+    pl.semaphore_wait(barrier, n - 1)
+    copies = []
+    for d in range(1, n):
+        copy = pltpu.make_async_remote_copy(
+            src_ref=x_ref,
+            dst_ref=recv.at[d],
+            send_sem=send_sem.at[d],
+            recv_sem=recv_sem.at[d],
+            device_id={"mp": lax.rem(me + d, n)},
+            device_id_type=pl.DeviceIdType.MESH,
+        )
+        copy.start()
+        copies.append(copy)
+    for copy in copies:
+        copy.wait()
+    total = x_ref[...]
+    for d in range(1, n):
+        total = total + recv[d]
+    out_ref[...] = total
+
+
+def mp_sum(x, n):
+    vmem = pl.BlockSpec(memory_space=pltpu.VMEM)
+    return pl.pallas_call(
+        sum_kernel,
+        out_shape=jax.ShapeDtypeStruct(x.shape, x.dtype),
+        in_specs=[vmem],
+        out_specs=vmem,
+        scratch_shapes=[
+            pltpu.VMEM((n,) + x.shape, x.dtype),
+            pltpu.SemaphoreType.DMA((n,)),
+            pltpu.SemaphoreType.DMA((n,)),
+        ],
+        compiler_params=pltpu.CompilerParams(collective_id=0, has_side_effects=True),
+    )(x)
 
 
 def self_attention(queries, keys, values):
@@ -249,7 +348,9 @@
     projected = lax.psum_scatter(
         partial_value.astype(jnp.bfloat16), "mp", scatter_dimension=1, tiled=True
     ).astype(jnp.float32)
-    squares = lax.psum(jnp.sum(projected * projected, axis=1), "mp")
+    squares = mp_sum(
+        jnp.sum(projected * projected, axis=1).reshape(1, tok_rows), lax.axis_size("mp")
+    ).reshape(tok_rows)
     row_scale = lax.rsqrt(squares / D + norm_eps)
     return (
         activations.astype(jnp.float32) + norm_gain[None, :] * projected * row_scale[:, None]

time: 247 us -> 231 us (0.935)
  blocking collectives: 15.6 us -> 0 us
  starting transfers between devices: 36.9 us -> 29.8 us
  Pallas kernels: 7.87 us -> 13.6 us
  waiting for transfers between devices: 131 us -> 128 us
  other arithmetic: 9.07 us -> 11.9 us
    psum x1 -> x0, blocking collectives: 15.6 us -> none  [on_device(): squares = lax.psum(jnp.sum(projected * projected, axis=1), 'mp')]
    all_to_all x1, starting transfers between devices: 22.4 us -> 15.3 us  [on_device(): lax.all_to_all(lse_pair.reshape(leaf_count, all_slots, 2, REQ_LEN * heads...]
    pallas_call x1 -> x2, Pallas kernels: 7.87 us -> 13.6 us  [the longest x1 9.02 us: mp_sum(): pl.pallas_call(sum_kernel, out_shape=jax.ShapeDtypeStruct(x.shape, x.dtyp...]
    another operation x0 -> x1, local copies, waits for them, and re-layouts: none -> 2.84 us  [on_device(): flat_lse = node_lse.reshape(leaf_count * all_slots, REQ_LEN * heads_local)]
    reshape x1 -> x0, local copies, waits for them, and re-layouts: 2.84 us -> none  [on_device(): flat_lse = node_lse.reshape(leaf_count * all_slots, REQ_LEN * heads_local)]
    unnamed x15 -> x17, local copies, waits for them, and re-layouts: 6.34 us -> 6.34 us
  transfers between devices with their start and end apart: 5 -> 5, of which waited for: 5 -> 5; matrix products, arithmetic and copies ran while one was open for 5% -> 7% of each run, Pallas kernels for 0% -> 0%
where the time goes in v3:
time: 231 us
  waiting for transfers between devices  128 us (55%)
  starting transfers between devices  29.8 us (13%)
  local copies, waits for them, and re-layouts  19.4 us (8%)
  between operations  13.9 us (6%)
  matrix products  13.6 us (6%)
  Pallas kernels  13.6 us (6%)
  other arithmetic  11.9 us (5%)
    all_gather x1, waiting for transfers between devices, on_device(): columns = lax.all_gather(activations, 'mp', axis=1, tiled=True)  40.1 us
    reduce_scatter x1, waiting for transfers between devices, on_device(): lax.psum_scatter(partial_value.astype(jnp.bfloat16), 'mp', scatter_dimens...  39.5 us
    all_to_all x1, waiting for transfers between devices, on_device(): lax.all_to_all(outgoing, 'leaf', split_axis=0, concat_axis=0, tiled=True)  22.9 us
    all_to_all x1, waiting for transfers between devices, on_device(): lax.all_to_all(node_out.reshape(leaf_count, all_slots, REQ_LEN, width_loc...  20.1 us
    all_to_all x1, starting transfers between devices, on_device(): lax.all_to_all(lse_pair.reshape(leaf_count, all_slots, 2, REQ_LEN * heads...  15.3 us
    pallas_call x1, Pallas kernels, mp_sum(): pl.pallas_call(sum_kernel, out_shape=jax.ShapeDtypeStruct(x.shape, x.dtyp...  9.02 us
    all_to_all x1, starting transfers between devices, on_device(): lax.all_to_all(outgoing, 'leaf', split_axis=0, concat_axis=0, tiled=True)  7.64 us
    dot_general x3, matrix products, on_device(): jnp.dot(columns, matrix, preferred_element_type=jnp.float32)  7.19 us
  transfers between devices with their start and end apart: 5, of which 5 were waited for; matrix products, arithmetic and copies ran while one was open for 7% of the time, Pallas kernels for 0%

profile of v3, /device:TPU:6, one launch (start us, length us, event | category | flops | bytes accessed | tf_op | source)
XLA Modules:
  0.0 230.6 jit_solution(8816287848927035181)
XLA Ops:
  6.5 0.7 all-gather.2.cloned.1.call-update
  7.3 0.8 stack.19
  8.0 0.9 select_reduce_fusion.4
  9.0 0.9 select_reduce_fusion.3
  10.0 0.9 select_reduce_fusion.1
  11.5 0.2 add_reduce_fusion
  12.6 0.3 multiply_cosine_fusion
  12.9 40.1 %all-gather.2.cloned.1.call-done = bf16[256,4096]{1,0:T(8,128)(2,1)} async-done(((bf16[256,512]{1,0:T(8,128)(2,1)}), bf16[256,4096]{1,0:T(8,128)(2,1)}) %all-gather.2.cloned.1.call-update) | async-done | bytes 2097168 | tf_op jit(solution)/shard_map/all_gather | solution.py:245
  52.9 3.3 %fusion.51 = f32[256,256]{0,1:T(8,128)S(1)} fusion(bf16[256,4096]{1,0:T(8,128)(2,1)} %all-gather.2.cloned.1.call-done, bf16[4096,256]{1,0:T(8,128)(2,1)} %param.13), kind=kOutput, calls=%fused_computation.118 | convolution fusion | flops 536870912 | bytes 4456448 | tf_op jit(solution)/shard_map/dot_general | solution.py:248
  56.3 0.2 copy-done.2
  56.4 1.0 fusion.50
  57.7 0.7 convolution_convert_fusion
  58.4 1.8 copy.179
  60.2 7.6 %all-to-all-start = ((bf16[32,2,64,256]{3,2,1,0:T(8,128)(2,1)}), bf16[32,2,64,256]{3,2,1,0:T(8,128)(2,1)}, u32[]{:S(2)}, u32[]{:S(2)}) async-start(bf16[32,2,64,256]{3,2,1,0:T(8,128)(2,1)} %bitcast.87), calls=%async_computation | async-start | bytes 4194304 | tf_op jit(solution)/shard_map/all_to_all | solution.py:295
  68.4 0.2 select_reduce_fusion.5
  68.9 0.6 reduce_max.61.glen_ref
  70.3 0.5 select_select_fusion.mode_ref
  70.9 0.5 broadcast_select_fusion
  71.4 22.9 %all-to-all-done = bf16[32,2,64,256]{3,2,1,0:T(8,128)(2,1)} async-done(((bf16[32,2,64,256]{3,2,1,0:T(8,128)(2,1)}), bf16[32,2,64,256]{3,2,1,0:T(8,128)(2,1)}, u32[]{:S(2)}, u32[]{:S(2)}) %all-to-all-start) | async-done | bytes 2097184 | tf_op jit(solution)/shard_map/all_to_all | solution.py:295
  94.3 4.6 %shard_map.109 = (bf16[4096,256]{1,0:T(8,128)(2,1)}, f32[4096,2]{1,0:T(8,128)}) custom-call(s32[64]{0:T(128)} %get-tuple-element.37.slot_ref, s32[64]{0:T(128)} %get-tuple-element.36.len_ref, s32[8]{0:T(128)} %select_select_fusion.mode_ref, s32[8]{0:T(128)} %copy-done.4, s32[8]{0:T(128)} %reduce_max.61.glen_ref, bf16[4096,256]{1,0:T(8,128)(2,1)} %bitcast.3.q_ref, ...), custom_call_target="tpu_custom_call" | custom-call | flops 1073741824 | bytes 6291456 | tf_op jit(solution)/shard_map/pallas_call | solution.py:137
  98.9 2.8 %reshape_reshape.10 = f32[32,2,1,128]{3,1,0,2:T(2,128)S(1)} reshape(f32[4096,2]{1,0:T(8,128)} %get-tuple-element.7) | data formatting | bytes 65536 | tf_op jit(solution)/shard_map/reshape;reshape | solution.py:309
  101.8 0.6 copy.153
  102.4 15.3 %all-to-all-start.1 = ((bf16[32,2,2,128]{3,1,2,0:T(2,128)(2,1)}), bf16[32,2,2,128]{3,1,2,0:T(2,128)(2,1)S(1)}, u32[]{:S(2)}, u32[]{:S(2)}) async-start(bf16[32,2,2,128]{3,1,2,0:T(2,128)(2,1)} %copy.153), calls=%async_computation.1 | async-start | bytes 65536 | tf_op jit(solution)/shard_map/all_to_all | solution.py:320
  118.1 5.1 %all-to-all-done.1 = bf16[32,2,2,128]{3,1,2,0:T(2,128)(2,1)S(1)} async-done(((bf16[32,2,2,128]{3,1,2,0:T(2,128)(2,1)}), bf16[32,2,2,128]{3,1,2,0:T(2,128)(2,1)S(1)}, u32[]{:S(2)}, u32[]{:S(2)}) %all-to-all-start.1) | async-done | bytes 32800 | tf_op jit(solution)/shard_map/all_to_all | solution.py:320
  123.2 6.6 %all-to-all-start.2 = ((bf16[32,2,64,256]{3,2,1,0:T(8,128)(2,1)}), bf16[32,2,64,256]{3,2,1,0:T(8,128)(2,1)}, u32[]{:S(2)}, u32[]{:S(2)}) async-start(bf16[32,2,64,256]{3,2,1,0:T(8,128)(2,1)} %bitcast.90), calls=%async_computation.2 | async-start | bytes 4194304 | tf_op jit(solution)/shard_map/all_to_all | solution.py:313
  129.9 0.2 reduce-scatter.2.cloned.1.call-start
  130.1 2.9 %convolution_convert_fusion.2 = bf16[256,256]{1,0:T(8,128)(2,1)S(1)} fusion(bf16[256,4096]{1,0:T(8,128)(2,1)} %all-gather.2.cloned.1.call-done, bf16[4096,256]{1,0:T(8,128)(2,1)} %param.14), kind=kOutput, calls=%fused_computation.7 | convolution fusion | flops 536936448 | bytes 4325376 | tf_op jit(solution)/shard_map/dot_general | solution.py:248
  133.6 0.1 copy.158
  133.8 0.1 copy.157
  133.9 0.3 fusion.49
  134.4 0.2 fusion.12
  134.7 0.2 fusion.9
  135.0 0.2 fusion.25
  135.3 0.1 add.119
  135.6 0.2 reduce_max.64
  136.0 0.2 copy.165
  136.2 20.1 %all-to-all-done.2 = bf16[32,2,64,256]{3,2,1,0:T(8,128)(2,1)} async-done(((bf16[32,2,64,256]{3,2,1,0:T(8,128)(2,1)}), bf16[32,2,64,256]{3,2,1,0:T(8,128)(2,1)}, u32[]{:S(2)}, u32[]{:S(2)}) %all-to-all-start.2) | async-done | bytes 2097184 | tf_op jit(solution)/shard_map/all_to_all | solution.py:313
  156.3 4.2 %copy.181 = bf16[8,8,64,256]{3,1,2,0:T(8,128)(2,1)} copy(bf16[8,8,64,256]{3,2,1,0:T(8,128)(2,1)} %bitcast.36) | data formatting | bytes 4194304
  160.5 4.5 %dot_general.43 = bf16[64,2,128,64]{2,1,0,3:T(2,128)(2,1)} reshape(bf16[16384,64]{0,1:T(8,128)(2,1)} %bitcast.89) | data formatting | bytes 4194304 | tf_op jit(solution)/shard_map/dot_general | solution.py:332
  164.9 2.9 %fusion = f32[3,4,64,2,128]{4,1,3,2,0:T(4,128)S(1)} fusion(bf16[64,2,128,64]{2,1,0,3:T(2,128)(2,1)} %dot_general.43, s32[3,4]{1,0:T(4,128)S(1)} %add.123), kind=kOutput, calls=%fused_computation.2 | convolution fusion | flops 25166592 | bytes 2883632 | tf_op jit(solution)/shard_map/dot_general | solution.py:332
  167.8 0.8 fusion.4
  168.6 0.2 divide_convert_fusion
  169.0 2.1 convolution_convert_fusion.1
  171.1 39.5 %reduce-scatter.2.cloned.1.call-done = bf16[256,512]{1,0:T(8,128)(2,1)} async-done(((bf16[256,4096]{1,0:T(8,128)(2,1)}), bf16[256,512]{1,0:T(8,128)(2,1)}) %reduce-scatter.2.cloned.1.call-update) | async-done | bytes 262160 | tf_op jit(solution)/shard_map/reduce_scatter | solution.py:348
  210.6 1.6 fusion.8
  212.2 9.0 %shard_map.110 = f32[1,256]{1,0:T(1,128)} custom-call(f32[1,256]{1,0:T(1,128)} %bitcast.97), custom_call_target="tpu_custom_call" | custom-call | tf_op jit(solution)/shard_map/pallas_call | solution.py:189
  221.3 0.7 add_rsqrt_fusion
  222.0 1.8 fusion.7
  (87 shorter events, 5.2 us)
Async XLA Ops:
  6.5 162.4 %copy-start = (bf16[256,4096]{1,0:T(8,128)(2,1)S(1)}, bf16[256,4096]{1,0:T(8,128)(2,1)}, u32[]{:S(2)}) copy-start(bf16[256,4096]{1,0:T(8,128)(2,1)} %param.15) | copy-start | bytes 6291460
  6.5 46.4 %all-gather.2.cloned.1.call-start = ((), (), s32[]{:S(2)}) async-start(), calls=%async_computation.4 | async-start | bytes 2359296 | tf_op jit(solution)/shard_map/all_gather | solution.py:245
  52.9 3.3 %copy-start.1 = (bf16[256,4096]{1,0:T(8,128)(2,1)S(1)}, bf16[256,4096]{1,0:T(8,128)(2,1)}, u32[]{:S(2)}) copy-start(bf16[256,4096]{1,0:T(8,128)(2,1)} %all-gather.2.cloned.1.call-done) | copy-start | bytes 6291460
  52.9 3.5 %copy-start.2 = (bf16[4096,256]{1,0:T(8,128)(2,1)S(1)}, bf16[4096,256]{1,0:T(8,128)(2,1)}, u32[]{:S(2)}) copy-start(bf16[4096,256]{1,0:T(8,128)(2,1)} %param.12) | copy-start | bytes 6291460
  60.2 8.1 %copy-start.5 = (s32[256]{0:T(256)S(1)}, s32[256]{0:T(256)}, u32[]{:S(2)}) copy-start(s32[256]{0:T(256)} %param.20) | copy-start | bytes 3076
  60.2 34.0 %all-to-all-start = ((bf16[32,2,64,256]{3,2,1,0:T(8,128)(2,1)}), bf16[32,2,64,256]{3,2,1,0:T(8,128)(2,1)}, u32[]{:S(2)}, u32[]{:S(2)}) async-start(bf16[32,2,64,256]{3,2,1,0:T(8,128)(2,1)} %bitcast.87), calls=%async_computation | async-start | bytes 4194304 | tf_op jit(solution)/shard_map/all_to_all | solution.py:295
  69.7 24.6 %copy-start.4 = (s32[8]{0:T(128)}, s32[8]{0:T(128)S(1)}, u32[]{:S(2)}) copy-start(s32[8]{0:T(128)S(1)} %reduce_max.58.gnode_ref) | copy-start | bytes 100
  102.4 20.8 %all-to-all-start.1 = ((bf16[32,2,2,128]{3,1,2,0:T(2,128)(2,1)}), bf16[32,2,2,128]{3,1,2,0:T(2,128)(2,1)S(1)}, u32[]{:S(2)}, u32[]{:S(2)}) async-start(bf16[32,2,2,128]{3,1,2,0:T(2,128)(2,1)} %copy.153), calls=%async_computation.1 | async-start | bytes 65536 | tf_op jit(solution)/shard_map/all_to_all | solution.py:320
  123.2 33.1 %all-to-all-start.2 = ((bf16[32,2,64,256]{3,2,1,0:T(8,128)(2,1)}), bf16[32,2,64,256]{3,2,1,0:T(8,128)(2,1)}, u32[]{:S(2)}, u32[]{:S(2)}) async-start(bf16[32,2,64,256]{3,2,1,0:T(8,128)(2,1)} %bitcast.90), calls=%async_computation.2 | async-start | bytes 4194304 | tf_op jit(solution)/shard_map/all_to_all | solution.py:313
  129.9 80.7 %reduce-scatter.2.cloned.1.call-start = ((), (), s32[]{:S(2)}) async-start(), calls=%async_computation.5 | async-start | bytes 2359296 | tf_op jit(solution)/shard_map/reduce_scatter | solution.py:348
  171.0 50.9 %copy-start.3 = (bf16[256,512]{1,0:T(8,128)(2,1)S(1)}, bf16[256,512]{1,0:T(8,128)(2,1)}, u32[]{:S(2)}) copy-start(bf16[256,512]{1,0:T(8,128)(2,1)} %param.11) | copy-start | bytes 786436
  171.0 50.9 %copy-start.6 = (f32[512]{0:T(512)S(1)}, f32[512]{0:T(512)}, u32[]{:S(2)}) copy-start(f32[512]{0:T(512)} %param.16) | copy-start | bytes 6148
Sparse Core Ops, SparseCore 0:
  9.1 43.7 all-gather.1
  171.2 39.3 reduce-scatter.1

commit v4 on v3

--- a/solution.py
+++ b/solution.py
@@ -220,6 +220,120 @@
     )
 
 
+def self_part(q_ref, k_ref, v_ref, out_ref, lse_ref):
+    tokens, width = q_ref.shape
+    heads = width // HD
+    causal = (
+        lax.broadcasted_iota(jnp.int32, (REQ_LEN, REQ_LEN), 0)
+        >= lax.broadcasted_iota(jnp.int32, (REQ_LEN, REQ_LEN), 1)
+    )
+    for r in range(tokens // REQ_LEN):
+        rows = pl.ds(r * REQ_LEN, REQ_LEN)
+        for h in range(heads):
+            cols = pl.ds(h * HD, HD)
+            s = lax.dot_general(
+                q_ref[rows, cols], k_ref[rows, cols], (((1,), (1,)), ((), ())),
+                preferred_element_type=jnp.float32,
+            ) * HD ** (-0.5)
+            s = jnp.where(causal, s, mask_value)
+            m = jnp.max(s, axis=1, keepdims=True)
+            p = jnp.exp(s - m)
+            l = jnp.sum(p, axis=1, keepdims=True)
+            o = jnp.dot(p.astype(jnp.bfloat16), v_ref[rows, cols], preferred_element_type=jnp.float32)
+            out_ref[rows, cols] = o / l
+            lse_ref[rows, pl.ds(h, 1)] = m + jnp.log(l)
+
+
+def back_kernel(
+    out_in, lse_in, q_ref, k_ref, v_ref,
+    out_back, lse_back, self_out, self_lse,
+    recv_out, recv_lse, send_sems, recv_sems, lse_send_sems, lse_recv_sems,
+):
+    n = recv_out.shape[0]
+    me = lax.axis_index("leaf")
+    mesh_ids = pl.DeviceIdType.MESH
+    barrier = pltpu.get_barrier_semaphore()
+
+    def greet(d, carry):
+        pl.semaphore_signal(barrier, inc=1, device_id={"leaf": lax.rem(me + d, n)}, device_id_type=mesh_ids)
+        return carry
+
+    lax.fori_loop(1, n, greet, 0)
+    pl.semaphore_wait(barrier, n - 1)
+
+    def out_copy(d, peer):
+        return pltpu.make_async_remote_copy(
+            src_ref=out_in.at[peer], dst_ref=recv_out.at[me],
+            send_sem=send_sems.at[d], recv_sem=recv_sems.at[d],
+            device_id={"leaf": peer}, device_id_type=mesh_ids,
+        )
+
+    def lse_copy(d, peer):
+        return pltpu.make_async_remote_copy(
+            src_ref=lse_in.at[peer], dst_ref=recv_lse.at[me],
+            send_sem=lse_send_sems.at[d], recv_sem=lse_recv_sems.at[d],
+            device_id={"leaf": peer}, device_id_type=mesh_ids,
+        )
+
+    def send(d, carry):
+        peer = lax.rem(me + d, n)
+        out_copy(d, peer).start()
+        lse_copy(d, peer).start()
+        return carry
+
+    lax.fori_loop(1, n, send, 0)
+    recv_out[me] = out_in[me]
+    recv_lse[me] = lse_in[me]
+    self_part(q_ref, k_ref, v_ref, self_out, self_lse)
+
+    def finish(d, carry):
+        peer = lax.rem(me + d, n)
+        out_copy(d, peer).wait_send()
+        lse_copy(d, peer).wait_send()
+        sender = lax.rem(me + n - d, n)
+        pltpu.make_async_remote_copy(
+            src_ref=out_in.at[sender], dst_ref=recv_out.at[sender],
+            send_sem=send_sems.at[d], recv_sem=recv_sems.at[d],
+            device_id={"leaf": sender}, device_id_type=mesh_ids,
+        ).wait_recv()
+        pltpu.make_async_remote_copy(
+            src_ref=lse_in.at[sender], dst_ref=recv_lse.at[sender],
+            send_sem=lse_send_sems.at[d], recv_sem=lse_recv_sems.at[d],
+            device_id={"leaf": sender}, device_id_type=mesh_ids,
+        ).wait_recv()
+        return carry
+
+    lax.fori_loop(1, n, finish, 0)
+    out_back[...] = recv_out[...]
+    lse_back[...] = recv_lse[...]
+
+
+def back_exchange(out_payload, lse_payload, q_self, k_self, v_self, heads_local):
+    n = out_payload.shape[0]
+    tokens, width = q_self.shape
+    vmem = pl.BlockSpec(memory_space=pltpu.VMEM)
+    return pl.pallas_call(
+        back_kernel,
+        out_shape=(
+            jax.ShapeDtypeStruct(out_payload.shape, out_payload.dtype),
+            jax.ShapeDtypeStruct(lse_payload.shape, lse_payload.dtype),
+            jax.ShapeDtypeStruct((tokens, width), jnp.float32),
+            jax.ShapeDtypeStruct((tokens, heads_local), jnp.float32),
+        ),
+        in_specs=[vmem] * 5,
+        out_specs=(vmem,) * 4,
+        scratch_shapes=[
+            pltpu.VMEM(out_payload.shape, out_payload.dtype),
+            pltpu.VMEM(lse_payload.shape, lse_payload.dtype),
+            pltpu.SemaphoreType.DMA((n,)),
+            pltpu.SemaphoreType.DMA((n,)),
+            pltpu.SemaphoreType.DMA((n,)),
+            pltpu.SemaphoreType.DMA((n,)),
+        ],
+        compiler_params=pltpu.CompilerParams(collective_id=1, has_side_effects=True),
+    )(out_payload, lse_payload, q_self, k_self, v_self)
+
+
 def on_device(
     activations,
     w_query,
@@ -261,11 +375,6 @@
     keys = rotate(key_f.reshape(tok_rows, heads_local, HD), position).astype(jnp.bfloat16)
     values = value_f.astype(jnp.bfloat16)
     q_blocks = queries.reshape(REQ_DEV, block)
-    self_out, self_lse = self_attention(
-        queries.reshape(REQ_DEV, REQ_LEN, heads_local, HD),
-        keys.reshape(REQ_DEV, REQ_LEN, heads_local, HD),
-        values.reshape(REQ_DEV, REQ_LEN, heads_local, HD),
-    )
     levels_all = jnp.stack([root_all, middle_all, req_leaf], axis=0).reshape(3, leaf_count, REQ_DEV)
     level_count = levels_all.shape[0]
     items = level_count * REQ_DEV
@@ -306,24 +415,21 @@
         lengths,
         heads_local,
     )
-    flat_lse = node_lse.reshape(leaf_count * all_slots, REQ_LEN * heads_local)
-    lse_high = lax.reduce_precision(flat_lse, exponent_bits=8, mantissa_bits=7)
-    lse_low = flat_lse - lse_high
-    lse_pair = jnp.stack([lse_high, lse_low], axis=1).astype(jnp.bfloat16)
-    back_out = lax.all_to_all(
-        node_out.reshape(leaf_count, all_slots, REQ_LEN, width_local),
-        "leaf",
-        split_axis=0,
-        concat_axis=0,
-        tiled=True,
-    )
-    back_lse = lax.all_to_all(
-        lse_pair.reshape(leaf_count, all_slots, 2, REQ_LEN * heads_local),
-        "leaf",
-        split_axis=0,
-        concat_axis=0,
-        tiled=True,
-    )
+    lse_rows = 8
+    lse_payload = jnp.pad(
+        node_lse.reshape(leaf_count, all_slots * REQ_LEN * heads_local // 128, 128),
+        ((0, 0), (0, lse_rows - all_slots * REQ_LEN * heads_local // 128), (0, 0)),
+    )
+    back_out, back_lse, self_out, self_lse = back_exchange(
+        node_out.reshape(leaf_count, all_slots * REQ_LEN, width_local),
+        lse_payload,
+        queries.reshape(tok_rows, width_local),
+        keys.reshape(tok_rows, width_local),
+        values.reshape(tok_rows, width_local),
+        heads_local,
+    )
+    self_out = self_out.reshape(REQ_DEV, REQ_LEN, heads_local, HD)
+    self_lse = self_lse.reshape(REQ_DEV, REQ_LEN, heads_local)
     take = (
         (my_holders * all_slots + my_ranks)[:, None]
         == jnp.arange(leaf_count * all_slots, dtype=jnp.int32)[None, :]
@@ -332,12 +438,13 @@
         jnp.dot(take, back_out.reshape(leaf_count * all_slots, block), preferred_element_type=jnp.float32)
         .reshape(level_count, REQ_DEV, REQ_LEN, heads_local, HD)
     )
-    got_pair = jnp.dot(
-        take,
-        back_lse.reshape(leaf_count * all_slots, 2 * REQ_LEN * heads_local),
+    slot_lse = back_lse[:, : all_slots * REQ_LEN * heads_local // 128].reshape(
+        leaf_count * all_slots, REQ_LEN * heads_local
+    )
+    got_lse = jnp.dot(
+        take.astype(jnp.float32), slot_lse, precision=lax.Precision.HIGHEST,
         preferred_element_type=jnp.float32,
-    ).reshape(items, 2, REQ_LEN * heads_local)
-    got_lse = (got_pair[:, 0] + got_pair[:, 1]).reshape(level_count, REQ_DEV, REQ_LEN, heads_local)
+    ).reshape(level_count, REQ_DEV, REQ_LEN, heads_local)
     partial_out = jnp.concatenate([got_out, self_out[None]], axis=0)
     partial_lse = jnp.concatenate([got_lse, self_lse[None]], axis=0)
     highest = jnp.max(partial_lse, axis=0)

time: 231 us -> 249 us (1.078)
  Pallas kernels: 13.6 us -> 67.3 us
  starting transfers between devices: 29.8 us -> 7.73 us
  waiting for transfers between devices: 128 us -> 107 us
  local copies, waits for them, and re-layouts: 19.4 us -> 23.1 us
    pallas_call x0 -> x1, Pallas kernels: none -> 48.8 us  [back_exchange(): pl.pallas_call(back_kernel, out_shape=(jax.ShapeDtypeStruct(out_payload.s...]
    all_to_all x2 -> x0, waiting for transfers between devices: 25.2 us -> none  [the longest x1 20.1 us: on_device(): lax.all_to_all(node_out.reshape(leaf_count, all_slots, REQ_LEN, width_loc...]
    all_to_all x2 -> x0, starting transfers between devices: 21.9 us -> none  [the longest x1 15.3 us: on_device(): lax.all_to_all(lse_pair.reshape(leaf_count, all_slots, 2, REQ_LEN * heads...]
    reduce_scatter x1, waiting for transfers between devices: 39.5 us -> 53 us  [on_device(): lax.psum_scatter(partial_value.astype(jnp.bfloat16), 'mp', scatter_dimens...]
    all_to_all x1, waiting for transfers between devices: 22.9 us -> 16.1 us  [on_device(): lax.all_to_all(outgoing, 'leaf', split_axis=0, concat_axis=0, tiled=True)]
    pallas_call x1, Pallas kernels: 4.59 us -> 9.59 us  [node_attention(): pl.pallas_call(node_kernel, out_shape=(jax.ShapeDtypeStruct((slots * rows...]
    reshape x1 -> x2, local copies, waits for them, and re-layouts: 0.04 us -> 4.3 us  [the longest x1 4.21 us: on_device(): back_out.reshape(leaf_count * all_slots, block)]
    unnamed x17 -> x13, local copies, waits for them, and re-layouts: 6.34 us -> 2.47 us
  transfers between devices with their start and end apart: 5 -> 3, of which waited for: 5 -> 3; matrix products, arithmetic and copies ran while one was open for 7% -> 7% of each run, Pallas kernels for 0% -> 0%
where the time goes in v4:
time: 249 us; the launch traced here: 248 us
  waiting for transfers between devices  107 us (43%)
  Pallas kernels  67.3 us (27%)
  local copies, waits for them, and re-layouts  23.1 us (9%)
  matrix products  15.8 us (6%)
  between operations  13.8 us (6%)
  other arithmetic  13.5 us (5%)
  starting transfers between devices  7.73 us (3%)
    reduce_scatter x1, waiting for transfers between devices, on_device(): lax.psum_scatter(partial_value.astype(jnp.bfloat16), 'mp', scatter_dimens...  53 us
    pallas_call x1, Pallas kernels, back_exchange(): pl.pallas_call(back_kernel, out_shape=(jax.ShapeDtypeStruct(out_payload.s...  48.8 us
    all_gather x1, waiting for transfers between devices, on_device(): columns = lax.all_gather(activations, 'mp', axis=1, tiled=True)  37.1 us
    all_to_all x1, waiting for transfers between devices, on_device(): lax.all_to_all(outgoing, 'leaf', split_axis=0, concat_axis=0, tiled=True)  16.1 us
    dot_general x3, matrix products, on_device(): jnp.dot(columns, matrix, preferred_element_type=jnp.float32)  9.88 us
    pallas_call x1, Pallas kernels, node_attention(): pl.pallas_call(node_kernel, out_shape=(jax.ShapeDtypeStruct((slots * rows...  9.59 us
    pallas_call x1, Pallas kernels, mp_sum(): pl.pallas_call(sum_kernel, out_shape=jax.ShapeDtypeStruct(x.shape, x.dtyp...  8.94 us
    all_to_all x1, starting transfers between devices, on_device(): lax.all_to_all(outgoing, 'leaf', split_axis=0, concat_axis=0, tiled=True)  7.51 us
  transfers between devices with their start and end apart: 3, of which 3 were waited for; matrix products, arithmetic and copies ran while one was open for 7% of the time, Pallas kernels for 0%

profile of v4, /device:TPU:6, one launch (start us, length us, event | category | flops | bytes accessed | tf_op | source)
XLA Modules:
  0.0 248.2 jit_solution(3396978527504746254)
XLA Ops:
  6.5 0.7 all-gather.2.cloned.1.call-update
  7.3 0.8 stack.14
  8.0 0.9 select_reduce_fusion.4
  9.0 0.9 select_reduce_fusion.3
  10.0 0.9 select_reduce_fusion.1
  11.5 0.2 add_reduce_fusion
  13.1 0.9 select_reduce_fusion.5
  14.3 0.7 reduce_max.52.glen_ref
  15.3 0.5 multiply_cosine_fusion
  15.8 37.1 %all-gather.2.cloned.1.call-done = bf16[256,4096]{1,0:T(8,128)(2,1)} async-done(((bf16[256,512]{1,0:T(8,128)(2,1)}), bf16[256,4096]{1,0:T(8,128)(2,1)}) %all-gather.2.cloned.1.call-update) | async-done | bytes 2097168 | tf_op jit(solution)/shard_map/all_gather | solution.py:359
  52.9 3.1 %fusion.34 = f32[256,256]{0,1:T(8,128)S(1)} fusion(bf16[256,4096]{1,0:T(8,128)(2,1)} %all-gather.2.cloned.1.call-done, bf16[4096,256]{1,0:T(8,128)(2,1)} %param.12), kind=kOutput, calls=%fused_computation.93 | convolution fusion | flops 536870912 | bytes 4456448 | tf_op jit(solution)/shard_map/dot_general | solution.py:362
  56.3 0.1 copy.122
  56.4 0.3 multiply_subtract_fusion
  56.7 0.4 maximum_convert_fusion
  57.1 0.7 convolution_convert_fusion
  57.9 1.9 copy.126
  59.8 7.5 %all-to-all-start = ((bf16[32,2,64,256]{3,2,1,0:T(8,128)(2,1)}), bf16[32,2,64,256]{3,2,1,0:T(8,128)(2,1)}, u32[]{:S(2)}, u32[]{:S(2)}) async-start(bf16[32,2,64,256]{3,2,1,0:T(8,128)(2,1)} %bitcast.63), calls=%async_computation | async-start | bytes 4194304 | tf_op jit(solution)/shard_map/all_to_all | solution.py:404
  67.3 0.2 reduce-scatter.2.cloned.1.call-start
  68.0 0.6 select_select_fusion.mode_ref
  68.6 0.6 broadcast_select_fusion
  69.1 3.1 %fusion.35 = f32[256,256]{0,1:T(8,128)S(1)} fusion(bf16[256,4096]{1,0:T(8,128)(2,1)} %all-gather.2.cloned.1.call-done, bf16[4096,256]{1,0:T(8,128)(2,1)} %param.13), kind=kOutput, calls=%fused_computation.94 | convolution fusion | flops 536870912 | bytes 4456448 | tf_op jit(solution)/shard_map/dot_general | solution.py:362
  72.6 0.3 subtract_convert_fusion
  72.9 0.4 pad_maximum_fusion
  73.3 0.7 copy_bitcast_fusion
  74.0 3.6 %convolution_convert_fusion.2.v_ref = bf16[256,256]{1,0:T(8,128)(2,1)} fusion(bf16[256,4096]{1,0:T(8,128)(2,1)} %all-gather.2.cloned.1.call-done, bf16[4096,256]{1,0:T(8,128)(2,1)} %param.14), kind=kOutput, calls=%fused_computation.5 | convolution fusion | flops 536936448 | bytes 4325376 | tf_op jit(solution)/shard_map/dot_general | solution.py:362
  77.6 16.1 %all-to-all-done = bf16[32,2,64,256]{3,2,1,0:T(8,128)(2,1)} async-done(((bf16[32,2,64,256]{3,2,1,0:T(8,128)(2,1)}), bf16[32,2,64,256]{3,2,1,0:T(8,128)(2,1)}, u32[]{:S(2)}, u32[]{:S(2)}) %all-to-all-start) | async-done | bytes 2097184 | tf_op jit(solution)/shard_map/all_to_all | solution.py:404
  93.7 9.6 %shard_map.109 = (bf16[4096,256]{1,0:T(8,128)(2,1)}, f32[4096,2]{1,0:T(8,128)}) custom-call(s32[64]{0:T(128)} %get-tuple-element.43.slot_ref, s32[64]{0:T(128)} %get-tuple-element.42.len_ref, s32[8]{0:T(128)} %select_select_fusion.mode_ref, s32[8]{0:T(128)} %copy-done.2, s32[8]{0:T(128)} %reduce_max.52.glen_ref, bf16[4096,256]{1,0:T(8,128)(2,1)} %bitcast.5.q_ref, ...), custom_call_target="tpu_custom_call" | custom-call | flops 1073741824 | bytes 6291456 | tf_op jit(solution)/shard_map/pallas_call | solution.py:137
  103.3 2.8 %reshape_reshape.11 = f32[32,2,128]{2,1,0:T(2,128)S(1)} reshape(f32[4096,2]{1,0:T(8,128)} %get-tuple-element.12) | data formatting | bytes 65536 | tf_op jit(solution)/shard_map/reshape;reshape | solution.py:420
  106.1 0.7 pad.4.lse_in
  106.8 48.8 %shard_map.110 = (bf16[32,128,256]{2,1,0:T(8,128)(2,1)}, f32[32,8,128]{2,1,0:T(8,128)}, f32[256,256]{1,0:T(8,128)}, f32[256,2]{1,0:T(8,128)}) custom-call(bf16[32,128,256]{2,1,0:T(8,128)(2,1)} %bitcast.66, f32[32,8,128]{2,1,0:T(8,128)} %pad.4.lse_in, bf16[256,256]{1,0:T(8,128)(2,1)} %get-tuple-element.47.q_ref, bf16[256,256]{1,0:T(8,128)(2,1)} %get-tuple-element.46.k_ref, ...), custom_call_target="tpu_custom_call" | custom-call | tf_op jit(solution)/shard_map/pallas_call | solution.py:315
  155.6 0.9 slice.19
  156.5 1.0 copy.111
  157.5 1.0 copy.112
  158.6 0.3 fusion.33
  159.0 0.2 copy.113
  159.2 1.1 broadcast_in_dim_reshape.9
  160.3 0.2 copy.115
  160.5 4.2 %reshape.397 = bf16[64,16384]{1,0:T(8,128)(2,1)} reshape(bf16[32,128,256]{2,1,0:T(8,128)(2,1)} %get-tuple-element.15) | data formatting | bytes 4194304 | tf_op jit(solution)/shard_map/reshape | solution.py:438
  164.7 4.5 %dot_general.37 = bf16[64,2,128,64]{2,1,0,3:T(2,128)(2,1)} reshape(bf16[16384,64]{0,1:T(8,128)(2,1)} %bitcast.65) | data formatting | bytes 4194304 | tf_op jit(solution)/shard_map/dot_general | solution.py:438
  169.2 2.9 %fusion = f32[3,4,64,2,128]{4,1,3,2,0:T(4,128)S(1)} fusion(bf16[64,2,128,64]{2,1,0,3:T(2,128)(2,1)} %dot_general.37, s32[3,4]{1,0:T(4,128)S(1)} %add.92), kind=kOutput, calls=%fused_computation.2 | convolution fusion | flops 25166592 | bytes 2883632 | tf_op jit(solution)/shard_map/dot_general | solution.py:438
  172.0 0.8 fusion.3
  172.8 0.2 divide_convert_fusion
  173.2 2.1 convolution_convert_fusion.1
  175.3 53.0 %reduce-scatter.2.cloned.1.call-done = bf16[256,512]{1,0:T(8,128)(2,1)} async-done(((bf16[256,4096]{1,0:T(8,128)(2,1)}), bf16[256,512]{1,0:T(8,128)(2,1)}) %reduce-scatter.2.cloned.1.call-update) | async-done | bytes 262160 | tf_op jit(solution)/shard_map/reduce_scatter | solution.py:455
  228.2 1.6 fusion.7
  229.9 8.9 %shard_map.111 = f32[1,256]{1,0:T(1,128)} custom-call(f32[1,256]{1,0:T(1,128)} %bitcast.77), custom_call_target="tpu_custom_call" | custom-call | tf_op jit(solution)/shard_map/pallas_call | solution.py:189
  238.8 0.7 add_rsqrt_fusion
  239.5 1.8 fusion.6
  (65 shorter events, 4.1 us)
Async XLA Ops:
  6.5 166.6 %copy-start = (bf16[256,4096]{1,0:T(8,128)(2,1)S(1)}, bf16[256,4096]{1,0:T(8,128)(2,1)}, u32[]{:S(2)}) copy-start(bf16[256,4096]{1,0:T(8,128)(2,1)} %param.15) | copy-start | bytes 6291460
  6.5 46.4 %all-gather.2.cloned.1.call-start = ((), (), s32[]{:S(2)}) async-start(), calls=%async_computation.2 | async-start | bytes 2359296 | tf_op jit(solution)/shard_map/all_gather | solution.py:359
  15.1 41.0 %copy-start.2 = (s32[8]{0:T(128)}, s32[8]{0:T(128)S(1)}, u32[]{:S(2)}) copy-start(s32[8]{0:T(128)S(1)} %reduce_max.49.gnode_ref) | copy-start | bytes 100
  59.8 33.9 %all-to-all-start = ((bf16[32,2,64,256]{3,2,1,0:T(8,128)(2,1)}), bf16[32,2,64,256]{3,2,1,0:T(8,128)(2,1)}, u32[]{:S(2)}, u32[]{:S(2)}) async-start(bf16[32,2,64,256]{3,2,1,0:T(8,128)(2,1)} %bitcast.63), calls=%async_computation | async-start | bytes 4194304 | tf_op jit(solution)/shard_map/all_to_all | solution.py:404
  67.3 161.0 %reduce-scatter.2.cloned.1.call-start = ((), (), s32[]{:S(2)}) async-start(), calls=%async_computation.3 | async-start | bytes 2359296 | tf_op jit(solution)/shard_map/reduce_scatter | solution.py:455
  175.3 64.3 %copy-start.1 = (bf16[256,512]{1,0:T(8,128)(2,1)S(1)}, bf16[256,512]{1,0:T(8,128)(2,1)}, u32[]{:S(2)}) copy-start(bf16[256,512]{1,0:T(8,128)(2,1)} %param.11) | copy-start | bytes 786436
  175.3 64.3 %copy-start.3 = (f32[512]{0:T(512)S(1)}, f32[512]{0:T(512)}, u32[]{:S(2)}) copy-start(f32[512]{0:T(512)} %param.16) | copy-start | bytes 6148
Sparse Core Ops, SparseCore 0:
  9.1 43.7 all-gather.1
  175.4 52.7 reduce-scatter.1

commit v5 on v3

--- a/solution.py
+++ b/solution.py
@@ -328,10 +328,10 @@
         (my_holders * all_slots + my_ranks)[:, None]
         == jnp.arange(leaf_count * all_slots, dtype=jnp.int32)[None, :]
     ).astype(jnp.bfloat16)
-    got_out = (
-        jnp.dot(take, back_out.reshape(leaf_count * all_slots, block), preferred_element_type=jnp.float32)
-        .reshape(level_count, REQ_DEV, REQ_LEN, heads_local, HD)
-    )
+    chosen = my_holders * all_slots + my_ranks
+    got_out = jnp.take(
+        back_out.reshape(leaf_count * all_slots, REQ_LEN, width_local), chosen, axis=0
+    ).astype(jnp.float32).reshape(level_count, REQ_DEV, REQ_LEN, heads_local, HD)
     got_pair = jnp.dot(
         take,
         back_lse.reshape(leaf_count * all_slots, 2 * REQ_LEN * heads_local),

time: 231 us -> 224 us (0.970)
  starting transfers between devices: 29.8 us -> 19.5 us
  Pallas kernels: 13.6 us -> 23.6 us
  local copies, waits for them, and re-layouts: 19.4 us -> 13.7 us
  matrix products: 13.6 us -> 10.7 us
    all_to_all x1, starting transfers between devices: 15.3 us -> 5.06 us  [on_device(): lax.all_to_all(lse_pair.reshape(leaf_count, all_slots, 2, REQ_LEN * heads...]
    pallas_call x1, Pallas kernels: 4.59 us -> 14.6 us  [node_attention(): pl.pallas_call(node_kernel, out_shape=(jax.ShapeDtypeStruct((slots * rows...]
    dot_general x1 -> x0, local copies, waits for them, and re-layouts: 4.46 us -> none  [on_device(): jnp.dot(take, back_out.reshape(leaf_count * all_slots, block), preferred_...]
    unnamed x17 -> x15, local copies, waits for them, and re-layouts: 6.34 us -> 2.02 us
    dot_general x1 -> x0, matrix products: 2.89 us -> none  [on_device(): jnp.dot(take, back_out.reshape(leaf_count * all_slots, block), preferred_...]
where the time goes in v5:
time: 224 us; the launch traced here: 223 us
  waiting for transfers between devices  128 us (57%)
  Pallas kernels  23.6 us (11%)
  starting transfers between devices  19.5 us (9%)
  between operations  13.9 us (6%)
  other arithmetic  13.8 us (6%)
  local copies, waits for them, and re-layouts  13.7 us (6%)
  matrix products  10.7 us (5%)
    all_gather x1, waiting for transfers between devices, on_device(): columns = lax.all_gather(activations, 'mp', axis=1, tiled=True)  40.1 us
    reduce_scatter x1, waiting for transfers between devices, on_device(): lax.psum_scatter(partial_value.astype(jnp.bfloat16), 'mp', scatter_dimens...  39.9 us
    all_to_all x1, waiting for transfers between devices, on_device(): lax.all_to_all(outgoing, 'leaf', split_axis=0, concat_axis=0, tiled=True)  22.9 us
    all_to_all x1, waiting for transfers between devices, on_device(): lax.all_to_all(node_out.reshape(leaf_count, all_slots, REQ_LEN, width_loc...  19.2 us
    pallas_call x1, Pallas kernels, node_attention(): pl.pallas_call(node_kernel, out_shape=(jax.ShapeDtypeStruct((slots * rows...  14.6 us
    pallas_call x1, Pallas kernels, mp_sum(): pl.pallas_call(sum_kernel, out_shape=jax.ShapeDtypeStruct(x.shape, x.dtyp...  8.94 us
    all_to_all x1, starting transfers between devices, on_device(): lax.all_to_all(outgoing, 'leaf', split_axis=0, concat_axis=0, tiled=True)  7.64 us
    dot_general x3, matrix products, on_device(): jnp.dot(columns, matrix, preferred_element_type=jnp.float32)  7.19 us
  transfers between devices with their start and end apart: 5, of which 5 were waited for; matrix products, arithmetic and copies ran while one was open for 7% of the time, Pallas kernels for 0%

profile of v5, /device:TPU:6, one launch (start us, length us, event | category | flops | bytes accessed | tf_op | source)
XLA Modules:
  0.0 223.4 jit_solution(162811903863561846)
XLA Ops:
  6.5 0.7 all-gather.2.cloned.1.call-update
  7.3 0.8 stack.19
  8.0 0.9 select_reduce_fusion.4
  9.0 0.9 select_reduce_fusion.3
  10.0 0.9 select_reduce_fusion.1
  11.5 0.2 add_reduce_fusion
  12.6 0.3 multiply_cosine_fusion
  12.9 40.1 %all-gather.2.cloned.1.call-done = bf16[256,4096]{1,0:T(8,128)(2,1)} async-done(((bf16[256,512]{1,0:T(8,128)(2,1)}), bf16[256,4096]{1,0:T(8,128)(2,1)}) %all-gather.2.cloned.1.call-update) | async-done | bytes 2097168 | tf_op jit(solution)/shard_map/all_gather | solution.py:245
  52.9 3.3 %fusion.47 = f32[256,256]{0,1:T(8,128)S(1)} fusion(bf16[256,4096]{1,0:T(8,128)(2,1)} %all-gather.2.cloned.1.call-done, bf16[4096,256]{1,0:T(8,128)(2,1)} %param.13), kind=kOutput, calls=%fused_computation.120 | convolution fusion | flops 536870912 | bytes 4456448 | tf_op jit(solution)/shard_map/dot_general | solution.py:248
  56.3 0.2 copy-done.2
  56.4 1.0 fusion.46
  57.7 0.7 convolution_convert_fusion
  58.4 1.8 copy.145
  60.2 7.6 %all-to-all-start = ((bf16[32,2,64,256]{3,2,1,0:T(8,128)(2,1)}), bf16[32,2,64,256]{3,2,1,0:T(8,128)(2,1)}, u32[]{:S(2)}, u32[]{:S(2)}) async-start(bf16[32,2,64,256]{3,2,1,0:T(8,128)(2,1)} %bitcast.77), calls=%async_computation | async-start | bytes 4194304 | tf_op jit(solution)/shard_map/all_to_all | solution.py:295
  68.4 0.2 select_reduce_fusion.5
  68.9 0.6 reduce_max.61.glen_ref
  70.3 0.5 select_select_fusion.mode_ref
  70.9 0.5 broadcast_select_fusion.1
  71.4 22.9 %all-to-all-done = bf16[32,2,64,256]{3,2,1,0:T(8,128)(2,1)} async-done(((bf16[32,2,64,256]{3,2,1,0:T(8,128)(2,1)}), bf16[32,2,64,256]{3,2,1,0:T(8,128)(2,1)}, u32[]{:S(2)}, u32[]{:S(2)}) %all-to-all-start) | async-done | bytes 2097184 | tf_op jit(solution)/shard_map/all_to_all | solution.py:295
  94.3 14.6 %shard_map.109 = (bf16[4096,256]{1,0:T(8,128)(2,1)}, f32[4096,2]{1,0:T(8,128)}) custom-call(s32[64]{0:T(128)} %get-tuple-element.37.slot_ref, s32[64]{0:T(128)} %get-tuple-element.36.len_ref, s32[8]{0:T(128)} %select_select_fusion.mode_ref, s32[8]{0:T(128)} %copy-done.4, s32[8]{0:T(128)} %reduce_max.61.glen_ref, bf16[4096,256]{1,0:T(8,128)(2,1)} %bitcast.3.q_ref, ...), custom_call_target="tpu_custom_call" | custom-call | flops 1073741824 | bytes 6291456 | tf_op jit(solution)/shard_map/pallas_call | solution.py:137
  108.9 2.8 %reshape_reshape.10 = f32[32,2,1,128]{3,1,0,2:T(2,128)S(1)} reshape(f32[4096,2]{1,0:T(8,128)} %get-tuple-element.7) | data formatting | bytes 65536 | tf_op jit(solution)/shard_map/reshape;reshape | solution.py:309
  111.8 0.6 copy.121
  112.5 5.1 %all-to-all-start.1 = ((bf16[32,2,2,128]{3,1,2,0:T(2,128)(2,1)}), bf16[32,2,2,128]{3,1,2,0:T(2,128)(2,1)S(1)}, u32[]{:S(2)}, u32[]{:S(2)}) async-start(bf16[32,2,2,128]{3,1,2,0:T(2,128)(2,1)} %copy.121), calls=%async_computation.1 | async-start | bytes 65536 | tf_op jit(solution)/shard_map/all_to_all | solution.py:320
  117.6 5.4 %all-to-all-done.1 = bf16[32,2,2,128]{3,1,2,0:T(2,128)(2,1)S(1)} async-done(((bf16[32,2,2,128]{3,1,2,0:T(2,128)(2,1)}), bf16[32,2,2,128]{3,1,2,0:T(2,128)(2,1)S(1)}, u32[]{:S(2)}, u32[]{:S(2)}) %all-to-all-start.1) | async-done | bytes 32800 | tf_op jit(solution)/shard_map/all_to_all | solution.py:320
  123.1 6.6 %all-to-all-start.2 = ((bf16[32,2,64,256]{3,2,1,0:T(8,128)(2,1)}), bf16[32,2,64,256]{3,2,1,0:T(8,128)(2,1)}, u32[]{:S(2)}, u32[]{:S(2)}) async-start(bf16[32,2,64,256]{3,2,1,0:T(8,128)(2,1)} %bitcast.79), calls=%async_computation.2 | async-start | bytes 4194304 | tf_op jit(solution)/shard_map/all_to_all | solution.py:313
  129.7 0.2 reduce-scatter.2.cloned.1.call-start
  130.2 2.9 %convolution_convert_fusion.2 = bf16[256,256]{1,0:T(8,128)(2,1)S(1)} fusion(bf16[256,4096]{1,0:T(8,128)(2,1)} %all-gather.2.cloned.1.call-done, bf16[4096,256]{1,0:T(8,128)(2,1)} %param.14), kind=kOutput, calls=%fused_computation.8 | convolution fusion | flops 536936448 | bytes 4325376 | tf_op jit(solution)/shard_map/dot_general | solution.py:248
  133.3 0.1 copy.127
  133.7 0.1 copy.126
  133.9 0.1 copy.125
  134.0 0.3 fusion.45
  134.4 0.2 fusion.2
  134.7 0.9 copy.136
  135.6 0.2 fusion.23
  135.9 0.1 add.147
  136.2 0.2 reduce_max.64
  136.7 0.2 copy.133
  136.9 19.2 %all-to-all-done.2 = bf16[32,2,64,256]{3,2,1,0:T(8,128)(2,1)} async-done(((bf16[32,2,64,256]{3,2,1,0:T(8,128)(2,1)}), bf16[32,2,64,256]{3,2,1,0:T(8,128)(2,1)}, u32[]{:S(2)}, u32[]{:S(2)}) %all-to-all-start.2) | async-done | bytes 2097184 | tf_op jit(solution)/shard_map/all_to_all | solution.py:313
  156.1 2.2 gather_fusion
  158.4 0.4 fusion.8
  158.8 2.3 %fusion.3 = f32[4,64,2,128]{3,2,1,0:T(2,128)S(1)} fusion(f32[1,4,64,2,128]{4,3,2,1,0:T(2,128)} %copy.136, f32[3,4,64,2,128]{4,3,2,1,0:T(2,128)S(1)} %fusion.8, f32[4,4,64,2]{3,2,1,0:T(8,128)S(1)} %copy.133), kind=kLoop, calls=%fused_computation.10 | loop fusion | flops 720896 | bytes 1318912 | tf_op jit(solution)/shard_map/reduce_sum | solution.py:345
  161.1 0.3 divide_convert_fusion
  161.5 2.1 convolution_convert_fusion.1
  163.6 39.9 %reduce-scatter.2.cloned.1.call-done = bf16[256,512]{1,0:T(8,128)(2,1)} async-done(((bf16[256,4096]{1,0:T(8,128)(2,1)}), bf16[256,512]{1,0:T(8,128)(2,1)}) %reduce-scatter.2.cloned.1.call-update) | async-done | bytes 262160 | tf_op jit(solution)/shard_map/reduce_scatter | solution.py:348
  203.5 1.6 fusion.7
  205.1 8.9 %shard_map.110 = f32[1,256]{1,0:T(1,128)} custom-call(f32[1,256]{1,0:T(1,128)} %bitcast.86), custom_call_target="tpu_custom_call" | custom-call | tf_op jit(solution)/shard_map/pallas_call | solution.py:189
  214.1 0.7 add_rsqrt_fusion
  214.8 1.8 fusion.6
  (88 shorter events, 5.0 us)
Async XLA Ops:
  6.5 154.9 %copy-start = (bf16[256,4096]{1,0:T(8,128)(2,1)S(1)}, bf16[256,4096]{1,0:T(8,128)(2,1)}, u32[]{:S(2)}) copy-start(bf16[256,4096]{1,0:T(8,128)(2,1)} %param.15) | copy-start | bytes 6291460
  6.5 46.4 %all-gather.2.cloned.1.call-start = ((), (), s32[]{:S(2)}) async-start(), calls=%async_computation.4 | async-start | bytes 2359296 | tf_op jit(solution)/shard_map/all_gather | solution.py:245
  52.9 3.3 %copy-start.1 = (bf16[256,4096]{1,0:T(8,128)(2,1)S(1)}, bf16[256,4096]{1,0:T(8,128)(2,1)}, u32[]{:S(2)}) copy-start(bf16[256,4096]{1,0:T(8,128)(2,1)} %all-gather.2.cloned.1.call-done) | copy-start | bytes 6291460
  52.9 3.5 %copy-start.2 = (bf16[4096,256]{1,0:T(8,128)(2,1)S(1)}, bf16[4096,256]{1,0:T(8,128)(2,1)}, u32[]{:S(2)}) copy-start(bf16[4096,256]{1,0:T(8,128)(2,1)} %param.12) | copy-start | bytes 6291460
  60.2 8.1 %copy-start.5 = (s32[256]{0:T(256)S(1)}, s32[256]{0:T(256)}, u32[]{:S(2)}) copy-start(s32[256]{0:T(256)} %param.20) | copy-start | bytes 3076
  60.2 34.0 %all-to-all-start = ((bf16[32,2,64,256]{3,2,1,0:T(8,128)(2,1)}), bf16[32,2,64,256]{3,2,1,0:T(8,128)(2,1)}, u32[]{:S(2)}, u32[]{:S(2)}) async-start(bf16[32,2,64,256]{3,2,1,0:T(8,128)(2,1)} %bitcast.77), calls=%async_computation | async-start | bytes 4194304 | tf_op jit(solution)/shard_map/all_to_all | solution.py:295
  69.7 24.6 %copy-start.4 = (s32[8]{0:T(128)}, s32[8]{0:T(128)S(1)}, u32[]{:S(2)}) copy-start(s32[8]{0:T(128)S(1)} %reduce_max.58.gnode_ref) | copy-start | bytes 100
  112.5 10.6 %all-to-all-start.1 = ((bf16[32,2,2,128]{3,1,2,0:T(2,128)(2,1)}), bf16[32,2,2,128]{3,1,2,0:T(2,128)(2,1)S(1)}, u32[]{:S(2)}, u32[]{:S(2)}) async-start(bf16[32,2,2,128]{3,1,2,0:T(2,128)(2,1)} %copy.121), calls=%async_computation.1 | async-start | bytes 65536 | tf_op jit(solution)/shard_map/all_to_all | solution.py:320
  123.1 33.0 %all-to-all-start.2 = ((bf16[32,2,64,256]{3,2,1,0:T(8,128)(2,1)}), bf16[32,2,64,256]{3,2,1,0:T(8,128)(2,1)}, u32[]{:S(2)}, u32[]{:S(2)}) async-start(bf16[32,2,64,256]{3,2,1,0:T(8,128)(2,1)} %bitcast.79), calls=%async_computation.2 | async-start | bytes 4194304 | tf_op jit(solution)/shard_map/all_to_all | solution.py:313
  129.7 73.8 %reduce-scatter.2.cloned.1.call-start = ((), (), s32[]{:S(2)}) async-start(), calls=%async_computation.5 | async-start | bytes 2359296 | tf_op jit(solution)/shard_map/reduce_scatter | solution.py:348
  163.6 51.2 %copy-start.3 = (bf16[256,512]{1,0:T(8,128)(2,1)S(1)}, bf16[256,512]{1,0:T(8,128)(2,1)}, u32[]{:S(2)}) copy-start(bf16[256,512]{1,0:T(8,128)(2,1)} %param.11) | copy-start | bytes 786436
  163.6 51.2 %copy-start.6 = (f32[512]{0:T(512)S(1)}, f32[512]{0:T(512)}, u32[]{:S(2)}) copy-start(f32[512]{0:T(512)} %param.16) | copy-start | bytes 6148
Sparse Core Ops, SparseCore 0:
  9.1 43.7 all-gather.1
  163.7 39.7 reduce-scatter.1

commit v6 on v3

--- a/solution.py
+++ b/solution.py
@@ -42,6 +42,7 @@
 
 
 GROUP = 8
+PAD_ROWS = 80
 
 
 def attend(q, k, v, length, rows, cache_rows):
@@ -62,6 +63,7 @@
 ):
     total_rows, width = q_ref.shape
     cache_rows = k_ref.shape[1]
+    out_rows = out_ref.shape[1]
     heads = width // HD
     groups = mode_ref.shape[0]
     span = GROUP * REQ_LEN
@@ -79,12 +81,12 @@
                     q_ref[rows, cols], k_ref[node, :, cols], v_ref[node, :, cols],
                     length, REQ_LEN, cache_rows,
                 )
-                out_ref[rows, cols] = o.astype(out_ref.dtype)
+                out_ref[i, pl.ds(0, REQ_LEN), cols] = o.astype(out_ref.dtype)
                 lse_ref[rows, pl.ds(h, 1)] = lse
 
         @pl.when(length == 0)
         def _():
-            out_ref[rows, :] = jnp.zeros((REQ_LEN, width), out_ref.dtype)
+            out_ref[i] = jnp.zeros((out_rows, width), out_ref.dtype)
             lse_ref[rows, :] = jnp.zeros((REQ_LEN, heads), lse_ref.dtype)
 
         return carry
@@ -95,7 +97,8 @@
 
         @pl.when(mode == 0)
         def _():
-            out_ref[rows, :] = jnp.zeros((span, width), out_ref.dtype)
+            for j in range(GROUP):
+                out_ref[g * GROUP + j] = jnp.zeros((out_rows, width), out_ref.dtype)
             lse_ref[rows, :] = jnp.zeros((span, heads), lse_ref.dtype)
 
         @pl.when(mode == 1)
@@ -108,7 +111,10 @@
                     q_ref[rows, cols], k_ref[node, :, cols], v_ref[node, :, cols],
                     length, span, cache_rows,
                 )
-                out_ref[rows, cols] = o.astype(out_ref.dtype)
+                for j in range(GROUP):
+                    out_ref[g * GROUP + j, pl.ds(0, REQ_LEN), cols] = (
+                        o[j * REQ_LEN : (j + 1) * REQ_LEN].astype(out_ref.dtype)
+                    )
                 lse_ref[rows, pl.ds(h, 1)] = lse
 
         @pl.when(mode == 2)
@@ -137,7 +143,7 @@
     out, lse = pl.pallas_call(
         node_kernel,
         out_shape=(
-            jax.ShapeDtypeStruct((slots * rows, width), jnp.bfloat16),
+            jax.ShapeDtypeStruct((slots, PAD_ROWS, width), jnp.bfloat16),
             jax.ShapeDtypeStruct((slots * rows, heads_local), jnp.float32),
         ),
         in_specs=[smem] * 5 + [vmem] * 3,
@@ -151,7 +157,7 @@
         local_slot, lengths, mode, group_node, group_len,
         queries.reshape(slots * rows, width), key_cache, value_cache,
     )
-    return out.reshape(slots, rows, width), lse.reshape(slots, rows, heads_local)
+    return out, lse.reshape(slots, rows, heads_local)
 
 
 def sum_kernel(x_ref, out_ref, recv, send_sem, recv_sem):
@@ -306,38 +312,34 @@
         lengths,
         heads_local,
     )
-    flat_lse = node_lse.reshape(leaf_count * all_slots, REQ_LEN * heads_local)
+    slot_count = leaf_count * all_slots
+    flat_lse = node_lse.reshape(slot_count, REQ_LEN * heads_local)
     lse_high = lax.reduce_precision(flat_lse, exponent_bits=8, mantissa_bits=7)
     lse_low = flat_lse - lse_high
-    lse_pair = jnp.stack([lse_high, lse_low], axis=1).astype(jnp.bfloat16)
+    lse_rows = jnp.pad(
+        jnp.concatenate([lse_high, lse_low], axis=1).astype(jnp.bfloat16).reshape(
+            slot_count, 1, 2 * REQ_LEN * heads_local
+        ),
+        ((0, 0), (0, PAD_ROWS - REQ_LEN - 1), (0, width_local - 2 * REQ_LEN * heads_local)),
+    )
+    payload = lax.dynamic_update_slice(node_out, lse_rows, (0, REQ_LEN, 0))
     back_out = lax.all_to_all(
-        node_out.reshape(leaf_count, all_slots, REQ_LEN, width_local),
+        payload.reshape(leaf_count, all_slots, PAD_ROWS, width_local),
         "leaf",
         split_axis=0,
         concat_axis=0,
         tiled=True,
     )
-    back_lse = lax.all_to_all(
-        lse_pair.reshape(leaf_count, all_slots, 2, REQ_LEN * heads_local),
-        "leaf",
-        split_axis=0,
-        concat_axis=0,
-        tiled=True,
-    )
-    take = (
-        (my_holders * all_slots + my_ranks)[:, None]
-        == jnp.arange(leaf_count * all_slots, dtype=jnp.int32)[None, :]
-    ).astype(jnp.bfloat16)
-    got_out = (
-        jnp.dot(take, back_out.reshape(leaf_count * all_slots, block), preferred_element_type=jnp.float32)
-        .reshape(level_count, REQ_DEV, REQ_LEN, heads_local, HD)
-    )
-    got_pair = jnp.dot(
-        take,
-        back_lse.reshape(leaf_count * all_slots, 2 * REQ_LEN * heads_local),
-        preferred_element_type=jnp.float32,
-    ).reshape(items, 2, REQ_LEN * heads_local)
-    got_lse = (got_pair[:, 0] + got_pair[:, 1]).reshape(level_count, REQ_DEV, REQ_LEN, heads_local)
+    chosen = my_holders * all_slots + my_ranks
+    got = jnp.take(back_out.reshape(slot_count, PAD_ROWS, width_local), chosen, axis=0)
+    got_out = got[:, :REQ_LEN].astype(jnp.float32).reshape(
+        level_count, REQ_DEV, REQ_LEN, heads_local, HD
+    )
+    lse_width = REQ_LEN * heads_local
+    got_pair = got[:, REQ_LEN, : 2 * lse_width].astype(jnp.float32)
+    got_lse = (got_pair[:, :lse_width] + got_pair[:, lse_width:]).reshape(
+        level_count, REQ_DEV, REQ_LEN, heads_local
+    )
     partial_out = jnp.concatenate([got_out, self_out[None]], axis=0)
     partial_lse = jnp.concatenate([got_lse, self_lse[None]], axis=0)
     highest = jnp.max(partial_lse, axis=0)

time: 231 us -> 220 us (0.952)
  starting transfers between devices: 29.8 us -> 17.3 us
  local copies, waits for them, and re-layouts: 19.4 us -> 14.5 us
  Pallas kernels: 13.6 us -> 18.2 us
  other arithmetic: 11.9 us -> 15.4 us
  matrix products: 13.6 us -> 10.5 us
    all_to_all x2 -> x1, starting transfers between devices: 21.9 us -> 9.39 us  [on_device(): lax.all_to_all(payload.reshape(leaf_count, all_slots, PAD_ROWS, width_loc...]
    pallas_call x1, Pallas kernels: 4.59 us -> 9.24 us  [node_attention(): pl.pallas_call(node_kernel, out_shape=(jax.ShapeDtypeStruct((slots, PAD_R...]
    dot_general x1 -> x0, local copies, waits for them, and re-layouts: 4.46 us -> none  [on_device(): jnp.dot(take, back_out.reshape(leaf_count * all_slots, block), preferred_...]
    unnamed x17 -> x16, local copies, waits for them, and re-layouts: 6.34 us -> 2.02 us
    dot_general x2 -> x0, matrix products: 3.08 us -> none  [the longest x1 2.89 us: on_device(): jnp.dot(take, back_out.reshape(leaf_count * all_slots, block), preferred_...]
    gather x0 -> x1, local copies, waits for them, and re-layouts: none -> 2.32 us  [on_device(): jnp.take(back_out.reshape(slot_count, PAD_ROWS, width_local), chosen, axi...]
    all_to_all x2 -> x1, waiting for transfers between devices: 25.2 us -> 26 us  [on_device(): lax.all_to_all(payload.reshape(leaf_count, all_slots, PAD_ROWS, width_loc...]
  transfers between devices with their start and end apart: 5 -> 4, of which waited for: 5 -> 4; matrix products, arithmetic and copies ran while one was open for 7% -> 7% of each run, Pallas kernels for 0% -> 0%
where the time goes in v6:
time: 220 us
  waiting for transfers between devices  130 us (59%)
  Pallas kernels  18.2 us (8%)
  starting transfers between devices  17.3 us (8%)
  other arithmetic  15.4 us (7%)
  local copies, waits for them, and re-layouts  14.5 us (7%)
  between operations  13.9 us (6%)
  matrix products  10.5 us (5%)
    reduce_scatter x1, waiting for transfers between devices, on_device(): lax.psum_scatter(partial_value.astype(jnp.bfloat16), 'mp', scatter_dimens...  40.4 us
    all_gather x1, waiting for transfers between devices, on_device(): columns = lax.all_gather(activations, 'mp', axis=1, tiled=True)  40.1 us
    all_to_all x1, waiting for transfers between devices, on_device(): lax.all_to_all(payload.reshape(leaf_count, all_slots, PAD_ROWS, width_loc...  26 us
    all_to_all x1, waiting for transfers between devices, on_device(): lax.all_to_all(outgoing, 'leaf', split_axis=0, concat_axis=0, tiled=True)  22.8 us
    all_to_all x1, starting transfers between devices, on_device(): lax.all_to_all(payload.reshape(leaf_count, all_slots, PAD_ROWS, width_loc...  9.39 us
    pallas_call x1, Pallas kernels, node_attention(): pl.pallas_call(node_kernel, out_shape=(jax.ShapeDtypeStruct((slots, PAD_R...  9.24 us
    pallas_call x1, Pallas kernels, mp_sum(): pl.pallas_call(sum_kernel, out_shape=jax.ShapeDtypeStruct(x.shape, x.dtyp...  8.92 us
    all_to_all x1, starting transfers between devices, on_device(): lax.all_to_all(outgoing, 'leaf', split_axis=0, concat_axis=0, tiled=True)  7.64 us
  transfers between devices with their start and end apart: 4, of which 4 were waited for; matrix products, arithmetic and copies ran while one was open for 7% of the time, Pallas kernels for 0%

profile of v6, /device:TPU:6, one launch (start us, length us, event | category | flops | bytes accessed | tf_op | source)
XLA Modules:
  0.0 219.8 jit_solution(18023992238780580005)
XLA Ops:
  6.5 0.7 all-gather.2.cloned.1.call-update
  7.3 0.8 stack.14
  8.0 0.9 select_reduce_fusion.4
  9.0 0.9 select_reduce_fusion.3
  10.0 0.9 select_reduce_fusion.1
  11.5 0.2 add_reduce_fusion
  12.6 0.3 multiply_cosine_fusion
  12.9 40.1 %all-gather.2.cloned.1.call-done = bf16[256,4096]{1,0:T(8,128)(2,1)} async-done(((bf16[256,512]{1,0:T(8,128)(2,1)}), bf16[256,4096]{1,0:T(8,128)(2,1)}) %all-gather.2.cloned.1.call-update) | async-done | bytes 2097168 | tf_op jit(solution)/shard_map/all_gather | solution.py:251
  52.9 3.3 %fusion.46 = f32[256,256]{0,1:T(8,128)S(1)} fusion(bf16[256,4096]{1,0:T(8,128)(2,1)} %all-gather.2.cloned.1.call-done, bf16[4096,256]{1,0:T(8,128)(2,1)} %param.13), kind=kOutput, calls=%fused_computation.120 | convolution fusion | flops 536870912 | bytes 4456448 | tf_op jit(solution)/shard_map/dot_general | solution.py:254
  56.3 0.2 copy-done.2
  56.4 1.0 fusion.45
  57.7 0.7 convolution_convert_fusion
  58.4 1.8 copy.140
  60.2 7.6 %all-to-all-start = ((bf16[32,2,64,256]{3,2,1,0:T(8,128)(2,1)}), bf16[32,2,64,256]{3,2,1,0:T(8,128)(2,1)}, u32[]{:S(2)}, u32[]{:S(2)}) async-start(bf16[32,2,64,256]{3,2,1,0:T(8,128)(2,1)} %bitcast.67), calls=%async_computation | async-start | bytes 4194304 | tf_op jit(solution)/shard_map/all_to_all | solution.py:301
  68.4 0.2 select_reduce_fusion.5
  69.4 0.7 reduce_max.61.glen_ref
  70.3 0.5 select_select_fusion.mode_ref
  70.8 0.6 broadcast_select_fusion.1
  71.4 22.8 %all-to-all-done = bf16[32,2,64,256]{3,2,1,0:T(8,128)(2,1)} async-done(((bf16[32,2,64,256]{3,2,1,0:T(8,128)(2,1)}), bf16[32,2,64,256]{3,2,1,0:T(8,128)(2,1)}, u32[]{:S(2)}, u32[]{:S(2)}) %all-to-all-start) | async-done | bytes 2097184 | tf_op jit(solution)/shard_map/all_to_all | solution.py:301
  94.3 9.2 %shard_map.109 = (bf16[64,80,256]{2,1,0:T(8,128)(2,1)}, f32[4096,2]{1,0:T(8,128)}) custom-call(s32[64]{0:T(128)} %get-tuple-element.37.slot_ref, s32[64]{0:T(128)} %get-tuple-element.36.len_ref, s32[8]{0:T(128)} %select_select_fusion.mode_ref, s32[8]{0:T(128)} %copy-done.4, s32[8]{0:T(128)} %reduce_max.61.glen_ref, bf16[4096,256]{1,0:T(8,128)(2,1)} %bitcast.2.q_ref, ...), custom_call_target="tpu_custom_call" | custom-call | flops 1073741824 | bytes 6291456 | tf_op jit(solution)/shard_map/pallas_call | solution.py:143
  103.5 2.7 %reshape_reshape.7 = f32[64,128]{1,0:T(8,128)S(1)} reshape(f32[4096,2]{1,0:T(8,128)} %get-tuple-element.8) | data formatting | bytes 65536 | tf_op jit(solution)/shard_map/reshape;reshape | solution.py:316
  106.3 1.0 fusion.11
  107.3 9.4 %all-to-all-start.1 = ((bf16[32,2,80,256]{3,2,1,0:T(8,128)(2,1)}), bf16[32,2,80,256]{3,2,1,0:T(8,128)(2,1)}, u32[]{:S(2)}, u32[]{:S(2)}) async-start(bf16[32,2,80,256]{3,2,1,0:T(8,128)(2,1)} %bitcast.69), calls=%async_computation.1 | async-start | bytes 5242880 | tf_op jit(solution)/shard_map/all_to_all | solution.py:326
  116.7 0.2 reduce-scatter.2.cloned.1.call-start
  117.4 0.1 copy.123
  117.7 0.1 copy.122
  117.8 0.1 copy.121
  118.0 0.1 copy.120
  118.1 2.9 %convolution_convert_fusion.2 = bf16[256,256]{1,0:T(8,128)(2,1)S(1)} fusion(bf16[256,4096]{1,0:T(8,128)(2,1)} %all-gather.2.cloned.1.call-done, bf16[4096,256]{1,0:T(8,128)(2,1)} %param.14), kind=kOutput, calls=%fused_computation.8 | convolution fusion | flops 536936448 | bytes 4325376 | tf_op jit(solution)/shard_map/dot_general | solution.py:254
  121.1 0.3 fusion.44
  121.5 0.2 fusion.2
  121.7 0.9 copy.131
  122.6 26.0 %all-to-all-done.1 = bf16[32,2,80,256]{3,2,1,0:T(8,128)(2,1)} async-done(((bf16[32,2,80,256]{3,2,1,0:T(8,128)(2,1)}), bf16[32,2,80,256]{3,2,1,0:T(8,128)(2,1)}, u32[]{:S(2)}, u32[]{:S(2)}) %all-to-all-start.1) | async-done | bytes 2621472 | tf_op jit(solution)/shard_map/all_to_all | solution.py:326
  148.6 2.3 %gather_fusion = bf16[12,80,256]{2,1,0:T(8,128)(2,1)S(1)} fusion(bf16[64,80,256]{2,1,0:T(8,128)(2,1)} %bitcast.6, s32[1024]{0:T(1024)S(1)} %pad_clamp_fusion), kind=kCustom, calls=%fused_computation | custom fusion | bytes 983088 | tf_op jit(solution)/shard_map/jit(_take)/gather | solution.py:334
  151.1 1.0 slice_convert_fusion
  152.0 1.5 reshape.450
  153.7 0.1 concatenate.55
  153.8 0.1 copy.124
  154.0 0.2 reduce_max.64
  154.3 0.2 copy.128
  154.7 2.3 %fusion.5 = f32[4,64,2,128]{3,2,1,0:T(2,128)S(1)} fusion(f32[1,4,64,2,128]{4,3,2,1,0:T(2,128)} %copy.131, f32[3,4,64,2,128]{4,3,2,1,0:T(2,128)S(1)} %reshape.450, f32[4,4,64,2]{3,2,1,0:T(8,128)S(1)} %copy.128), kind=kLoop, calls=%fused_computation.13 | loop fusion | flops 720896 | bytes 1318912 | tf_op jit(solution)/shard_map/reduce_sum | solution.py:347
  157.0 0.3 divide_convert_fusion
  157.3 2.1 convolution_convert_fusion.1
  159.4 40.4 %reduce-scatter.2.cloned.1.call-done = bf16[256,512]{1,0:T(8,128)(2,1)} async-done(((bf16[256,4096]{1,0:T(8,128)(2,1)}), bf16[256,512]{1,0:T(8,128)(2,1)}) %reduce-scatter.2.cloned.1.call-update) | async-done | bytes 262160 | tf_op jit(solution)/shard_map/reduce_scatter | solution.py:350
  199.9 1.6 fusion.9
  201.5 8.9 %shard_map.110 = f32[1,256]{1,0:T(1,128)} custom-call(f32[1,256]{1,0:T(1,128)} %bitcast.76), custom_call_target="tpu_custom_call" | custom-call | tf_op jit(solution)/shard_map/pallas_call | solution.py:195
  210.4 0.7 add_rsqrt_fusion
  211.1 1.8 fusion.8
  (86 shorter events, 4.6 us)
Async XLA Ops:
  6.5 150.8 %copy-start = (bf16[256,4096]{1,0:T(8,128)(2,1)S(1)}, bf16[256,4096]{1,0:T(8,128)(2,1)}, u32[]{:S(2)}) copy-start(bf16[256,4096]{1,0:T(8,128)(2,1)} %param.15) | copy-start | bytes 6291460
  6.5 46.4 %all-gather.2.cloned.1.call-start = ((), (), s32[]{:S(2)}) async-start(), calls=%async_computation.3 | async-start | bytes 2359296 | tf_op jit(solution)/shard_map/all_gather | solution.py:251
  52.9 3.3 %copy-start.1 = (bf16[256,4096]{1,0:T(8,128)(2,1)S(1)}, bf16[256,4096]{1,0:T(8,128)(2,1)}, u32[]{:S(2)}) copy-start(bf16[256,4096]{1,0:T(8,128)(2,1)} %all-gather.2.cloned.1.call-done) | copy-start | bytes 6291460
  52.9 3.5 %copy-start.2 = (bf16[4096,256]{1,0:T(8,128)(2,1)S(1)}, bf16[4096,256]{1,0:T(8,128)(2,1)}, u32[]{:S(2)}) copy-start(bf16[4096,256]{1,0:T(8,128)(2,1)} %param.12) | copy-start | bytes 6291460
  60.2 8.1 %copy-start.5 = (s32[256]{0:T(256)S(1)}, s32[256]{0:T(256)}, u32[]{:S(2)}) copy-start(s32[256]{0:T(256)} %param.20) | copy-start | bytes 3076
  60.2 34.0 %all-to-all-start = ((bf16[32,2,64,256]{3,2,1,0:T(8,128)(2,1)}), bf16[32,2,64,256]{3,2,1,0:T(8,128)(2,1)}, u32[]{:S(2)}, u32[]{:S(2)}) async-start(bf16[32,2,64,256]{3,2,1,0:T(8,128)(2,1)} %bitcast.67), calls=%async_computation | async-start | bytes 4194304 | tf_op jit(solution)/shard_map/all_to_all | solution.py:301
  69.0 25.3 %copy-start.4 = (s32[8]{0:T(128)}, s32[8]{0:T(128)S(1)}, u32[]{:S(2)}) copy-start(s32[8]{0:T(128)S(1)} %reduce_max.58.gnode_ref) | copy-start | bytes 100
  107.3 41.3 %all-to-all-start.1 = ((bf16[32,2,80,256]{3,2,1,0:T(8,128)(2,1)}), bf16[32,2,80,256]{3,2,1,0:T(8,128)(2,1)}, u32[]{:S(2)}, u32[]{:S(2)}) async-start(bf16[32,2,80,256]{3,2,1,0:T(8,128)(2,1)} %bitcast.69), calls=%async_computation.1 | async-start | bytes 5242880 | tf_op jit(solution)/shard_map/all_to_all | solution.py:326
  116.7 83.2 %reduce-scatter.2.cloned.1.call-start = ((), (), s32[]{:S(2)}) async-start(), calls=%async_computation.4 | async-start | bytes 2359296 | tf_op jit(solution)/shard_map/reduce_scatter | solution.py:350
  159.4 51.7 %copy-start.3 = (bf16[256,512]{1,0:T(8,128)(2,1)S(1)}, bf16[256,512]{1,0:T(8,128)(2,1)}, u32[]{:S(2)}) copy-start(bf16[256,512]{1,0:T(8,128)(2,1)} %param.11) | copy-start | bytes 786436
  159.4 51.7 %copy-start.6 = (f32[512]{0:T(512)S(1)}, f32[512]{0:T(512)}, u32[]{:S(2)}) copy-start(f32[512]{0:T(512)} %param.16) | copy-start | bytes 6148
Sparse Core Ops, SparseCore 0:
  9.1 43.7 all-gather.1
  159.6 40.2 reduce-scatter.1

commit v7 on v5

--- a/solution.py
+++ b/solution.py
@@ -57,101 +57,95 @@
     return o / l, m + jnp.log(l)
 
 
+CHUNK = 4
+
+
 def node_kernel(
-    slot_ref, len_ref, mode_ref, gnode_ref, glen_ref, q_ref, k_ref, v_ref, out_ref, lse_ref
+    perm_ref, start_ref, count_ref, nlen_ref, total_ref, q_ref, k_ref, v_ref, out_ref, lse_ref, qbuf
 ):
-    total_rows, width = q_ref.shape
-    cache_rows = k_ref.shape[1]
+    slots, rows, width = q_ref.shape
+    nodes, cache_rows, _ = k_ref.shape
     heads = width // HD
-    groups = mode_ref.shape[0]
-    span = GROUP * REQ_LEN
-
-    def one_slot(i, carry):
-        node = slot_ref[i]
-        length = len_ref[i]
-        rows = pl.ds(pl.multiple_of(i * REQ_LEN, REQ_LEN), REQ_LEN)
-
-        @pl.when(length > 0)
-        def _():
+    span = CHUNK * rows
+
+    def per_node(n, carry):
+        first = start_ref[n]
+        count = count_ref[n]
+        length = nlen_ref[n]
+        last = first + count - 1
+
+        def per_chunk(c, carry2):
+            base = first + c * CHUNK
+            picked = [perm_ref[jnp.minimum(base + j, last)] for j in range(CHUNK)]
+            for j in range(CHUNK):
+                qbuf[pl.ds(j * rows, rows), :] = q_ref[picked[j]]
             for h in range(heads):
                 cols = pl.ds(h * HD, HD)
                 o, lse = attend(
-                    q_ref[rows, cols], k_ref[node, :, cols], v_ref[node, :, cols],
-                    length, REQ_LEN, cache_rows,
+                    qbuf[:, cols], k_ref[n, :, cols], v_ref[n, :, cols], length, span, cache_rows
                 )
-                out_ref[rows, cols] = o.astype(out_ref.dtype)
-                lse_ref[rows, pl.ds(h, 1)] = lse
-
-        @pl.when(length == 0)
-        def _():
-            out_ref[rows, :] = jnp.zeros((REQ_LEN, width), out_ref.dtype)
-            lse_ref[rows, :] = jnp.zeros((REQ_LEN, heads), lse_ref.dtype)
-
+                for j in range(CHUNK):
+
+                    @pl.when(base + j <= last)
+                    def _():
+                        out_ref[picked[j], :, cols] = o[j * rows : (j + 1) * rows].astype(out_ref.dtype)
+                        lse_ref[pl.ds(pl.multiple_of(picked[j] * rows, rows), rows), pl.ds(h, 1)] = (
+                            lse[j * rows : (j + 1) * rows]
+                        )
+
+            return carry2
+
+        lax.fori_loop(0, (count + CHUNK - 1) // CHUNK, per_chunk, 0)
         return carry
 
-    def one_group(g, carry):
-        mode = mode_ref[g]
-        rows = pl.ds(pl.multiple_of(g * span, span), span)
-
-        @pl.when(mode == 0)
-        def _():
-            out_ref[rows, :] = jnp.zeros((span, width), out_ref.dtype)
-            lse_ref[rows, :] = jnp.zeros((span, heads), lse_ref.dtype)
-
-        @pl.when(mode == 1)
-        def _():
-            node = gnode_ref[g]
-            length = glen_ref[g]
-            for h in range(heads):
-                cols = pl.ds(h * HD, HD)
-                o, lse = attend(
-                    q_ref[rows, cols], k_ref[node, :, cols], v_ref[node, :, cols],
-                    length, span, cache_rows,
-                )
-                out_ref[rows, cols] = o.astype(out_ref.dtype)
-                lse_ref[rows, pl.ds(h, 1)] = lse
-
-        @pl.when(mode == 2)
-        def _():
-            lax.fori_loop(g * GROUP, (g + 1) * GROUP, one_slot, 0)
-
+    lax.fori_loop(0, nodes, per_node, 0)
+
+    def clear(p, carry):
+        slot = perm_ref[p]
+        out_ref[slot] = jnp.zeros((rows, width), out_ref.dtype)
+        lse_ref[pl.ds(pl.multiple_of(slot * rows, rows), rows), :] = jnp.zeros(
+            (rows, heads), lse_ref.dtype
+        )
         return carry
 
-    lax.fori_loop(0, groups, one_group, 0)
-
-
-def node_attention(queries, key_cache, value_cache, local_slot, lengths, heads_local):
+    lax.fori_loop(total_ref[0], slots, clear, 0)
+
+
+def node_attention(queries, key_cache, value_cache, local_slot, filled, local_len, heads_local):
     slots, rows, width = queries.shape
     nodes, cache_rows, _ = key_cache.shape
-    groups = slots // GROUP
-    live = (lengths > 0).reshape(groups, GROUP)
-    grouped_node = local_slot.reshape(groups, GROUP)
-    grouped_len = lengths.reshape(groups, GROUP)
-    group_node = jnp.max(jnp.where(live, grouped_node, 0), axis=1)
-    group_len = jnp.max(grouped_len, axis=1)
-    uniform = jnp.all(~live | (grouped_node == group_node[:, None]), axis=1)
-    mode = jnp.where(jnp.any(live, axis=1), jnp.where(uniform, 1, 2), 0).astype(jnp.int32)
+    order_key = jnp.where(filled, local_slot, nodes)
+    index = jnp.arange(slots, dtype=jnp.int32)
+    before = (order_key[None, :] < order_key[:, None]) | (
+        (order_key[None, :] == order_key[:, None]) & (index[None, :] < index[:, None])
+    )
+    rank = jnp.sum(before, axis=1).astype(jnp.int32)
+    perm = jnp.sum(
+        jnp.where(rank[None, :] == index[:, None], index[None, :], 0), axis=1
+    ).astype(jnp.int32)
+    node_ids = jnp.arange(nodes, dtype=jnp.int32)
+    count = jnp.sum(filled[None, :] & (local_slot[None, :] == node_ids[:, None]), axis=1).astype(jnp.int32)
+    first = jnp.sum(filled[None, :] & (local_slot[None, :] < node_ids[:, None]), axis=1).astype(jnp.int32)
+    total = jnp.sum(filled).astype(jnp.int32).reshape(1)
     vmem = pl.BlockSpec(memory_space=pltpu.VMEM)
     smem = pl.BlockSpec(memory_space=pltpu.SMEM)
     flops = 4 * slots * rows * cache_rows * width
     out, lse = pl.pallas_call(
         node_kernel,
         out_shape=(
-            jax.ShapeDtypeStruct((slots * rows, width), jnp.bfloat16),
+            jax.ShapeDtypeStruct((slots, rows, width), jnp.bfloat16),
             jax.ShapeDtypeStruct((slots * rows, heads_local), jnp.float32),
         ),
         in_specs=[smem] * 5 + [vmem] * 3,
         out_specs=(vmem, vmem),
+        scratch_shapes=[pltpu.VMEM((CHUNK * rows, width), queries.dtype)],
         cost_estimate=pl.CostEstimate(
             flops=flops,
             transcendentals=slots * rows * cache_rows * heads_local,
             bytes_accessed=2 * queries.size * 2 + 2 * key_cache.size * 2,
         ),
-    )(
-        local_slot, lengths, mode, group_node, group_len,
-        queries.reshape(slots * rows, width), key_cache, value_cache,
-    )
-    return out.reshape(slots, rows, width), lse.reshape(slots, rows, heads_local)
+    )(perm, first, count, local_len, total, queries, key_cache, value_cache)
+    return out, lse.reshape(slots, rows, heads_local)
 
 
 def sum_kernel(x_ref, out_ref, recv, send_sem, recv_sem):
@@ -303,7 +297,8 @@
         key_cache,
         value_cache,
         local_slot,
-        lengths,
+        filled,
+        lax.dynamic_slice_in_dim(node_len, device * NODE_DEV, NODE_DEV),
         heads_local,
     )
     flat_lse = node_lse.reshape(leaf_count * all_slots, REQ_LEN * heads_local)

time: 224 us -> 222 us (level)
  Pallas kernels: 23.6 us -> 18.7 us
  starting transfers between devices: 19.5 us -> 22.8 us
    pallas_call x1, Pallas kernels: 14.6 us -> 9.72 us  [node_attention(): pl.pallas_call(node_kernel, out_shape=(jax.ShapeDtypeStruct((slots, rows,...]
    all_to_all x1, starting transfers between devices: 5.06 us -> 8.33 us  [on_device(): lax.all_to_all(lse_pair.reshape(leaf_count, all_slots, 2, REQ_LEN * heads...]
where the time goes in v7:
time: 222 us
  waiting for transfers between devices  128 us (58%)
  starting transfers between devices  22.8 us (10%)
  Pallas kernels  18.7 us (8%)
  between operations  13.8 us (6%)
  local copies, waits for them, and re-layouts  13.6 us (6%)
  other arithmetic  13.6 us (6%)
  matrix products  10.7 us (5%)
    reduce_scatter x1, waiting for transfers between devices, on_device(): lax.psum_scatter(partial_value.astype(jnp.bfloat16), 'mp', scatter_dimens...  39.8 us
    all_gather x1, waiting for transfers between devices, on_device(): columns = lax.all_gather(activations, 'mp', axis=1, tiled=True)  39.6 us
    all_to_all x1, waiting for transfers between devices, on_device(): lax.all_to_all(outgoing, 'leaf', split_axis=0, concat_axis=0, tiled=True)  23.7 us
    all_to_all x1, waiting for transfers between devices, on_device(): lax.all_to_all(node_out.reshape(leaf_count, all_slots, REQ_LEN, width_loc...  19.2 us
    pallas_call x1, Pallas kernels, node_attention(): pl.pallas_call(node_kernel, out_shape=(jax.ShapeDtypeStruct((slots, rows,...  9.72 us
    pallas_call x1, Pallas kernels, mp_sum(): pl.pallas_call(sum_kernel, out_shape=jax.ShapeDtypeStruct(x.shape, x.dtyp...  8.94 us
    all_to_all x1, starting transfers between devices, on_device(): lax.all_to_all(lse_pair.reshape(leaf_count, all_slots, 2, REQ_LEN * heads...  8.33 us
    all_to_all x1, starting transfers between devices, on_device(): lax.all_to_all(outgoing, 'leaf', split_axis=0, concat_axis=0, tiled=True)  7.64 us
  transfers between devices with their start and end apart: 5, of which 5 were waited for; matrix products, arithmetic and copies ran while one was open for 7% of the time, Pallas kernels for 0%

profile of v7, /device:TPU:6, one launch (start us, length us, event | category | flops | bytes accessed | tf_op | source)
XLA Modules:
  0.0 221.7 jit_solution(9830454047697921647)
XLA Ops:
  6.5 0.7 all-gather.2.cloned.1.call-update
  7.3 0.8 stack.19
  8.0 0.9 select_reduce_fusion.4
  9.0 0.9 select_reduce_fusion.3
  10.0 0.9 select_reduce_fusion.1
  11.5 0.2 add_reduce_fusion
  13.1 0.3 multiply_cosine_fusion
  13.4 39.6 %all-gather.2.cloned.1.call-done = bf16[256,4096]{1,0:T(8,128)(2,1)} async-done(((bf16[256,512]{1,0:T(8,128)(2,1)}), bf16[256,4096]{1,0:T(8,128)(2,1)}) %all-gather.2.cloned.1.call-update) | async-done | bytes 2097168 | tf_op jit(solution)/shard_map/all_gather | solution.py:239
  52.9 3.3 %fusion.51 = f32[256,256]{0,1:T(8,128)S(1)} fusion(bf16[256,4096]{1,0:T(8,128)(2,1)} %all-gather.2.cloned.1.call-done, bf16[4096,256]{1,0:T(8,128)(2,1)} %param.13), kind=kOutput, calls=%fused_computation.126 | convolution fusion | flops 536870912 | bytes 4456448 | tf_op jit(solution)/shard_map/dot_general | solution.py:242
  56.3 0.2 copy-done.2
  56.4 1.0 fusion.50
  57.7 0.7 convolution_convert_fusion
  58.4 1.8 copy.144
  60.2 7.6 %all-to-all-start = ((bf16[32,2,64,256]{3,2,1,0:T(8,128)(2,1)}), bf16[32,2,64,256]{3,2,1,0:T(8,128)(2,1)}, u32[]{:S(2)}, u32[]{:S(2)}) async-start(bf16[32,2,64,256]{3,2,1,0:T(8,128)(2,1)} %bitcast.78), calls=%async_computation | async-start | bytes 4194304 | tf_op jit(solution)/shard_map/all_to_all | solution.py:289
  67.9 0.6 dynamic_slice.15.nlen_ref
  68.5 0.6 convert_reduce_fusion.4
  69.1 0.7 convert_reduce_fusion.2
  69.8 0.2 convert_reduce_fusion.1
  70.0 0.6 select_reduce_fusion.5.perm_ref
  70.6 23.7 %all-to-all-done = bf16[32,2,64,256]{3,2,1,0:T(8,128)(2,1)} async-done(((bf16[32,2,64,256]{3,2,1,0:T(8,128)(2,1)}), bf16[32,2,64,256]{3,2,1,0:T(8,128)(2,1)}, u32[]{:S(2)}, u32[]{:S(2)}) %all-to-all-start) | async-done | bytes 2097184 | tf_op jit(solution)/shard_map/all_to_all | solution.py:289
  94.3 9.7 %shard_map.109 = (bf16[64,64,256]{2,1,0:T(8,128)(2,1)}, f32[4096,2]{1,0:T(8,128)}) custom-call(s32[64]{0:T(128)} %select_reduce_fusion.5.perm_ref, s32[8]{0:T(128)} %get-tuple-element.13.start_ref, s32[8]{0:T(128)} %get-tuple-element.12.count_ref, s32[8]{0:T(128)} %dynamic_slice.15.nlen_ref, s32[1]{0:T(128)} %bitcast.2.total_ref, ...), custom_call_target="tpu_custom_call" | custom-call | flops 1073741824 | bytes 6291456 | tf_op jit(solution)/shard_map/pallas_call | solution.py:133
  104.0 2.8 %reshape_reshape.3 = f32[32,2,1,128]{3,1,0,2:T(2,128)S(1)} reshape(f32[4096,2]{1,0:T(8,128)} %get-tuple-element.7) | data formatting | bytes 65536 | tf_op jit(solution)/shard_map/reshape;reshape | solution.py:304
  106.9 0.6 copy.120
  107.6 8.3 %all-to-all-start.1 = ((bf16[32,2,2,128]{3,1,2,0:T(2,128)(2,1)}), bf16[32,2,2,128]{3,1,2,0:T(2,128)(2,1)S(1)}, u32[]{:S(2)}, u32[]{:S(2)}) async-start(bf16[32,2,2,128]{3,1,2,0:T(2,128)(2,1)} %copy.120), calls=%async_computation.1 | async-start | bytes 65536 | tf_op jit(solution)/shard_map/all_to_all | solution.py:315
  116.0 5.4 %all-to-all-done.1 = bf16[32,2,2,128]{3,1,2,0:T(2,128)(2,1)S(1)} async-done(((bf16[32,2,2,128]{3,1,2,0:T(2,128)(2,1)}), bf16[32,2,2,128]{3,1,2,0:T(2,128)(2,1)S(1)}, u32[]{:S(2)}, u32[]{:S(2)}) %all-to-all-start.1) | async-done | bytes 32800 | tf_op jit(solution)/shard_map/all_to_all | solution.py:315
  121.5 6.6 %all-to-all-start.2 = ((bf16[32,2,64,256]{3,2,1,0:T(8,128)(2,1)}), bf16[32,2,64,256]{3,2,1,0:T(8,128)(2,1)}, u32[]{:S(2)}, u32[]{:S(2)}) async-start(bf16[32,2,64,256]{3,2,1,0:T(8,128)(2,1)} %bitcast.80), calls=%async_computation.2 | async-start | bytes 4194304 | tf_op jit(solution)/shard_map/all_to_all | solution.py:308
  128.1 0.2 reduce-scatter.2.cloned.1.call-start
  128.6 2.9 %convolution_convert_fusion.2 = bf16[256,256]{1,0:T(8,128)(2,1)S(1)} fusion(bf16[256,4096]{1,0:T(8,128)(2,1)} %all-gather.2.cloned.1.call-done, bf16[4096,256]{1,0:T(8,128)(2,1)} %param.14), kind=kOutput, calls=%fused_computation.8 | convolution fusion | flops 536936448 | bytes 4325376 | tf_op jit(solution)/shard_map/dot_general | solution.py:242
  132.1 0.1 copy.125
  132.3 0.1 copy.124
  132.4 0.3 fusion.49
  132.8 0.2 fusion.2
  133.0 0.9 copy.135
  134.0 0.2 fusion.23
  134.3 0.1 add.151
  134.6 0.2 reduce_max.26
  135.0 0.2 copy.132
  135.3 19.2 %all-to-all-done.2 = bf16[32,2,64,256]{3,2,1,0:T(8,128)(2,1)} async-done(((bf16[32,2,64,256]{3,2,1,0:T(8,128)(2,1)}), bf16[32,2,64,256]{3,2,1,0:T(8,128)(2,1)}, u32[]{:S(2)}, u32[]{:S(2)}) %all-to-all-start.2) | async-done | bytes 2097184 | tf_op jit(solution)/shard_map/all_to_all | solution.py:308
  154.5 2.2 gather_fusion
  156.7 0.4 fusion.8
  157.2 2.3 %fusion.3 = f32[4,64,2,128]{3,2,1,0:T(2,128)S(1)} fusion(f32[1,4,64,2,128]{4,3,2,1,0:T(2,128)} %copy.135, f32[3,4,64,2,128]{4,3,2,1,0:T(2,128)S(1)} %fusion.8, f32[4,4,64,2]{3,2,1,0:T(8,128)S(1)} %copy.132), kind=kLoop, calls=%fused_computation.10 | loop fusion | flops 720896 | bytes 1318912 | tf_op jit(solution)/shard_map/reduce_sum | solution.py:340
  159.5 0.3 divide_convert_fusion
  159.9 2.1 convolution_convert_fusion.1
  162.0 39.8 %reduce-scatter.2.cloned.1.call-done = bf16[256,512]{1,0:T(8,128)(2,1)} async-done(((bf16[256,4096]{1,0:T(8,128)(2,1)}), bf16[256,512]{1,0:T(8,128)(2,1)}) %reduce-scatter.2.cloned.1.call-update) | async-done | bytes 262160 | tf_op jit(solution)/shard_map/reduce_scatter | solution.py:343
  201.8 1.6 fusion.7
  203.4 8.9 %shard_map.110 = f32[1,256]{1,0:T(1,128)} custom-call(f32[1,256]{1,0:T(1,128)} %bitcast.87), custom_call_target="tpu_custom_call" | custom-call | tf_op jit(solution)/shard_map/pallas_call | solution.py:183
  212.4 0.7 add_rsqrt_fusion
  213.1 1.8 fusion.6
  (75 shorter events, 4.0 us)
Async XLA Ops:
  6.5 153.3 %copy-start = (bf16[256,4096]{1,0:T(8,128)(2,1)S(1)}, bf16[256,4096]{1,0:T(8,128)(2,1)}, u32[]{:S(2)}) copy-start(bf16[256,4096]{1,0:T(8,128)(2,1)} %param.15) | copy-start | bytes 6291460
  6.5 46.4 %all-gather.2.cloned.1.call-start = ((), (), s32[]{:S(2)}) async-start(), calls=%async_computation.4 | async-start | bytes 2359296 | tf_op jit(solution)/shard_map/all_gather | solution.py:239
  52.9 3.3 %copy-start.1 = (bf16[256,4096]{1,0:T(8,128)(2,1)S(1)}, bf16[256,4096]{1,0:T(8,128)(2,1)}, u32[]{:S(2)}) copy-start(bf16[256,4096]{1,0:T(8,128)(2,1)} %all-gather.2.cloned.1.call-done) | copy-start | bytes 6291460
  52.9 3.5 %copy-start.2 = (bf16[4096,256]{1,0:T(8,128)(2,1)S(1)}, bf16[4096,256]{1,0:T(8,128)(2,1)}, u32[]{:S(2)}) copy-start(bf16[4096,256]{1,0:T(8,128)(2,1)} %param.12) | copy-start | bytes 6291460
  60.2 7.6 %copy-start.5 = (s32[256]{0:T(256)S(1)}, s32[256]{0:T(256)}, u32[]{:S(2)}) copy-start(s32[256]{0:T(256)} %param.20) | copy-start | bytes 3076
  60.2 34.0 %all-to-all-start = ((bf16[32,2,64,256]{3,2,1,0:T(8,128)(2,1)}), bf16[32,2,64,256]{3,2,1,0:T(8,128)(2,1)}, u32[]{:S(2)}, u32[]{:S(2)}) async-start(bf16[32,2,64,256]{3,2,1,0:T(8,128)(2,1)} %bitcast.78), calls=%async_computation | async-start | bytes 4194304 | tf_op jit(solution)/shard_map/all_to_all | solution.py:289
  107.6 13.9 %all-to-all-start.1 = ((bf16[32,2,2,128]{3,1,2,0:T(2,128)(2,1)}), bf16[32,2,2,128]{3,1,2,0:T(2,128)(2,1)S(1)}, u32[]{:S(2)}, u32[]{:S(2)}) async-start(bf16[32,2,2,128]{3,1,2,0:T(2,128)(2,1)} %copy.120), calls=%async_computation.1 | async-start | bytes 65536 | tf_op jit(solution)/shard_map/all_to_all | solution.py:315
  121.5 33.0 %all-to-all-start.2 = ((bf16[32,2,64,256]{3,2,1,0:T(8,128)(2,1)}), bf16[32,2,64,256]{3,2,1,0:T(8,128)(2,1)}, u32[]{:S(2)}, u32[]{:S(2)}) async-start(bf16[32,2,64,256]{3,2,1,0:T(8,128)(2,1)} %bitcast.80), calls=%async_computation.2 | async-start | bytes 4194304 | tf_op jit(solution)/shard_map/all_to_all | solution.py:308
  128.1 73.7 %reduce-scatter.2.cloned.1.call-start = ((), (), s32[]{:S(2)}) async-start(), calls=%async_computation.5 | async-start | bytes 2359296 | tf_op jit(solution)/shard_map/reduce_scatter | solution.py:343
  161.9 51.1 %copy-start.3 = (bf16[256,512]{1,0:T(8,128)(2,1)S(1)}, bf16[256,512]{1,0:T(8,128)(2,1)}, u32[]{:S(2)}) copy-start(bf16[256,512]{1,0:T(8,128)(2,1)} %param.11) | copy-start | bytes 786436
  161.9 51.1 %copy-start.4 = (f32[512]{0:T(512)S(1)}, f32[512]{0:T(512)}, u32[]{:S(2)}) copy-start(f32[512]{0:T(512)} %param.16) | copy-start | bytes 6148
Sparse Core Ops, SparseCore 0:
  9.1 43.7 all-gather.1
  162.1 39.6 reduce-scatter.1

commit v8 on v7

--- a/solution.py
+++ b/solution.py
@@ -88,7 +88,9 @@
 
                     @pl.when(base + j <= last)
                     def _():
-                        out_ref[picked[j], :, cols] = o[j * rows : (j + 1) * rows].astype(out_ref.dtype)
+                        out_ref[picked[j] // 2, pl.ds(pl.multiple_of(picked[j] % 2 * rows, rows), rows), cols] = (
+                            o[j * rows : (j + 1) * rows].astype(out_ref.dtype)
+                        )
                         lse_ref[pl.ds(pl.multiple_of(picked[j] * rows, rows), rows), pl.ds(h, 1)] = (
                             lse[j * rows : (j + 1) * rows]
                         )
@@ -102,7 +104,9 @@
 
     def clear(p, carry):
         slot = perm_ref[p]
-        out_ref[slot] = jnp.zeros((rows, width), out_ref.dtype)
+        out_ref[slot // 2, pl.ds(pl.multiple_of(slot % 2 * rows, rows), rows), :] = jnp.zeros(
+            (rows, width), out_ref.dtype
+        )
         lse_ref[pl.ds(pl.multiple_of(slot * rows, rows), rows), :] = jnp.zeros(
             (rows, heads), lse_ref.dtype
         )
@@ -133,7 +137,7 @@
     out, lse = pl.pallas_call(
         node_kernel,
         out_shape=(
-            jax.ShapeDtypeStruct((slots, rows, width), jnp.bfloat16),
+            jax.ShapeDtypeStruct((slots // 2, 2 * rows + 16, width), jnp.bfloat16),
             jax.ShapeDtypeStruct((slots * rows, heads_local), jnp.float32),
         ),
         in_specs=[smem] * 5 + [vmem] * 3,
@@ -301,38 +305,34 @@
         lax.dynamic_slice_in_dim(node_len, device * NODE_DEV, NODE_DEV),
         heads_local,
     )
-    flat_lse = node_lse.reshape(leaf_count * all_slots, REQ_LEN * heads_local)
+    slot_count = leaf_count * all_slots
+    flat_lse = node_lse.reshape(slot_count, REQ_LEN * heads_local)
     lse_high = lax.reduce_precision(flat_lse, exponent_bits=8, mantissa_bits=7)
     lse_low = flat_lse - lse_high
-    lse_pair = jnp.stack([lse_high, lse_low], axis=1).astype(jnp.bfloat16)
-    back_out = lax.all_to_all(
-        node_out.reshape(leaf_count, all_slots, REQ_LEN, width_local),
-        "leaf",
-        split_axis=0,
-        concat_axis=0,
-        tiled=True,
-    )
-    back_lse = lax.all_to_all(
-        lse_pair.reshape(leaf_count, all_slots, 2, REQ_LEN * heads_local),
-        "leaf",
-        split_axis=0,
-        concat_axis=0,
-        tiled=True,
-    )
-    take = (
-        (my_holders * all_slots + my_ranks)[:, None]
-        == jnp.arange(leaf_count * all_slots, dtype=jnp.int32)[None, :]
-    ).astype(jnp.bfloat16)
-    chosen = my_holders * all_slots + my_ranks
-    got_out = jnp.take(
-        back_out.reshape(leaf_count * all_slots, REQ_LEN, width_local), chosen, axis=0
-    ).astype(jnp.float32).reshape(level_count, REQ_DEV, REQ_LEN, heads_local, HD)
-    got_pair = jnp.dot(
-        take,
-        back_lse.reshape(leaf_count * all_slots, 2 * REQ_LEN * heads_local),
-        preferred_element_type=jnp.float32,
-    ).reshape(items, 2, REQ_LEN * heads_local)
-    got_lse = (got_pair[:, 0] + got_pair[:, 1]).reshape(level_count, REQ_DEV, REQ_LEN, heads_local)
+    pair_width = 2 * REQ_LEN * heads_local
+    lse_rows = jnp.pad(
+        jnp.concatenate([lse_high, lse_low], axis=1).astype(jnp.bfloat16).reshape(
+            leaf_count, all_slots, pair_width
+        ),
+        ((0, 0), (0, 16 - all_slots), (0, width_local - pair_width)),
+    )
+    payload = lax.dynamic_update_slice(node_out, lse_rows, (0, all_slots * REQ_LEN, 0))
+    back = lax.all_to_all(payload, "leaf", split_axis=0, concat_axis=0, tiled=True)
+    got = jnp.take(back, my_holders, axis=0)
+    second = (my_ranks == 1)[:, None, None]
+    got_out = (
+        jnp.where(second, got[:, REQ_LEN : 2 * REQ_LEN], got[:, :REQ_LEN])
+        .astype(jnp.float32)
+        .reshape(level_count, REQ_DEV, REQ_LEN, heads_local, HD)
+    )
+    lse_at = all_slots * REQ_LEN
+    got_pair = jnp.where(
+        second[:, 0], got[:, lse_at + 1, :pair_width], got[:, lse_at, :pair_width]
+    ).astype(jnp.float32)
+    lse_width = REQ_LEN * heads_local
+    got_lse = (got_pair[:, :lse_width] + got_pair[:, lse_width:]).reshape(
+        level_count, REQ_DEV, REQ_LEN, heads_local
+    )
     partial_out = jnp.concatenate([got_out, self_out[None]], axis=0)
     partial_lse = jnp.concatenate([got_lse, self_lse[None]], axis=0)
     highest = jnp.max(partial_lse, axis=0)

time: 222 us -> 219 us (0.986)
  starting transfers between devices: 22.8 us -> 17.8 us
    all_to_all x2 -> x1, starting transfers between devices: 14.9 us -> 9.95 us  [on_device(): lax.all_to_all(payload, 'leaf', split_axis=0, concat_axis=0, tiled=True)]
    all_to_all x2 -> x1, waiting for transfers between devices: 24.6 us -> 23.2 us  [on_device(): lax.all_to_all(payload, 'leaf', split_axis=0, concat_axis=0, tiled=True)]
  transfers between devices with their start and end apart: 5 -> 4, of which waited for: 5 -> 4; matrix products, arithmetic and copies ran while one was open for 7% -> 7% of each run, Pallas kernels for 0% -> 0%
where the time goes in v8:
time: 219 us; the launch traced here: 218 us
  waiting for transfers between devices  127 us (58%)
  Pallas kernels  19.2 us (9%)
  starting transfers between devices  17.8 us (8%)
  other arithmetic  15 us (7%)
  local copies, waits for them, and re-layouts  14.8 us (7%)
  between operations  13.9 us (6%)
  matrix products  10.5 us (5%)
    reduce_scatter x1, waiting for transfers between devices, on_device(): lax.psum_scatter(partial_value.astype(jnp.bfloat16), 'mp', scatter_dimens...  39.9 us
    all_gather x1, waiting for transfers between devices, on_device(): columns = lax.all_gather(activations, 'mp', axis=1, tiled=True)  39.4 us
    all_to_all x1, waiting for transfers between devices, on_device(): lax.all_to_all(outgoing, 'leaf', split_axis=0, concat_axis=0, tiled=True)  23.6 us
    all_to_all x1, waiting for transfers between devices, on_device(): lax.all_to_all(payload, 'leaf', split_axis=0, concat_axis=0, tiled=True)  23.2 us
    pallas_call x1, Pallas kernels, node_attention(): pl.pallas_call(node_kernel, out_shape=(jax.ShapeDtypeStruct((slots // 2,...  10.3 us
    all_to_all x1, starting transfers between devices, on_device(): lax.all_to_all(payload, 'leaf', split_axis=0, concat_axis=0, tiled=True)  9.95 us
    pallas_call x1, Pallas kernels, mp_sum(): pl.pallas_call(sum_kernel, out_shape=jax.ShapeDtypeStruct(x.shape, x.dtyp...  8.92 us
    all_to_all x1, starting transfers between devices, on_device(): lax.all_to_all(outgoing, 'leaf', split_axis=0, concat_axis=0, tiled=True)  7.64 us
  transfers between devices with their start and end apart: 4, of which 4 were waited for; matrix products, arithmetic and copies ran while one was open for 7% of the time, Pallas kernels for 0%

profile of v8, /device:TPU:6, one launch (start us, length us, event | category | flops | bytes accessed | tf_op | source)
XLA Modules:
  0.0 218.1 jit_solution(10584508125848978800)
XLA Ops:
  6.5 0.7 all-gather.2.cloned.1.call-update
  7.3 0.8 stack.14
  8.0 0.9 select_reduce_fusion.4
  9.0 0.9 select_reduce_fusion.3
  10.0 0.9 select_reduce_fusion.1
  12.0 0.2 dynamic-slice_reduce_fusion.1
  12.2 0.2 dynamic-slice_reduce_fusion
  13.2 0.3 multiply_cosine_fusion
  13.5 39.4 %all-gather.2.cloned.1.call-done = bf16[256,4096]{1,0:T(8,128)(2,1)} async-done(((bf16[256,512]{1,0:T(8,128)(2,1)}), bf16[256,4096]{1,0:T(8,128)(2,1)}) %all-gather.2.cloned.1.call-update) | async-done | bytes 2097168 | tf_op jit(solution)/shard_map/all_gather | solution.py:243
  52.9 3.3 %fusion.51 = f32[256,256]{0,1:T(8,128)S(1)} fusion(bf16[256,4096]{1,0:T(8,128)(2,1)} %all-gather.2.cloned.1.call-done, bf16[4096,256]{1,0:T(8,128)(2,1)} %param.13), kind=kOutput, calls=%fused_computation.126 | convolution fusion | flops 536870912 | bytes 4456448 | tf_op jit(solution)/shard_map/dot_general | solution.py:246
  56.3 0.2 copy-done.2
  56.4 1.0 fusion.50
  57.7 0.7 convolution_convert_fusion
  58.4 1.8 copy.154
  60.2 7.6 %all-to-all-start = ((bf16[32,2,64,256]{3,2,1,0:T(8,128)(2,1)}), bf16[32,2,64,256]{3,2,1,0:T(8,128)(2,1)}, u32[]{:S(2)}, u32[]{:S(2)}) async-start(bf16[32,2,64,256]{3,2,1,0:T(8,128)(2,1)} %bitcast.65), calls=%async_computation | async-start | bytes 4194304 | tf_op jit(solution)/shard_map/all_to_all | solution.py:293
  67.9 0.6 dynamic_slice.15.nlen_ref
  68.5 0.7 convert_reduce_fusion.4
  69.2 0.7 convert_reduce_fusion.2
  69.9 0.2 convert_reduce_fusion.1
  70.1 0.6 select_reduce_fusion.5.perm_ref
  70.7 23.6 %all-to-all-done = bf16[32,2,64,256]{3,2,1,0:T(8,128)(2,1)} async-done(((bf16[32,2,64,256]{3,2,1,0:T(8,128)(2,1)}), bf16[32,2,64,256]{3,2,1,0:T(8,128)(2,1)}, u32[]{:S(2)}, u32[]{:S(2)}) %all-to-all-start) | async-done | bytes 2097184 | tf_op jit(solution)/shard_map/all_to_all | solution.py:293
  94.3 10.3 %shard_map.109 = (bf16[32,144,256]{2,1,0:T(8,128)(2,1)}, f32[4096,2]{1,0:T(8,128)}) custom-call(s32[64]{0:T(128)} %select_reduce_fusion.5.perm_ref, s32[8]{0:T(128)} %get-tuple-element.10.start_ref, s32[8]{0:T(128)} %get-tuple-element.9.count_ref, s32[8]{0:T(128)} %dynamic_slice.15.nlen_ref, s32[1]{0:T(128)} %bitcast.1.total_ref, ...), custom_call_target="tpu_custom_call" | custom-call | flops 1073741824 | bytes 6291456 | tf_op jit(solution)/shard_map/pallas_call | solution.py:137
  104.5 2.8 %reshape_reshape.3 = f32[32,2,128]{2,1,0:T(2,128)S(1)} reshape(f32[4096,2]{1,0:T(8,128)} %get-tuple-element.8) | data formatting | bytes 65536 | tf_op jit(solution)/shard_map/reshape;reshape | solution.py:309
  107.4 0.8 fusion.12
  108.2 9.9 %all-to-all-start.1 = ((bf16[32,144,256]{2,1,0:T(8,128)(2,1)}), bf16[32,144,256]{2,1,0:T(8,128)(2,1)}, u32[]{:S(2)}, u32[]{:S(2)}) async-start(bf16[32,144,256]{2,1,0:T(8,128)(2,1)} %fusion.12), calls=%async_computation.1 | async-start | bytes 4718592 | tf_op jit(solution)/shard_map/all_to_all | solution.py:320
  118.2 0.2 reduce-scatter.2.cloned.1.call-start
  119.3 0.1 copy.134
  119.5 0.1 copy.133
  119.6 2.9 %convolution_convert_fusion.2 = bf16[256,256]{1,0:T(8,128)(2,1)S(1)} fusion(bf16[256,4096]{1,0:T(8,128)(2,1)} %all-gather.2.cloned.1.call-done, bf16[4096,256]{1,0:T(8,128)(2,1)} %param.14), kind=kOutput, calls=%fused_computation.8 | convolution fusion | flops 536936448 | bytes 4325376 | tf_op jit(solution)/shard_map/dot_general | solution.py:246
  122.6 0.3 fusion.49
  123.0 0.2 fusion.2
  123.2 0.9 copy.144
  124.1 23.2 %all-to-all-done.1 = bf16[32,144,256]{2,1,0:T(8,128)(2,1)} async-done(((bf16[32,144,256]{2,1,0:T(8,128)(2,1)}), bf16[32,144,256]{2,1,0:T(8,128)(2,1)}, u32[]{:S(2)}, u32[]{:S(2)}) %all-to-all-start.1) | async-done | bytes 2359328 | tf_op jit(solution)/shard_map/all_to_all | solution.py:320
  147.4 2.3 %gather_fusion = bf16[12,144,256]{2,1,0:T(8,128)(2,1)S(1)} fusion(bf16[32,144,256]{2,1,0:T(8,128)(2,1)} %all-to-all-done.1, s32[1024]{0:T(1024)S(1)} %pad_clamp_fusion), kind=kCustom, calls=%fused_computation | custom fusion | bytes 1769520 | tf_op jit(solution)/shard_map/jit(_take)/gather | solution.py:321
  149.6 0.1 broadcast_select_fusion
  149.8 1.0 fusion.10
  150.8 1.5 reshape.439
  152.5 0.1 concatenate.43
  152.8 0.2 reduce_max.26
  153.2 0.2 copy.141
  153.6 2.3 %fusion.3 = f32[4,64,2,128]{3,2,1,0:T(2,128)S(1)} fusion(f32[1,4,64,2,128]{4,3,2,1,0:T(2,128)} %copy.144, f32[3,4,64,2,128]{4,3,2,1,0:T(2,128)S(1)} %reshape.439, f32[4,4,64,2]{3,2,1,0:T(8,128)S(1)} %copy.141), kind=kLoop, calls=%fused_computation.10 | loop fusion | flops 720896 | bytes 1318912 | tf_op jit(solution)/shard_map/reduce_sum | solution.py:340
  155.9 0.3 divide_convert_fusion
  156.2 2.1 convolution_convert_fusion.1
  158.3 39.9 %reduce-scatter.2.cloned.1.call-done = bf16[256,512]{1,0:T(8,128)(2,1)} async-done(((bf16[256,4096]{1,0:T(8,128)(2,1)}), bf16[256,512]{1,0:T(8,128)(2,1)}) %reduce-scatter.2.cloned.1.call-update) | async-done | bytes 262160 | tf_op jit(solution)/shard_map/reduce_scatter | solution.py:343
  198.2 1.6 fusion.7
  199.9 8.9 %shard_map.110 = f32[1,256]{1,0:T(1,128)} custom-call(f32[1,256]{1,0:T(1,128)} %bitcast.72), custom_call_target="tpu_custom_call" | custom-call | tf_op jit(solution)/shard_map/pallas_call | solution.py:187
  208.8 0.7 add_rsqrt_fusion
  209.5 1.8 fusion.6
  (73 shorter events, 3.9 us)
Async XLA Ops:
  6.5 149.7 %copy-start = (bf16[256,4096]{1,0:T(8,128)(2,1)S(1)}, bf16[256,4096]{1,0:T(8,128)(2,1)}, u32[]{:S(2)}) copy-start(bf16[256,4096]{1,0:T(8,128)(2,1)} %param.15) | copy-start | bytes 6291460
  6.5 46.4 %all-gather.2.cloned.1.call-start = ((), (), s32[]{:S(2)}) async-start(), calls=%async_computation.3 | async-start | bytes 2359296 | tf_op jit(solution)/shard_map/all_gather | solution.py:243
  52.9 3.3 %copy-start.1 = (bf16[256,4096]{1,0:T(8,128)(2,1)S(1)}, bf16[256,4096]{1,0:T(8,128)(2,1)}, u32[]{:S(2)}) copy-start(bf16[256,4096]{1,0:T(8,128)(2,1)} %all-gather.2.cloned.1.call-done) | copy-start | bytes 6291460
  52.9 3.5 %copy-start.2 = (bf16[4096,256]{1,0:T(8,128)(2,1)S(1)}, bf16[4096,256]{1,0:T(8,128)(2,1)}, u32[]{:S(2)}) copy-start(bf16[4096,256]{1,0:T(8,128)(2,1)} %param.12) | copy-start | bytes 6291460
  60.2 7.7 %copy-start.5 = (s32[256]{0:T(256)S(1)}, s32[256]{0:T(256)}, u32[]{:S(2)}) copy-start(s32[256]{0:T(256)} %param.20) | copy-start | bytes 3076
  60.2 34.0 %all-to-all-start = ((bf16[32,2,64,256]{3,2,1,0:T(8,128)(2,1)}), bf16[32,2,64,256]{3,2,1,0:T(8,128)(2,1)}, u32[]{:S(2)}, u32[]{:S(2)}) async-start(bf16[32,2,64,256]{3,2,1,0:T(8,128)(2,1)} %bitcast.65), calls=%async_computation | async-start | bytes 4194304 | tf_op jit(solution)/shard_map/all_to_all | solution.py:293
  108.2 39.1 %all-to-all-start.1 = ((bf16[32,144,256]{2,1,0:T(8,128)(2,1)}), bf16[32,144,256]{2,1,0:T(8,128)(2,1)}, u32[]{:S(2)}, u32[]{:S(2)}) async-start(bf16[32,144,256]{2,1,0:T(8,128)(2,1)} %fusion.12), calls=%async_computation.1 | async-start | bytes 4718592 | tf_op jit(solution)/shard_map/all_to_all | solution.py:320
  118.2 80.0 %reduce-scatter.2.cloned.1.call-start = ((), (), s32[]{:S(2)}) async-start(), calls=%async_computation.4 | async-start | bytes 2359296 | tf_op jit(solution)/shard_map/reduce_scatter | solution.py:343
  158.3 51.2 %copy-start.3 = (bf16[256,512]{1,0:T(8,128)(2,1)S(1)}, bf16[256,512]{1,0:T(8,128)(2,1)}, u32[]{:S(2)}) copy-start(bf16[256,512]{1,0:T(8,128)(2,1)} %param.11) | copy-start | bytes 786436
  158.3 51.2 %copy-start.4 = (f32[512]{0:T(512)S(1)}, f32[512]{0:T(512)}, u32[]{:S(2)}) copy-start(f32[512]{0:T(512)} %param.16) | copy-start | bytes 6148
Sparse Core Ops, SparseCore 0:
  9.1 43.7 all-gather.1
  158.4 39.7 reduce-scatter.1

commit v9 on v8

--- a/solution.py
+++ b/solution.py
@@ -79,11 +79,13 @@
             picked = [perm_ref[jnp.minimum(base + j, last)] for j in range(CHUNK)]
             for j in range(CHUNK):
                 qbuf[pl.ds(j * rows, rows), :] = q_ref[picked[j]]
+            lse_cols = []
             for h in range(heads):
                 cols = pl.ds(h * HD, HD)
                 o, lse = attend(
                     qbuf[:, cols], k_ref[n, :, cols], v_ref[n, :, cols], length, span, cache_rows
                 )
+                lse_cols.append(lse)
                 for j in range(CHUNK):
 
                     @pl.when(base + j <= last)
@@ -91,8 +93,19 @@
                         out_ref[picked[j] // 2, pl.ds(pl.multiple_of(picked[j] % 2 * rows, rows), rows), cols] = (
                             o[j * rows : (j + 1) * rows].astype(out_ref.dtype)
                         )
-                        lse_ref[pl.ds(pl.multiple_of(picked[j] * rows, rows), rows), pl.ds(h, 1)] = (
-                            lse[j * rows : (j + 1) * rows]
+
+            lane = lax.broadcasted_iota(jnp.int32, (span, 128), 1)
+            lse_tile = jnp.zeros((span, 128), jnp.float32)
+            for h in range(heads):
+                lse_tile = jnp.where(lane == h, lse_cols[h], lse_tile)
+            lse_t = jnp.transpose(lse_tile)
+            for j in range(CHUNK):
+
+                @pl.when(base + j <= last)
+                def _():
+                    for h in range(heads):
+                        lse_ref[pl.ds(picked[j], 1), pl.ds(h * rows, rows)] = (
+                            lse_t[h : h + 1, j * rows : (j + 1) * rows]
                         )
 
             return carry2
@@ -107,9 +120,7 @@
         out_ref[slot // 2, pl.ds(pl.multiple_of(slot % 2 * rows, rows), rows), :] = jnp.zeros(
             (rows, width), out_ref.dtype
         )
-        lse_ref[pl.ds(pl.multiple_of(slot * rows, rows), rows), :] = jnp.zeros(
-            (rows, heads), lse_ref.dtype
-        )
+        lse_ref[pl.ds(slot, 1), :] = jnp.zeros((1, rows * heads), lse_ref.dtype)
         return carry
 
     lax.fori_loop(total_ref[0], slots, clear, 0)
@@ -138,7 +149,7 @@
         node_kernel,
         out_shape=(
             jax.ShapeDtypeStruct((slots // 2, 2 * rows + 16, width), jnp.bfloat16),
-            jax.ShapeDtypeStruct((slots * rows, heads_local), jnp.float32),
+            jax.ShapeDtypeStruct((slots, rows * heads_local), jnp.float32),
         ),
         in_specs=[smem] * 5 + [vmem] * 3,
         out_specs=(vmem, vmem),
@@ -149,7 +160,7 @@
             bytes_accessed=2 * queries.size * 2 + 2 * key_cache.size * 2,
         ),
     )(perm, first, count, local_len, total, queries, key_cache, value_cache)
-    return out, lse.reshape(slots, rows, heads_local)
+    return out, lse
 
 
 def sum_kernel(x_ref, out_ref, recv, send_sem, recv_sem):
@@ -330,9 +341,11 @@
         second[:, 0], got[:, lse_at + 1, :pair_width], got[:, lse_at, :pair_width]
     ).astype(jnp.float32)
     lse_width = REQ_LEN * heads_local
-    got_lse = (got_pair[:, :lse_width] + got_pair[:, lse_width:]).reshape(
-        level_count, REQ_DEV, REQ_LEN, heads_local
-    )
+    got_lse = jnp.swapaxes(
+        (got_pair[:, :lse_width] + got_pair[:, lse_width:]).reshape(items, heads_local, REQ_LEN),
+        1,
+        2,
+    ).reshape(level_count, REQ_DEV, REQ_LEN, heads_local)
     partial_out = jnp.concatenate([got_out, self_out[None]], axis=0)
     partial_lse = jnp.concatenate([got_lse, self_lse[None]], axis=0)
     highest = jnp.max(partial_lse, axis=0)

time: 219 us -> 216 us (0.986)
  local copies, waits for them, and re-layouts: 14.8 us -> 11.6 us
    another operation x1 -> x0, local copies, waits for them, and re-layouts: 2.84 us -> none  [on_device(): flat_lse = node_lse.reshape(slot_count, REQ_LEN * heads_local)]
where the time goes in v9:
time: 216 us; the launch traced here: 215 us
  waiting for transfers between devices  127 us (59%)
  Pallas kernels  20.8 us (10%)
  starting transfers between devices  15.9 us (7%)
  other arithmetic  15.5 us (7%)
  between operations  13.8 us (6%)
  local copies, waits for them, and re-layouts  11.6 us (5%)
  matrix products  10.5 us (5%)
    reduce_scatter x1, waiting for transfers between devices, on_device(): lax.psum_scatter(partial_value.astype(jnp.bfloat16), 'mp', scatter_dimens...  39.9 us
    all_gather x1, waiting for transfers between devices, on_device(): columns = lax.all_gather(activations, 'mp', axis=1, tiled=True)  39.4 us
    all_to_all x1, waiting for transfers between devices, on_device(): lax.all_to_all(outgoing, 'leaf', split_axis=0, concat_axis=0, tiled=True)  23.6 us
    all_to_all x1, waiting for transfers between devices, on_device(): lax.all_to_all(payload, 'leaf', split_axis=0, concat_axis=0, tiled=True)  23.4 us
    pallas_call x1, Pallas kernels, node_attention(): pl.pallas_call(node_kernel, out_shape=(jax.ShapeDtypeStruct((slots // 2,...  11.8 us
    pallas_call x1, Pallas kernels, mp_sum(): pl.pallas_call(sum_kernel, out_shape=jax.ShapeDtypeStruct(x.shape, x.dtyp...  8.94 us
    all_to_all x1, starting transfers between devices, on_device(): lax.all_to_all(payload, 'leaf', split_axis=0, concat_axis=0, tiled=True)  8.22 us
    all_to_all x1, starting transfers between devices, on_device(): lax.all_to_all(outgoing, 'leaf', split_axis=0, concat_axis=0, tiled=True)  7.64 us
  transfers between devices with their start and end apart: 4, of which 4 were waited for; matrix products, arithmetic and copies ran while one was open for 7% of the time, Pallas kernels for 0%

profile of v9, /device:TPU:6, one launch (start us, length us, event | category | flops | bytes accessed | tf_op | source)
XLA Modules:
  0.0 215.3 jit_solution(14008528465604300528)
XLA Ops:
  6.5 0.7 all-gather.2.cloned.1.call-update
  7.3 0.8 stack.14
  8.0 0.9 select_reduce_fusion.4
  9.0 0.9 select_reduce_fusion.3
  10.0 0.9 select_reduce_fusion.1
  12.0 0.2 dynamic-slice_reduce_fusion.1
  12.2 0.2 dynamic-slice_reduce_fusion
  13.2 0.3 multiply_cosine_fusion
  13.5 39.4 %all-gather.2.cloned.1.call-done = bf16[256,4096]{1,0:T(8,128)(2,1)} async-done(((bf16[256,512]{1,0:T(8,128)(2,1)}), bf16[256,4096]{1,0:T(8,128)(2,1)}) %all-gather.2.cloned.1.call-update) | async-done | bytes 2097168 | tf_op jit(solution)/shard_map/all_gather | solution.py:254
  52.9 3.3 %fusion.51 = f32[256,256]{0,1:T(8,128)S(1)} fusion(bf16[256,4096]{1,0:T(8,128)(2,1)} %all-gather.2.cloned.1.call-done, bf16[4096,256]{1,0:T(8,128)(2,1)} %param.13), kind=kOutput, calls=%fused_computation.126 | convolution fusion | flops 536870912 | bytes 4456448 | tf_op jit(solution)/shard_map/dot_general | solution.py:257
  56.3 0.2 copy-done.2
  56.4 1.0 fusion.50
  57.7 0.7 convolution_convert_fusion
  58.4 1.9 copy.157
  60.3 7.6 %all-to-all-start = ((bf16[32,2,64,256]{3,2,1,0:T(8,128)(2,1)}), bf16[32,2,64,256]{3,2,1,0:T(8,128)(2,1)}, u32[]{:S(2)}, u32[]{:S(2)}) async-start(bf16[32,2,64,256]{3,2,1,0:T(8,128)(2,1)} %bitcast.68), calls=%async_computation | async-start | bytes 4194304 | tf_op jit(solution)/shard_map/all_to_all | solution.py:304
  68.0 0.6 dynamic_slice.15.nlen_ref
  68.6 0.7 convert_reduce_fusion.4
  69.2 0.7 convert_reduce_fusion.2
  69.9 0.2 convert_reduce_fusion.1
  70.1 0.6 select_reduce_fusion.5.perm_ref
  70.7 23.6 %all-to-all-done = bf16[32,2,64,256]{3,2,1,0:T(8,128)(2,1)} async-done(((bf16[32,2,64,256]{3,2,1,0:T(8,128)(2,1)}), bf16[32,2,64,256]{3,2,1,0:T(8,128)(2,1)}, u32[]{:S(2)}, u32[]{:S(2)}) %all-to-all-start) | async-done | bytes 2097184 | tf_op jit(solution)/shard_map/all_to_all | solution.py:304
  94.3 11.8 %shard_map.109 = (bf16[32,144,256]{2,1,0:T(8,128)(2,1)}, f32[64,128]{1,0:T(8,128)}) custom-call(s32[64]{0:T(128)} %select_reduce_fusion.5.perm_ref, s32[8]{0:T(128)} %get-tuple-element.10.start_ref, s32[8]{0:T(128)} %get-tuple-element.9.count_ref, s32[8]{0:T(128)} %dynamic_slice.15.nlen_ref, s32[1]{0:T(128)} %bitcast.1.total_ref, ...), custom_call_target="tpu_custom_call" | custom-call | flops 1073741824 | bytes 6291456 | tf_op jit(solution)/shard_map/pallas_call | solution.py:148
  106.2 0.8 reduce-precision_convert_fusion
  107.0 0.8 fusion.12
  107.7 8.2 %all-to-all-start.1 = ((bf16[32,144,256]{2,1,0:T(8,128)(2,1)}), bf16[32,144,256]{2,1,0:T(8,128)(2,1)}, u32[]{:S(2)}, u32[]{:S(2)}) async-start(bf16[32,144,256]{2,1,0:T(8,128)(2,1)} %fusion.12), calls=%async_computation.1 | async-start | bytes 4718592 | tf_op jit(solution)/shard_map/all_to_all | solution.py:331
  116.5 0.1 copy.143
  116.6 0.1 concatenate.53
  116.7 0.1 copy.142
  116.9 0.1 copy.141
  117.0 0.1 copy.140
  117.2 2.9 %convolution_convert_fusion.2 = bf16[256,256]{1,0:T(8,128)(2,1)S(1)} fusion(bf16[256,4096]{1,0:T(8,128)(2,1)} %all-gather.2.cloned.1.call-done, bf16[4096,256]{1,0:T(8,128)(2,1)} %param.14), kind=kOutput, calls=%fused_computation.8 | convolution fusion | flops 536936448 | bytes 4325376 | tf_op jit(solution)/shard_map/dot_general | solution.py:257
  120.2 0.3 fusion.49
  120.5 0.2 fusion.2
  120.8 0.9 copy.150
  121.7 23.4 %all-to-all-done.1 = bf16[32,144,256]{2,1,0:T(8,128)(2,1)} async-done(((bf16[32,144,256]{2,1,0:T(8,128)(2,1)}), bf16[32,144,256]{2,1,0:T(8,128)(2,1)}, u32[]{:S(2)}, u32[]{:S(2)}) %all-to-all-start.1) | async-done | bytes 2359328 | tf_op jit(solution)/shard_map/all_to_all | solution.py:331
  145.1 2.3 %gather_fusion = bf16[12,144,256]{2,1,0:T(8,128)(2,1)S(1)} fusion(bf16[32,144,256]{2,1,0:T(8,128)(2,1)} %all-to-all-done.1, s32[1024]{0:T(1024)S(1)} %pad_clamp_fusion), kind=kCustom, calls=%fused_computation | custom fusion | bytes 1769520 | tf_op jit(solution)/shard_map/jit(_take)/gather | solution.py:332
  147.4 0.1 broadcast_select_fusion
  147.6 1.0 fusion.10
  148.6 1.5 reshape.443
  150.4 0.2 copy.147
  150.7 2.3 %fusion.3 = f32[4,64,2,128]{3,2,1,0:T(2,128)S(1)} fusion(f32[1,4,64,2,128]{4,3,2,1,0:T(2,128)} %copy.150, f32[3,4,64,2,128]{4,3,2,1,0:T(2,128)S(1)} %reshape.443, f32[4,4,64,2]{3,2,1,0:T(8,128)S(1)} %copy.147), kind=kLoop, calls=%fused_computation.10 | loop fusion | flops 720896 | bytes 1318912 | tf_op jit(solution)/shard_map/reduce_sum | solution.py:353
  153.0 0.3 divide_convert_fusion
  153.4 2.1 convolution_convert_fusion.1
  155.5 39.9 %reduce-scatter.2.cloned.1.call-done = bf16[256,512]{1,0:T(8,128)(2,1)} async-done(((bf16[256,4096]{1,0:T(8,128)(2,1)}), bf16[256,512]{1,0:T(8,128)(2,1)}) %reduce-scatter.2.cloned.1.call-update) | async-done | bytes 262160 | tf_op jit(solution)/shard_map/reduce_scatter | solution.py:356
  195.4 1.6 fusion.7
  197.0 8.9 %shard_map.110 = f32[1,256]{1,0:T(1,128)} custom-call(f32[1,256]{1,0:T(1,128)} %bitcast.79), custom_call_target="tpu_custom_call" | custom-call | tf_op jit(solution)/shard_map/pallas_call | solution.py:198
  206.0 0.7 add_rsqrt_fusion
  206.7 1.8 fusion.6
  (70 shorter events, 3.3 us)
Async XLA Ops:
  6.5 146.8 %copy-start = (bf16[256,4096]{1,0:T(8,128)(2,1)S(1)}, bf16[256,4096]{1,0:T(8,128)(2,1)}, u32[]{:S(2)}) copy-start(bf16[256,4096]{1,0:T(8,128)(2,1)} %param.15) | copy-start | bytes 6291460
  6.5 46.4 %all-gather.2.cloned.1.call-start = ((), (), s32[]{:S(2)}) async-start(), calls=%async_computation.3 | async-start | bytes 2359296 | tf_op jit(solution)/shard_map/all_gather | solution.py:254
  52.9 3.3 %copy-start.1 = (bf16[256,4096]{1,0:T(8,128)(2,1)S(1)}, bf16[256,4096]{1,0:T(8,128)(2,1)}, u32[]{:S(2)}) copy-start(bf16[256,4096]{1,0:T(8,128)(2,1)} %all-gather.2.cloned.1.call-done) | copy-start | bytes 6291460
  52.9 3.5 %copy-start.2 = (bf16[4096,256]{1,0:T(8,128)(2,1)S(1)}, bf16[4096,256]{1,0:T(8,128)(2,1)}, u32[]{:S(2)}) copy-start(bf16[4096,256]{1,0:T(8,128)(2,1)} %param.12) | copy-start | bytes 6291460
  60.3 7.6 %copy-start.5 = (s32[256]{0:T(256)S(1)}, s32[256]{0:T(256)}, u32[]{:S(2)}) copy-start(s32[256]{0:T(256)} %param.20) | copy-start | bytes 3076
  60.3 34.0 %all-to-all-start = ((bf16[32,2,64,256]{3,2,1,0:T(8,128)(2,1)}), bf16[32,2,64,256]{3,2,1,0:T(8,128)(2,1)}, u32[]{:S(2)}, u32[]{:S(2)}) async-start(bf16[32,2,64,256]{3,2,1,0:T(8,128)(2,1)} %bitcast.68), calls=%async_computation | async-start | bytes 4194304 | tf_op jit(solution)/shard_map/all_to_all | solution.py:304
  107.7 37.4 %all-to-all-start.1 = ((bf16[32,144,256]{2,1,0:T(8,128)(2,1)}), bf16[32,144,256]{2,1,0:T(8,128)(2,1)}, u32[]{:S(2)}, u32[]{:S(2)}) async-start(bf16[32,144,256]{2,1,0:T(8,128)(2,1)} %fusion.12), calls=%async_computation.1 | async-start | bytes 4718592 | tf_op jit(solution)/shard_map/all_to_all | solution.py:331
  116.0 79.4 %reduce-scatter.2.cloned.1.call-start = ((), (), s32[]{:S(2)}) async-start(), calls=%async_computation.4 | async-start | bytes 2359296 | tf_op jit(solution)/shard_map/reduce_scatter | solution.py:356
  155.5 51.2 %copy-start.3 = (bf16[256,512]{1,0:T(8,128)(2,1)S(1)}, bf16[256,512]{1,0:T(8,128)(2,1)}, u32[]{:S(2)}) copy-start(bf16[256,512]{1,0:T(8,128)(2,1)} %param.11) | copy-start | bytes 786436
  155.5 51.2 %copy-start.4 = (f32[512]{0:T(512)S(1)}, f32[512]{0:T(512)}, u32[]{:S(2)}) copy-start(f32[512]{0:T(512)} %param.16) | copy-start | bytes 6148
Sparse Core Ops, SparseCore 0:
  9.1 43.7 all-gather.1
  155.6 39.7 reduce-scatter.1

commit v10 on v9

--- a/solution.py
+++ b/solution.py
@@ -296,11 +296,14 @@
     pick = (
         send_valid[:, :, None] & (send_item[:, :, None] % REQ_DEV == jnp.arange(REQ_DEV))
     ).reshape(leaf_count * all_slots, REQ_DEV)
-    outgoing = (
-        jnp.dot(pick.astype(jnp.bfloat16), q_blocks, preferred_element_type=jnp.float32)
-        .astype(jnp.bfloat16)
-        .reshape(leaf_count, all_slots, REQ_LEN, width_local)
-    )
+    outgoing = jnp.sum(
+        jnp.where(
+            pick[:, :, None, None],
+            q_blocks.reshape(REQ_DEV, REQ_LEN, width_local)[None],
+            jnp.zeros((), jnp.bfloat16),
+        ),
+        axis=1,
+    ).reshape(leaf_count, all_slots, REQ_LEN, width_local)
     arrived = lax.all_to_all(outgoing, "leaf", split_axis=0, concat_axis=0, tiled=True)
     recv_hit = (holders[:, None, :] == device) & (ranks[:, None, :] == slot_ids[None, :, None])
     slot_nodes = jnp.sum(jnp.where(recv_hit, per_sender[:, None, :], 0), axis=2).reshape(-1)

time: 216 us -> 215 us (level)
  other arithmetic: 15.5 us -> 18 us
    reduce_sum x0 -> x1, other arithmetic: none -> 2.37 us  [on_device(): jnp.sum(jnp.where(pick[:, :, None, None], q_blocks.reshape(REQ_DEV, REQ_L...]
where the time goes in v10:
time: 215 us
  waiting for transfers between devices  127 us (59%)
  Pallas kernels  20.4 us (9%)
  other arithmetic  18 us (8%)
  starting transfers between devices  15.6 us (7%)
  between operations  13.8 us (6%)
  local copies, waits for them, and re-layouts  9.8 us (5%)
  matrix products  9.8 us (5%)
    reduce_scatter x1, waiting for transfers between devices, on_device(): lax.psum_scatter(partial_value.astype(jnp.bfloat16), 'mp', scatter_dimens...  40.3 us
    all_gather x1, waiting for transfers between devices, on_device(): columns = lax.all_gather(activations, 'mp', axis=1, tiled=True)  39.3 us
    all_to_all x1, waiting for transfers between devices, on_device(): lax.all_to_all(outgoing, 'leaf', split_axis=0, concat_axis=0, tiled=True)  23.6 us
    all_to_all x1, waiting for transfers between devices, on_device(): lax.all_to_all(payload, 'leaf', split_axis=0, concat_axis=0, tiled=True)  23.2 us
    pallas_call x1, Pallas kernels, node_attention(): pl.pallas_call(node_kernel, out_shape=(jax.ShapeDtypeStruct((slots // 2,...  11.5 us
    pallas_call x1, Pallas kernels, mp_sum(): pl.pallas_call(sum_kernel, out_shape=jax.ShapeDtypeStruct(x.shape, x.dtyp...  8.94 us
    all_to_all x1, starting transfers between devices, on_device(): lax.all_to_all(payload, 'leaf', split_axis=0, concat_axis=0, tiled=True)  7.77 us
    all_to_all x1, starting transfers between devices, on_device(): lax.all_to_all(outgoing, 'leaf', split_axis=0, concat_axis=0, tiled=True)  7.64 us
  transfers between devices with their start and end apart: 4, of which 4 were waited for; matrix products, arithmetic and copies ran while one was open for 7% of the time, Pallas kernels for 0%

profile of v10, /device:TPU:6, one launch (start us, length us, event | category | flops | bytes accessed | tf_op | source)
XLA Modules:
  0.0 214.6 jit_solution(14356508971811887362)
XLA Ops:
  6.5 0.7 all-gather.2.cloned.1.call-update
  7.3 0.8 stack.14
  8.0 0.9 select_reduce_fusion.5
  9.0 0.9 select_reduce_fusion.4
  10.0 0.9 select_reduce_fusion.2
  12.0 0.2 dynamic-slice_reduce_fusion.1
  12.2 0.2 dynamic-slice_reduce_fusion
  13.3 0.3 multiply_cosine_fusion
  13.6 39.3 %all-gather.2.cloned.1.call-done = bf16[256,4096]{1,0:T(8,128)(2,1)} async-done(((bf16[256,512]{1,0:T(8,128)(2,1)}), bf16[256,4096]{1,0:T(8,128)(2,1)}) %all-gather.2.cloned.1.call-update) | async-done | bytes 2097168 | tf_op jit(solution)/shard_map/all_gather | solution.py:254
  52.9 3.3 %fusion.48 = f32[256,256]{0,1:T(8,128)S(1)} fusion(bf16[256,4096]{1,0:T(8,128)(2,1)} %all-gather.2.cloned.1.call-done, bf16[4096,256]{1,0:T(8,128)(2,1)} %param.13), kind=kOutput, calls=%fused_computation.124 | convolution fusion | flops 536870912 | bytes 4456448 | tf_op jit(solution)/shard_map/dot_general | solution.py:257
  56.3 0.2 copy-done.2
  56.4 1.0 fusion.47
  57.7 2.4 %select_reduce_fusion = bf16[64,64,256]{2,1,0:T(8,128)(2,1)} fusion(pred[64,4]{1,0:T(8,128)(4,1)S(1)} %fusion.29, bf16[4,64,256]{2,1,0:T(8,128)(2,1)S(1)} %convert_element_type.81), kind=kLoop, calls=%fused_computation.1 | loop fusion | flops 7340032 | bytes 2228480 | tf_op jit(solution)/shard_map/reduce_sum | solution.py:299
  60.1 7.6 %all-to-all-start = ((bf16[32,2,64,256]{3,2,1,0:T(8,128)(2,1)}), bf16[32,2,64,256]{3,2,1,0:T(8,128)(2,1)}, u32[]{:S(2)}, u32[]{:S(2)}) async-start(bf16[32,2,64,256]{3,2,1,0:T(8,128)(2,1)} %bitcast.65), calls=%async_computation | async-start | bytes 4194304 | tf_op jit(solution)/shard_map/all_to_all | solution.py:307
  67.7 0.6 dynamic_slice.15.nlen_ref
  68.3 0.7 convert_reduce_fusion.4
  69.0 0.7 convert_reduce_fusion.2
  69.7 0.2 convert_reduce_fusion.1
  69.9 0.6 select_reduce_fusion.6.perm_ref
  70.5 23.6 %all-to-all-done = bf16[32,2,64,256]{3,2,1,0:T(8,128)(2,1)} async-done(((bf16[32,2,64,256]{3,2,1,0:T(8,128)(2,1)}), bf16[32,2,64,256]{3,2,1,0:T(8,128)(2,1)}, u32[]{:S(2)}, u32[]{:S(2)}) %all-to-all-start) | async-done | bytes 2097184 | tf_op jit(solution)/shard_map/all_to_all | solution.py:307
  94.1 11.5 %shard_map.109 = (bf16[32,144,256]{2,1,0:T(8,128)(2,1)}, f32[64,128]{1,0:T(8,128)}) custom-call(s32[64]{0:T(128)} %select_reduce_fusion.6.perm_ref, s32[8]{0:T(128)} %get-tuple-element.10.start_ref, s32[8]{0:T(128)} %get-tuple-element.9.count_ref, s32[8]{0:T(128)} %dynamic_slice.15.nlen_ref, s32[1]{0:T(128)} %bitcast.1.total_ref, ...), custom_call_target="tpu_custom_call" | custom-call | flops 1073741824 | bytes 6291456 | tf_op jit(solution)/shard_map/pallas_call | solution.py:148
  105.6 0.8 reduce-precision_convert_fusion
  106.3 0.8 fusion.12
  107.1 7.8 %all-to-all-start.1 = ((bf16[32,144,256]{2,1,0:T(8,128)(2,1)}), bf16[32,144,256]{2,1,0:T(8,128)(2,1)}, u32[]{:S(2)}, u32[]{:S(2)}) async-start(bf16[32,144,256]{2,1,0:T(8,128)(2,1)} %fusion.12), calls=%async_computation.1 | async-start | bytes 4718592 | tf_op jit(solution)/shard_map/all_to_all | solution.py:334
  114.9 0.2 reduce-scatter.2.cloned.1.call-start
  115.6 0.1 copy.144
  115.7 0.1 concatenate.53
  115.8 0.1 copy.143
  116.0 0.1 copy.142
  116.1 0.1 copy.141
  116.3 2.9 %convolution_convert_fusion.1 = bf16[256,256]{1,0:T(8,128)(2,1)S(1)} fusion(bf16[256,4096]{1,0:T(8,128)(2,1)} %all-gather.2.cloned.1.call-done, bf16[4096,256]{1,0:T(8,128)(2,1)} %param.14), kind=kOutput, calls=%fused_computation.8 | convolution fusion | flops 536936448 | bytes 4325376 | tf_op jit(solution)/shard_map/dot_general | solution.py:257
  119.3 0.3 fusion.46
  119.6 0.2 fusion.2
  119.9 0.9 copy.151
  120.8 23.2 %all-to-all-done.1 = bf16[32,144,256]{2,1,0:T(8,128)(2,1)} async-done(((bf16[32,144,256]{2,1,0:T(8,128)(2,1)}), bf16[32,144,256]{2,1,0:T(8,128)(2,1)}, u32[]{:S(2)}, u32[]{:S(2)}) %all-to-all-start.1) | async-done | bytes 2359328 | tf_op jit(solution)/shard_map/all_to_all | solution.py:334
  144.0 2.3 %gather_fusion = bf16[12,144,256]{2,1,0:T(8,128)(2,1)S(1)} fusion(bf16[32,144,256]{2,1,0:T(8,128)(2,1)} %all-to-all-done.1, s32[1024]{0:T(1024)S(1)} %pad_clamp_fusion), kind=kCustom, calls=%fused_computation | custom fusion | bytes 1769520 | tf_op jit(solution)/shard_map/jit(_take)/gather | solution.py:335
  146.3 0.1 broadcast_select_fusion
  146.5 1.0 fusion.10
  147.5 1.5 reshape.468
  149.3 0.2 copy.148
  149.7 2.3 %fusion.3 = f32[4,64,2,128]{3,2,1,0:T(2,128)S(1)} fusion(f32[1,4,64,2,128]{4,3,2,1,0:T(2,128)} %copy.151, f32[3,4,64,2,128]{4,3,2,1,0:T(2,128)S(1)} %reshape.468, f32[4,4,64,2]{3,2,1,0:T(8,128)S(1)} %copy.148), kind=kLoop, calls=%fused_computation.10 | loop fusion | flops 720896 | bytes 1318912 | tf_op jit(solution)/shard_map/reduce_sum | solution.py:356
  152.0 0.3 divide_convert_fusion
  152.3 2.1 convolution_convert_fusion
  154.4 40.3 %reduce-scatter.2.cloned.1.call-done = bf16[256,512]{1,0:T(8,128)(2,1)} async-done(((bf16[256,4096]{1,0:T(8,128)(2,1)}), bf16[256,512]{1,0:T(8,128)(2,1)}) %reduce-scatter.2.cloned.1.call-update) | async-done | bytes 262160 | tf_op jit(solution)/shard_map/reduce_scatter | solution.py:359
  194.7 1.6 fusion.7
  196.3 8.9 %shard_map.110 = f32[1,256]{1,0:T(1,128)} custom-call(f32[1,256]{1,0:T(1,128)} %bitcast.75), custom_call_target="tpu_custom_call" | custom-call | tf_op jit(solution)/shard_map/pallas_call | solution.py:198
  205.3 0.7 add_rsqrt_fusion
  206.0 1.8 fusion.6
  (70 shorter events, 3.4 us)
Async XLA Ops:
  6.5 145.8 %copy-start = (bf16[256,4096]{1,0:T(8,128)(2,1)S(1)}, bf16[256,4096]{1,0:T(8,128)(2,1)}, u32[]{:S(2)}) copy-start(bf16[256,4096]{1,0:T(8,128)(2,1)} %param.15) | copy-start | bytes 6291460
  6.5 46.4 %all-gather.2.cloned.1.call-start = ((), (), s32[]{:S(2)}) async-start(), calls=%async_computation.3 | async-start | bytes 2359296 | tf_op jit(solution)/shard_map/all_gather | solution.py:254
  52.9 3.3 %copy-start.1 = (bf16[256,4096]{1,0:T(8,128)(2,1)S(1)}, bf16[256,4096]{1,0:T(8,128)(2,1)}, u32[]{:S(2)}) copy-start(bf16[256,4096]{1,0:T(8,128)(2,1)} %all-gather.2.cloned.1.call-done) | copy-start | bytes 6291460
  52.9 3.5 %copy-start.2 = (bf16[4096,256]{1,0:T(8,128)(2,1)S(1)}, bf16[4096,256]{1,0:T(8,128)(2,1)}, u32[]{:S(2)}) copy-start(bf16[4096,256]{1,0:T(8,128)(2,1)} %param.12) | copy-start | bytes 6291460
  60.1 7.6 %copy-start.5 = (s32[256]{0:T(256)S(1)}, s32[256]{0:T(256)}, u32[]{:S(2)}) copy-start(s32[256]{0:T(256)} %param.20) | copy-start | bytes 3076
  60.1 34.0 %all-to-all-start = ((bf16[32,2,64,256]{3,2,1,0:T(8,128)(2,1)}), bf16[32,2,64,256]{3,2,1,0:T(8,128)(2,1)}, u32[]{:S(2)}, u32[]{:S(2)}) async-start(bf16[32,2,64,256]{3,2,1,0:T(8,128)(2,1)} %bitcast.65), calls=%async_computation | async-start | bytes 4194304 | tf_op jit(solution)/shard_map/all_to_all | solution.py:307
  107.1 36.9 %all-to-all-start.1 = ((bf16[32,144,256]{2,1,0:T(8,128)(2,1)}), bf16[32,144,256]{2,1,0:T(8,128)(2,1)}, u32[]{:S(2)}, u32[]{:S(2)}) async-start(bf16[32,144,256]{2,1,0:T(8,128)(2,1)} %fusion.12), calls=%async_computation.1 | async-start | bytes 4718592 | tf_op jit(solution)/shard_map/all_to_all | solution.py:334
  114.9 79.8 %reduce-scatter.2.cloned.1.call-start = ((), (), s32[]{:S(2)}) async-start(), calls=%async_computation.4 | async-start | bytes 2359296 | tf_op jit(solution)/shard_map/reduce_scatter | solution.py:359
  154.4 51.6 %copy-start.3 = (bf16[256,512]{1,0:T(8,128)(2,1)S(1)}, bf16[256,512]{1,0:T(8,128)(2,1)}, u32[]{:S(2)}) copy-start(bf16[256,512]{1,0:T(8,128)(2,1)} %param.11) | copy-start | bytes 786436
  154.4 51.6 %copy-start.4 = (f32[512]{0:T(512)S(1)}, f32[512]{0:T(512)}, u32[]{:S(2)}) copy-start(f32[512]{0:T(512)} %param.16) | copy-start | bytes 6148
Sparse Core Ops, SparseCore 0:
  9.1 43.7 all-gather.1
  154.5 40.1 reduce-scatter.1

commit v11 on v9

--- a/solution.py
+++ b/solution.py
@@ -297,10 +297,13 @@
         send_valid[:, :, None] & (send_item[:, :, None] % REQ_DEV == jnp.arange(REQ_DEV))
     ).reshape(leaf_count * all_slots, REQ_DEV)
     outgoing = (
-        jnp.dot(pick.astype(jnp.bfloat16), q_blocks, preferred_element_type=jnp.float32)
-        .astype(jnp.bfloat16)
-        .reshape(leaf_count, all_slots, REQ_LEN, width_local)
-    )
+        jnp.take(
+            q_blocks.reshape(REQ_DEV, REQ_LEN, width_local),
+            (send_item % REQ_DEV).reshape(-1),
+            axis=0,
+        )
+        * send_valid.reshape(-1, 1, 1).astype(jnp.bfloat16)
+    ).reshape(leaf_count, all_slots, REQ_LEN, width_local)
     arrived = lax.all_to_all(outgoing, "leaf", split_axis=0, concat_axis=0, tiled=True)
     recv_hit = (holders[:, None, :] == device) & (ranks[:, None, :] == slot_ids[None, :, None])
     slot_nodes = jnp.sum(jnp.where(recv_hit, per_sender[:, None, :], 0), axis=2).reshape(-1)

time: 216 us -> 218 us (level)
  other arithmetic: 15.5 us -> 18.7 us
    mul x0 -> x1, other arithmetic: none -> 3.21 us  [on_device(): jnp.take(q_blocks.reshape(REQ_DEV, REQ_LEN, width_local), (send_item % RE...]
where the time goes in v11:
time: 218 us; the launch traced here: 217 us
  waiting for transfers between devices  127 us (58%)
  Pallas kernels  21.1 us (10%)
  other arithmetic  18.7 us (9%)
  starting transfers between devices  15.1 us (7%)
  between operations  13.8 us (6%)
  local copies, waits for them, and re-layouts  11.6 us (5%)
  matrix products  9.81 us (4%)
    all_gather x1, waiting for transfers between devices, on_device(): columns = lax.all_gather(activations, 'mp', axis=1, tiled=True)  40.2 us
    reduce_scatter x1, waiting for transfers between devices, on_device(): lax.psum_scatter(partial_value.astype(jnp.bfloat16), 'mp', scatter_dimens...  39.6 us
    all_to_all x1, waiting for transfers between devices, on_device(): lax.all_to_all(payload, 'leaf', split_axis=0, concat_axis=0, tiled=True)  23.4 us
    all_to_all x1, waiting for transfers between devices, on_device(): lax.all_to_all(outgoing, 'leaf', split_axis=0, concat_axis=0, tiled=True)  23.1 us
    pallas_call x1, Pallas kernels, node_attention(): pl.pallas_call(node_kernel, out_shape=(jax.ShapeDtypeStruct((slots // 2,...  12.1 us
    pallas_call x1, Pallas kernels, mp_sum(): pl.pallas_call(sum_kernel, out_shape=jax.ShapeDtypeStruct(x.shape, x.dtyp...  9.05 us
    all_to_all x1, starting transfers between devices, on_device(): lax.all_to_all(outgoing, 'leaf', split_axis=0, concat_axis=0, tiled=True)  7.63 us
    all_to_all x1, starting transfers between devices, on_device(): lax.all_to_all(payload, 'leaf', split_axis=0, concat_axis=0, tiled=True)  7.44 us
  transfers between devices with their start and end apart: 4, of which 4 were waited for; matrix products, arithmetic and copies ran while one was open for 7% of the time, Pallas kernels for 0%

profile of v11, /device:TPU:6, one launch (start us, length us, event | category | flops | bytes accessed | tf_op | source)
XLA Modules:
  0.0 217.1 jit_solution(10622182161754793525)
XLA Ops:
  6.5 0.7 all-gather.2.cloned.1.call-update
  7.3 0.8 stack.14
  8.0 0.9 select_reduce_fusion.4
  9.0 0.9 select_reduce_fusion.3
  10.0 0.9 select_reduce_fusion.1
  11.5 0.2 dynamic-slice_reduce_fusion
  12.5 0.3 multiply_cosine_fusion
  12.8 40.2 %all-gather.2.cloned.1.call-done = bf16[256,4096]{1,0:T(8,128)(2,1)} async-done(((bf16[256,512]{1,0:T(8,128)(2,1)}), bf16[256,4096]{1,0:T(8,128)(2,1)}) %all-gather.2.cloned.1.call-update) | async-done | bytes 2097168 | tf_op jit(solution)/shard_map/all_gather | solution.py:254
  52.9 3.3 %fusion.50 = f32[256,256]{0,1:T(8,128)S(1)} fusion(bf16[256,4096]{1,0:T(8,128)(2,1)} %all-gather.2.cloned.1.call-done, bf16[4096,256]{1,0:T(8,128)(2,1)} %param.13), kind=kOutput, calls=%fused_computation.133 | convolution fusion | flops 536870912 | bytes 4456448 | tf_op jit(solution)/shard_map/dot_general | solution.py:257
  56.3 0.2 copy-done.2
  56.4 1.0 fusion.49
  57.7 2.0 gather_fusion
  59.7 3.2 %select_multiply_fusion = bf16[32,2,64,256]{3,2,1,0:T(8,128)(2,1)} fusion(bf16[32,2,64,256]{3,2,1,0:T(8,128)(2,1)} %bitcast.67, pred[32,2]{1,0:T(8,128)(4,1)S(1)} %copy.138, bf16[32,2]{1,0:T(8,128)(2,1)S(1)} %copy.141), kind=kLoop, calls=%fused_computation.3 | loop fusion | flops 2097152 | bytes 4194496 | tf_op jit(solution)/shard_map/mul | solution.py:300
  62.9 7.6 %all-to-all-start = ((bf16[32,2,64,256]{3,2,1,0:T(8,128)(2,1)}), bf16[32,2,64,256]{3,2,1,0:T(8,128)(2,1)}, u32[]{:S(2)}, u32[]{:S(2)}) async-start(bf16[32,2,64,256]{3,2,1,0:T(8,128)(2,1)} %select_multiply_fusion), calls=%async_computation | async-start | bytes 4194304 | tf_op jit(solution)/shard_map/all_to_all | solution.py:307
  71.0 0.6 dynamic_slice.15.nlen_ref
  71.6 0.7 convert_reduce_fusion.4
  72.3 0.7 convert_reduce_fusion.2
  73.0 0.2 convert_reduce_fusion.1
  73.2 0.6 select_reduce_fusion.5.perm_ref
  73.8 23.1 %all-to-all-done = bf16[32,2,64,256]{3,2,1,0:T(8,128)(2,1)} async-done(((bf16[32,2,64,256]{3,2,1,0:T(8,128)(2,1)}), bf16[32,2,64,256]{3,2,1,0:T(8,128)(2,1)}, u32[]{:S(2)}, u32[]{:S(2)}) %all-to-all-start) | async-done | bytes 2097184 | tf_op jit(solution)/shard_map/all_to_all | solution.py:307
  96.9 12.1 %shard_map.109 = (bf16[32,144,256]{2,1,0:T(8,128)(2,1)}, f32[64,128]{1,0:T(8,128)}) custom-call(s32[64]{0:T(128)} %select_reduce_fusion.5.perm_ref, s32[8]{0:T(128)} %get-tuple-element.10.start_ref, s32[8]{0:T(128)} %get-tuple-element.9.count_ref, s32[8]{0:T(128)} %dynamic_slice.15.nlen_ref, s32[1]{0:T(128)} %bitcast.1.total_ref, ...), custom_call_target="tpu_custom_call" | custom-call | flops 1073741824 | bytes 6291456 | tf_op jit(solution)/shard_map/pallas_call | solution.py:148
  109.0 0.8 reduce-precision_convert_fusion
  109.8 0.8 fusion.12
  110.5 7.4 %all-to-all-start.1 = ((bf16[32,144,256]{2,1,0:T(8,128)(2,1)}), bf16[32,144,256]{2,1,0:T(8,128)(2,1)}, u32[]{:S(2)}, u32[]{:S(2)}) async-start(bf16[32,144,256]{2,1,0:T(8,128)(2,1)} %fusion.12), calls=%async_computation.1 | async-start | bytes 4718592 | tf_op jit(solution)/shard_map/all_to_all | solution.py:334
  118.4 0.1 concatenate.54
  118.5 0.1 copy.145
  118.6 0.1 concatenate.53
  118.8 0.1 copy.144
  118.9 0.1 copy.143
  119.1 0.1 copy.142
  119.2 2.9 %convolution_convert_fusion.1 = bf16[256,256]{1,0:T(8,128)(2,1)S(1)} fusion(bf16[256,4096]{1,0:T(8,128)(2,1)} %all-gather.2.cloned.1.call-done, bf16[4096,256]{1,0:T(8,128)(2,1)} %param.14), kind=kOutput, calls=%fused_computation.9 | convolution fusion | flops 536936448 | bytes 4325376 | tf_op jit(solution)/shard_map/dot_general | solution.py:257
  122.2 0.3 fusion.48
  122.6 0.2 fusion.2
  122.8 0.9 copy.152
  123.7 23.4 %all-to-all-done.1 = bf16[32,144,256]{2,1,0:T(8,128)(2,1)} async-done(((bf16[32,144,256]{2,1,0:T(8,128)(2,1)}), bf16[32,144,256]{2,1,0:T(8,128)(2,1)}, u32[]{:S(2)}, u32[]{:S(2)}) %all-to-all-start.1) | async-done | bytes 2359328 | tf_op jit(solution)/shard_map/all_to_all | solution.py:334
  147.2 2.3 %gather_fusion.1 = bf16[12,144,256]{2,1,0:T(8,128)(2,1)S(1)} fusion(bf16[32,144,256]{2,1,0:T(8,128)(2,1)} %all-to-all-done.1, s32[1024]{0:T(1024)S(1)} %pad_clamp_fusion), kind=kCustom, calls=%fused_computation.1 | custom fusion | bytes 1769520 | tf_op jit(solution)/shard_map/jit(_take)/gather | solution.py:335
  149.4 0.1 broadcast_select_fusion
  149.6 1.0 fusion.10
  150.6 1.5 reshape.493
  152.4 0.2 copy.149
  152.8 2.3 %fusion.3 = f32[4,64,2,128]{3,2,1,0:T(2,128)S(1)} fusion(f32[1,4,64,2,128]{4,3,2,1,0:T(2,128)} %copy.152, f32[3,4,64,2,128]{4,3,2,1,0:T(2,128)S(1)} %reshape.493, f32[4,4,64,2]{3,2,1,0:T(8,128)S(1)} %copy.149), kind=kLoop, calls=%fused_computation.11 | loop fusion | flops 720896 | bytes 1318912 | tf_op jit(solution)/shard_map/reduce_sum | solution.py:356
  155.1 0.3 divide_convert_fusion
  155.4 2.1 convolution_convert_fusion
  157.5 39.6 %reduce-scatter.2.cloned.1.call-done = bf16[256,512]{1,0:T(8,128)(2,1)} async-done(((bf16[256,4096]{1,0:T(8,128)(2,1)}), bf16[256,512]{1,0:T(8,128)(2,1)}) %reduce-scatter.2.cloned.1.call-update) | async-done | bytes 262160 | tf_op jit(solution)/shard_map/reduce_scatter | solution.py:359
  197.1 1.6 fusion.7
  198.8 9.1 %shard_map.110 = f32[1,256]{1,0:T(1,128)} custom-call(f32[1,256]{1,0:T(1,128)} %bitcast.77), custom_call_target="tpu_custom_call" | custom-call | tf_op jit(solution)/shard_map/pallas_call | solution.py:198
  207.8 0.7 add_rsqrt_fusion
  208.5 1.8 fusion.6
  (73 shorter events, 3.1 us)
Async XLA Ops:
  6.5 148.9 %copy-start = (bf16[256,4096]{1,0:T(8,128)(2,1)S(1)}, bf16[256,4096]{1,0:T(8,128)(2,1)}, u32[]{:S(2)}) copy-start(bf16[256,4096]{1,0:T(8,128)(2,1)} %param.15) | copy-start | bytes 6291460
  6.5 46.4 %all-gather.2.cloned.1.call-start = ((), (), s32[]{:S(2)}) async-start(), calls=%async_computation.3 | async-start | bytes 2359296 | tf_op jit(solution)/shard_map/all_gather | solution.py:254
  52.9 3.3 %copy-start.1 = (bf16[256,4096]{1,0:T(8,128)(2,1)S(1)}, bf16[256,4096]{1,0:T(8,128)(2,1)}, u32[]{:S(2)}) copy-start(bf16[256,4096]{1,0:T(8,128)(2,1)} %all-gather.2.cloned.1.call-done) | copy-start | bytes 6291460
  52.9 3.5 %copy-start.2 = (bf16[4096,256]{1,0:T(8,128)(2,1)S(1)}, bf16[4096,256]{1,0:T(8,128)(2,1)}, u32[]{:S(2)}) copy-start(bf16[4096,256]{1,0:T(8,128)(2,1)} %param.12) | copy-start | bytes 6291460
  62.9 8.1 %copy-start.5 = (s32[256]{0:T(256)S(1)}, s32[256]{0:T(256)}, u32[]{:S(2)}) copy-start(s32[256]{0:T(256)} %param.20) | copy-start | bytes 3076
  62.9 34.0 %all-to-all-start = ((bf16[32,2,64,256]{3,2,1,0:T(8,128)(2,1)}), bf16[32,2,64,256]{3,2,1,0:T(8,128)(2,1)}, u32[]{:S(2)}, u32[]{:S(2)}) async-start(bf16[32,2,64,256]{3,2,1,0:T(8,128)(2,1)} %select_multiply_fusion), calls=%async_computation | async-start | bytes 4194304 | tf_op jit(solution)/shard_map/all_to_all | solution.py:307
  110.5 36.6 %all-to-all-start.1 = ((bf16[32,144,256]{2,1,0:T(8,128)(2,1)}), bf16[32,144,256]{2,1,0:T(8,128)(2,1)}, u32[]{:S(2)}, u32[]{:S(2)}) async-start(bf16[32,144,256]{2,1,0:T(8,128)(2,1)} %fusion.12), calls=%async_computation.1 | async-start | bytes 4718592 | tf_op jit(solution)/shard_map/all_to_all | solution.py:334
  118.0 79.1 %reduce-scatter.2.cloned.1.call-start = ((), (), s32[]{:S(2)}) async-start(), calls=%async_computation.4 | async-start | bytes 2359296 | tf_op jit(solution)/shard_map/reduce_scatter | solution.py:359
  157.5 51.0 %copy-start.3 = (bf16[256,512]{1,0:T(8,128)(2,1)S(1)}, bf16[256,512]{1,0:T(8,128)(2,1)}, u32[]{:S(2)}) copy-start(bf16[256,512]{1,0:T(8,128)(2,1)} %param.11) | copy-start | bytes 786436
  157.5 51.0 %copy-start.4 = (f32[512]{0:T(512)S(1)}, f32[512]{0:T(512)}, u32[]{:S(2)}) copy-start(f32[512]{0:T(512)} %param.16) | copy-start | bytes 6148
Sparse Core Ops, SparseCore 0:
  9.1 43.7 all-gather.1
  157.7 39.4 reduce-scatter.1

commit v12 on v10

--- a/solution.py
+++ b/solution.py
@@ -163,7 +163,7 @@
     return out, lse
 
 
-def sum_kernel(x_ref, out_ref, recv, send_sem, recv_sem):
+def norm_kernel(x_ref, proj_ref, act_ref, gain_ref, out_ref, recv, send_sem, recv_sem):
     n = recv.shape[0]
     me = lax.axis_index("mp")
     barrier = pltpu.get_barrier_semaphore()
@@ -190,7 +190,27 @@
     total = x_ref[...]
     for d in range(1, n):
         total = total + recv[d]
-    out_ref[...] = total
+    scale_row = lax.rsqrt(total / D + norm_eps)
+    scale = jnp.transpose(jnp.broadcast_to(scale_row, (128, scale_row.shape[1])))[:, 0:1]
+    out_ref[...] = (
+        act_ref[...].astype(jnp.float32) + gain_ref[...] * proj_ref[...] * scale
+    ).astype(out_ref.dtype)
+
+
+def mp_norm(x, projected, activations, gain, n):
+    vmem = pl.BlockSpec(memory_space=pltpu.VMEM)
+    return pl.pallas_call(
+        norm_kernel,
+        out_shape=jax.ShapeDtypeStruct(activations.shape, activations.dtype),
+        in_specs=[vmem] * 4,
+        out_specs=vmem,
+        scratch_shapes=[
+            pltpu.VMEM((n,) + x.shape, x.dtype),
+            pltpu.SemaphoreType.DMA((n,)),
+            pltpu.SemaphoreType.DMA((n,)),
+        ],
+        compiler_params=pltpu.CompilerParams(collective_id=0, has_side_effects=True),
+    )(x, projected, activations, gain)
 
 
 def mp_sum(x, n):
@@ -359,13 +379,13 @@
     projected = lax.psum_scatter(
         partial_value.astype(jnp.bfloat16), "mp", scatter_dimension=1, tiled=True
     ).astype(jnp.float32)
-    squares = mp_sum(
-        jnp.sum(projected * projected, axis=1).reshape(1, tok_rows), lax.axis_size("mp")
-    ).reshape(tok_rows)
-    row_scale = lax.rsqrt(squares / D + norm_eps)
-    return (
-        activations.astype(jnp.float32) + norm_gain[None, :] * projected * row_scale[:, None]
-    ).astype(jnp.bfloat16)
+    return mp_norm(
+        jnp.sum(projected * projected, axis=1).reshape(1, tok_rows),
+        projected,
+        activations,
+        norm_gain.reshape(1, -1),
+        lax.axis_size("mp"),
+    )
 
 
 def solution(mesh):

time: 215 us -> 218 us (1.014)
  starting transfers between devices: 15.6 us -> 18.2 us
    all_to_all x1, starting transfers between devices: 7.77 us -> 10.3 us  [on_device(): lax.all_to_all(payload, 'leaf', split_axis=0, concat_axis=0, tiled=True)]
where the time goes in v12:
time: 218 us; the launch traced here: 217 us
  waiting for transfers between devices  127 us (58%)
  Pallas kernels  20 us (9%)
  starting transfers between devices  18.2 us (8%)
  other arithmetic  17.3 us (8%)
  between operations  13.8 us (6%)
  local copies, waits for them, and re-layouts  11.5 us (5%)
  matrix products  9.8 us (4%)
    reduce_scatter x1, waiting for transfers between devices, on_device(): lax.psum_scatter(partial_value.astype(jnp.bfloat16), 'mp', scatter_dimens...  39.9 us
    all_gather x1, waiting for transfers between devices, on_device(): columns = lax.all_gather(activations, 'mp', axis=1, tiled=True)  39.3 us
    all_to_all x1, waiting for transfers between devices, on_device(): lax.all_to_all(outgoing, 'leaf', split_axis=0, concat_axis=0, tiled=True)  23.6 us
    all_to_all x1, waiting for transfers between devices, on_device(): lax.all_to_all(payload, 'leaf', split_axis=0, concat_axis=0, tiled=True)  23.2 us
    all_to_all x1, starting transfers between devices, on_device(): lax.all_to_all(payload, 'leaf', split_axis=0, concat_axis=0, tiled=True)  10.3 us
    pallas_call x1, Pallas kernels, node_attention(): pl.pallas_call(node_kernel, out_shape=(jax.ShapeDtypeStruct((slots // 2,...  10.3 us
    pallas_call x1, Pallas kernels, mp_norm(): pl.pallas_call(norm_kernel, out_shape=jax.ShapeDtypeStruct(activations.sh...  9.71 us
    all_to_all x1, starting transfers between devices, on_device(): lax.all_to_all(outgoing, 'leaf', split_axis=0, concat_axis=0, tiled=True)  7.64 us
  transfers between devices with their start and end apart: 4, of which 4 were waited for; matrix products, arithmetic and copies ran while one was open for 7% of the time, Pallas kernels for 0%

profile of v12, /device:TPU:6, one launch (start us, length us, event | category | flops | bytes accessed | tf_op | source)
XLA Modules:
  0.0 217.4 jit_solution(2554478443311462637)
XLA Ops:
  6.5 0.7 all-gather.2.cloned.1.call-update
  7.3 0.8 stack.14
  8.0 0.9 select_reduce_fusion.5
  9.0 0.9 select_reduce_fusion.4
  10.0 0.9 select_reduce_fusion.2
  12.0 0.2 dynamic-slice_reduce_fusion.1
  12.2 0.2 dynamic-slice_reduce_fusion
  13.3 0.3 multiply_cosine_fusion
  13.6 39.3 %all-gather.2.cloned.1.call-done = bf16[256,4096]{1,0:T(8,128)(2,1)} async-done(((bf16[256,512]{1,0:T(8,128)(2,1)}), bf16[256,4096]{1,0:T(8,128)(2,1)}) %all-gather.2.cloned.1.call-update) | async-done | bytes 2097168 | tf_op jit(solution)/shard_map/all_gather | solution.py:274
  52.9 3.3 %fusion.44 = f32[256,256]{0,1:T(8,128)S(1)} fusion(bf16[256,4096]{1,0:T(8,128)(2,1)} %all-gather.2.cloned.1.call-done, bf16[4096,256]{1,0:T(8,128)(2,1)} %param.13), kind=kOutput, calls=%fused_computation.118 | convolution fusion | flops 536870912 | bytes 4456448 | tf_op jit(solution)/shard_map/dot_general | solution.py:277
  56.3 0.2 copy-done.2
  56.4 1.0 fusion.43
  57.7 2.4 %select_reduce_fusion = bf16[64,64,256]{2,1,0:T(8,128)(2,1)} fusion(pred[64,4]{1,0:T(8,128)(4,1)S(1)} %fusion.25, bf16[4,64,256]{2,1,0:T(8,128)(2,1)S(1)} %convert_element_type.74), kind=kLoop, calls=%fused_computation.1 | loop fusion | flops 7340032 | bytes 2228480 | tf_op jit(solution)/shard_map/reduce_sum | solution.py:319
  60.1 7.6 %all-to-all-start = ((bf16[32,2,64,256]{3,2,1,0:T(8,128)(2,1)}), bf16[32,2,64,256]{3,2,1,0:T(8,128)(2,1)}, u32[]{:S(2)}, u32[]{:S(2)}) async-start(bf16[32,2,64,256]{3,2,1,0:T(8,128)(2,1)} %bitcast.65), calls=%async_computation | async-start | bytes 4194304 | tf_op jit(solution)/shard_map/all_to_all | solution.py:327
  67.7 0.6 dynamic_slice.15.nlen_ref
  68.3 0.7 convert_reduce_fusion.4
  69.0 0.7 convert_reduce_fusion.2
  69.7 0.2 convert_reduce_fusion.1
  69.9 0.6 select_reduce_fusion.6.perm_ref
  70.5 23.6 %all-to-all-done = bf16[32,2,64,256]{3,2,1,0:T(8,128)(2,1)} async-done(((bf16[32,2,64,256]{3,2,1,0:T(8,128)(2,1)}), bf16[32,2,64,256]{3,2,1,0:T(8,128)(2,1)}, u32[]{:S(2)}, u32[]{:S(2)}) %all-to-all-start) | async-done | bytes 2097184 | tf_op jit(solution)/shard_map/all_to_all | solution.py:327
  94.1 10.3 %shard_map.109 = (bf16[32,144,256]{2,1,0:T(8,128)(2,1)}, f32[64,128]{1,0:T(8,128)}) custom-call(s32[64]{0:T(128)} %select_reduce_fusion.6.perm_ref, s32[8]{0:T(128)} %get-tuple-element.10.start_ref, s32[8]{0:T(128)} %get-tuple-element.9.count_ref, s32[8]{0:T(128)} %dynamic_slice.15.nlen_ref, s32[1]{0:T(128)} %bitcast.1.total_ref, ...), custom_call_target="tpu_custom_call" | custom-call | flops 1073741824 | bytes 6291456 | tf_op jit(solution)/shard_map/pallas_call | solution.py:148
  104.4 0.8 reduce-precision_convert_fusion
  105.2 0.8 fusion.8
  106.0 10.3 %all-to-all-start.1 = ((bf16[32,144,256]{2,1,0:T(8,128)(2,1)}), bf16[32,144,256]{2,1,0:T(8,128)(2,1)}, u32[]{:S(2)}, u32[]{:S(2)}) async-start(bf16[32,144,256]{2,1,0:T(8,128)(2,1)} %fusion.8), calls=%async_computation.1 | async-start | bytes 4718592 | tf_op jit(solution)/shard_map/all_to_all | solution.py:354
  116.3 0.2 reduce-scatter.2.cloned.1.call-start
  116.9 0.1 copy.144
  117.1 0.1 concatenate.53
  117.2 0.1 copy.143
  117.4 0.1 copy.142
  117.5 0.1 copy.141
  117.7 2.9 %convolution_convert_fusion.1 = bf16[256,256]{1,0:T(8,128)(2,1)S(1)} fusion(bf16[256,4096]{1,0:T(8,128)(2,1)} %all-gather.2.cloned.1.call-done, bf16[4096,256]{1,0:T(8,128)(2,1)} %param.14), kind=kOutput, calls=%fused_computation.8 | convolution fusion | flops 536936448 | bytes 4325376 | tf_op jit(solution)/shard_map/dot_general | solution.py:277
  120.6 0.3 fusion.42
  121.0 0.2 fusion.2
  121.3 0.9 copy.151
  122.2 23.2 %all-to-all-done.1 = bf16[32,144,256]{2,1,0:T(8,128)(2,1)} async-done(((bf16[32,144,256]{2,1,0:T(8,128)(2,1)}), bf16[32,144,256]{2,1,0:T(8,128)(2,1)}, u32[]{:S(2)}, u32[]{:S(2)}) %all-to-all-start.1) | async-done | bytes 2359328 | tf_op jit(solution)/shard_map/all_to_all | solution.py:354
  145.4 2.3 %gather_fusion = bf16[12,144,256]{2,1,0:T(8,128)(2,1)S(1)} fusion(bf16[32,144,256]{2,1,0:T(8,128)(2,1)} %all-to-all-done.1, s32[1024]{0:T(1024)S(1)} %pad_clamp_fusion), kind=kCustom, calls=%fused_computation | custom fusion | bytes 1769520 | tf_op jit(solution)/shard_map/jit(_take)/gather | solution.py:355
  147.7 0.1 broadcast_select_fusion
  147.9 1.0 fusion.6
  148.9 1.5 reshape.458
  150.7 0.2 copy.148
  151.0 2.3 %fusion.3 = f32[4,64,2,128]{3,2,1,0:T(2,128)S(1)} fusion(f32[1,4,64,2,128]{4,3,2,1,0:T(2,128)} %copy.151, f32[3,4,64,2,128]{4,3,2,1,0:T(2,128)S(1)} %reshape.458, f32[4,4,64,2]{3,2,1,0:T(8,128)S(1)} %copy.148), kind=kLoop, calls=%fused_computation.10 | loop fusion | flops 720896 | bytes 1318912 | tf_op jit(solution)/shard_map/reduce_sum | solution.py:376
  153.3 0.3 divide_convert_fusion
  153.7 2.1 convolution_convert_fusion
  155.8 39.9 %reduce-scatter.2.cloned.1.call-done = bf16[256,512]{1,0:T(8,128)(2,1)} async-done(((bf16[256,4096]{1,0:T(8,128)(2,1)}), bf16[256,512]{1,0:T(8,128)(2,1)}) %reduce-scatter.2.cloned.1.call-update) | async-done | bytes 262160 | tf_op jit(solution)/shard_map/reduce_scatter | solution.py:379
  195.7 1.6 multiply_reduce_fusion
  197.4 1.8 convert_element_type.81.proj_ref
  199.2 9.7 %shard_map.110 = bf16[256,512]{1,0:T(8,128)(2,1)} custom-call(f32[1,256]{1,0:T(1,128)} %bitcast.74, f32[256,512]{1,0:T(8,128)} %convert_element_type.81.proj_ref, bf16[256,512]{1,0:T(8,128)(2,1)} %act_ref.1, f32[1,512]{1,0:T(1,128)} %bitcast.75), custom_call_target="tpu_custom_call" | custom-call | tf_op jit(solution)/shard_map/pallas_call | solution.py:202
  208.9 1.7 copy.169
  (66 shorter events, 3.3 us)
Async XLA Ops:
  6.5 147.2 %copy-start = (bf16[256,4096]{1,0:T(8,128)(2,1)S(1)}, bf16[256,4096]{1,0:T(8,128)(2,1)}, u32[]{:S(2)}) copy-start(bf16[256,4096]{1,0:T(8,128)(2,1)} %param.15) | copy-start | bytes 6291460
  6.5 46.4 %all-gather.2.cloned.1.call-start = ((), (), s32[]{:S(2)}) async-start(), calls=%async_computation.3 | async-start | bytes 2359296 | tf_op jit(solution)/shard_map/all_gather | solution.py:274
  52.9 3.3 %copy-start.1 = (bf16[256,4096]{1,0:T(8,128)(2,1)S(1)}, bf16[256,4096]{1,0:T(8,128)(2,1)}, u32[]{:S(2)}) copy-start(bf16[256,4096]{1,0:T(8,128)(2,1)} %all-gather.2.cloned.1.call-done) | copy-start | bytes 6291460
  52.9 3.5 %copy-start.2 = (bf16[4096,256]{1,0:T(8,128)(2,1)S(1)}, bf16[4096,256]{1,0:T(8,128)(2,1)}, u32[]{:S(2)}) copy-start(bf16[4096,256]{1,0:T(8,128)(2,1)} %param.12) | copy-start | bytes 6291460
  60.1 7.6 %copy-start.3 = (s32[256]{0:T(256)S(1)}, s32[256]{0:T(256)}, u32[]{:S(2)}) copy-start(s32[256]{0:T(256)} %param.20) | copy-start | bytes 3076
  60.1 34.0 %all-to-all-start = ((bf16[32,2,64,256]{3,2,1,0:T(8,128)(2,1)}), bf16[32,2,64,256]{3,2,1,0:T(8,128)(2,1)}, u32[]{:S(2)}, u32[]{:S(2)}) async-start(bf16[32,2,64,256]{3,2,1,0:T(8,128)(2,1)} %bitcast.65), calls=%async_computation | async-start | bytes 4194304 | tf_op jit(solution)/shard_map/all_to_all | solution.py:327
  106.0 39.5 %all-to-all-start.1 = ((bf16[32,144,256]{2,1,0:T(8,128)(2,1)}), bf16[32,144,256]{2,1,0:T(8,128)(2,1)}, u32[]{:S(2)}, u32[]{:S(2)}) async-start(bf16[32,144,256]{2,1,0:T(8,128)(2,1)} %fusion.8), calls=%async_computation.1 | async-start | bytes 4718592 | tf_op jit(solution)/shard_map/all_to_all | solution.py:354
  116.3 79.5 %reduce-scatter.2.cloned.1.call-start = ((), (), s32[]{:S(2)}) async-start(), calls=%async_computation.4 | async-start | bytes 2359296 | tf_op jit(solution)/shard_map/reduce_scatter | solution.py:379
Sparse Core Ops, SparseCore 0:
  9.1 43.7 all-gather.1
  155.9 39.7 reduce-scatter.1

commit v13 on v10

--- a/solution.py
+++ b/solution.py
@@ -252,12 +252,7 @@
     all_slots = max(REQ_DEV // TENANTS, node_slots)
     block = REQ_LEN * width_local
     columns = lax.all_gather(activations, "mp", axis=1, tiled=True)
-    query_f, key_f, value_f = tuple(
-        (
-            jnp.dot(columns, matrix, preferred_element_type=jnp.float32)
-            for matrix in (w_query, w_key, w_value)
-        )
-    )
+    query_f = jnp.dot(columns, w_query, preferred_element_type=jnp.float32)
     middle_all = lookup(parent, req_leaf)
     root_all = lookup(parent, middle_all)
     len_of = lambda nodes: lookup(node_len, nodes)
@@ -267,14 +262,7 @@
         tok_rows
     )
     queries = rotate(query_f.reshape(tok_rows, heads_local, HD), position).astype(jnp.bfloat16)
-    keys = rotate(key_f.reshape(tok_rows, heads_local, HD), position).astype(jnp.bfloat16)
-    values = value_f.astype(jnp.bfloat16)
     q_blocks = queries.reshape(REQ_DEV, block)
-    self_out, self_lse = self_attention(
-        queries.reshape(REQ_DEV, REQ_LEN, heads_local, HD),
-        keys.reshape(REQ_DEV, REQ_LEN, heads_local, HD),
-        values.reshape(REQ_DEV, REQ_LEN, heads_local, HD),
-    )
     levels_all = jnp.stack([root_all, middle_all, req_leaf], axis=0).reshape(3, leaf_count, REQ_DEV)
     level_count = levels_all.shape[0]
     items = level_count * REQ_DEV
@@ -305,6 +293,18 @@
         axis=1,
     ).reshape(leaf_count, all_slots, REQ_LEN, width_local)
     arrived = lax.all_to_all(outgoing, "leaf", split_axis=0, concat_axis=0, tiled=True)
+    columns_late = lax.optimization_barrier((columns, outgoing))[0]
+    key_f, value_f = (
+        jnp.dot(columns_late, matrix, preferred_element_type=jnp.float32)
+        for matrix in (w_key, w_value)
+    )
+    keys = rotate(key_f.reshape(tok_rows, heads_local, HD), position).astype(jnp.bfloat16)
+    values = value_f.astype(jnp.bfloat16)
+    self_out, self_lse = self_attention(
+        queries.reshape(REQ_DEV, REQ_LEN, heads_local, HD),
+        keys.reshape(REQ_DEV, REQ_LEN, heads_local, HD),
+        values.reshape(REQ_DEV, REQ_LEN, heads_local, HD),
+    )
     recv_hit = (holders[:, None, :] == device) & (ranks[:, None, :] == slot_ids[None, :, None])
     slot_nodes = jnp.sum(jnp.where(recv_hit, per_sender[:, None, :], 0), axis=2).reshape(-1)
     filled = jnp.any(recv_hit, axis=2).reshape(-1)

time: 215 us -> 215 us (level)
  waiting for transfers between devices: 127 us -> 124 us
  starting transfers between devices: 15.6 us -> 18.4 us
    all_to_all x1, waiting for transfers between devices: 23.2 us -> 20 us  [on_device(): lax.all_to_all(payload, 'leaf', split_axis=0, concat_axis=0, tiled=True)]
    all_to_all x1, starting transfers between devices: 7.77 us -> 10.5 us  [on_device(): lax.all_to_all(payload, 'leaf', split_axis=0, concat_axis=0, tiled=True)]
  transfers between devices with their start and end apart: 4 -> 4, of which waited for: 4 -> 4; matrix products, arithmetic and copies ran while one was open for 7% -> 8% of each run, Pallas kernels for 0% -> 0%
where the time goes in v13:
time: 215 us; the launch traced here: 214 us
  waiting for transfers between devices  124 us (58%)
  Pallas kernels  19.1 us (9%)
  starting transfers between devices  18.4 us (9%)
  other arithmetic  18 us (8%)
  between operations  13.8 us (6%)
  matrix products  11.8 us (5%)
  local copies, waits for them, and re-layouts  9.63 us (4%)
    reduce_scatter x1, waiting for transfers between devices, on_device(): lax.psum_scatter(partial_value.astype(jnp.bfloat16), 'mp', scatter_dimens...  39.9 us
    all_gather x1, waiting for transfers between devices, on_device(): columns = lax.all_gather(activations, 'mp', axis=1, tiled=True)  39.3 us
    all_to_all x1, waiting for transfers between devices, on_device(): lax.all_to_all(outgoing, 'leaf', split_axis=0, concat_axis=0, tiled=True)  23.6 us
    all_to_all x1, waiting for transfers between devices, on_device(): lax.all_to_all(payload, 'leaf', split_axis=0, concat_axis=0, tiled=True)  20 us
    all_to_all x1, starting transfers between devices, on_device(): lax.all_to_all(payload, 'leaf', split_axis=0, concat_axis=0, tiled=True)  10.5 us
    pallas_call x1, Pallas kernels, node_attention(): pl.pallas_call(node_kernel, out_shape=(jax.ShapeDtypeStruct((slots // 2,...  10.1 us
    pallas_call x1, Pallas kernels, mp_sum(): pl.pallas_call(sum_kernel, out_shape=jax.ShapeDtypeStruct(x.shape, x.dtyp...  8.94 us
    all_to_all x1, starting transfers between devices, on_device(): lax.all_to_all(outgoing, 'leaf', split_axis=0, concat_axis=0, tiled=True)  7.64 us
  transfers between devices with their start and end apart: 4, of which 4 were waited for; matrix products, arithmetic and copies ran while one was open for 8% of the time, Pallas kernels for 0%

profile of v13, /device:TPU:6, one launch (start us, length us, event | category | flops | bytes accessed | tf_op | source)
XLA Modules:
  0.0 214.3 jit_solution(13133207934190631071)
XLA Ops:
  6.5 0.7 all-gather.2.cloned.1.call-update
  7.3 0.8 stack.14
  8.1 0.9 select_reduce_fusion.5
  9.2 0.9 select_reduce_fusion.4
  10.9 0.2 dynamic-slice_reduce_fusion.1
  11.1 0.2 dynamic-slice_reduce_fusion
  12.0 0.9 select_reduce_fusion.2
  13.3 0.3 multiply_cosine_fusion
  13.6 39.3 %all-gather.2.cloned.1.call-done = bf16[256,4096]{1,0:T(8,128)(2,1)} async-done(((bf16[256,512]{1,0:T(8,128)(2,1)}), bf16[256,4096]{1,0:T(8,128)(2,1)}) %all-gather.2.cloned.1.call-update) | async-done | bytes 2097168 | tf_op jit(solution)/shard_map/all_gather | solution.py:254
  52.9 3.1 %fusion.47 = f32[256,256]{0,1:T(8,128)S(1)} fusion(bf16[256,4096]{1,0:T(8,128)(2,1)} %all-gather.2.cloned.1.call-done, bf16[4096,256]{1,0:T(8,128)(2,1)} %param.12), kind=kOutput, calls=%fused_computation.123 | convolution fusion | flops 536870912 | bytes 4456448 | tf_op jit(solution)/shard_map/dot_general | solution.py:255
  56.4 2.4 %select_reduce_fusion = bf16[64,64,256]{2,1,0:T(8,128)(2,1)} fusion(pred[64,4]{1,0:T(8,128)(4,1)S(1)} %fusion.29, bf16[4,64,256]{2,1,0:T(8,128)(2,1)S(1)} %convert_element_type.81), kind=kLoop, calls=%fused_computation.1 | loop fusion | flops 7340032 | bytes 2228480 | tf_op jit(solution)/shard_map/reduce_sum | solution.py:287
  58.7 7.6 %all-to-all-start = ((bf16[32,2,64,256]{3,2,1,0:T(8,128)(2,1)}), bf16[32,2,64,256]{3,2,1,0:T(8,128)(2,1)}, u32[]{:S(2)}, u32[]{:S(2)}) async-start(bf16[32,2,64,256]{3,2,1,0:T(8,128)(2,1)} %bitcast.65), calls=%async_computation | async-start | bytes 4194304 | tf_op jit(solution)/shard_map/all_to_all | solution.py:295
  66.4 0.6 dynamic_slice.15.nlen_ref
  67.0 0.7 convert_reduce_fusion.4
  67.7 0.7 convert_reduce_fusion.2
  68.4 0.2 convert_reduce_fusion.1
  68.5 0.6 select_reduce_fusion.6.perm_ref
  69.2 23.6 %all-to-all-done = bf16[32,2,64,256]{3,2,1,0:T(8,128)(2,1)} async-done(((bf16[32,2,64,256]{3,2,1,0:T(8,128)(2,1)}), bf16[32,2,64,256]{3,2,1,0:T(8,128)(2,1)}, u32[]{:S(2)}, u32[]{:S(2)}) %all-to-all-start) | async-done | bytes 2097184 | tf_op jit(solution)/shard_map/all_to_all | solution.py:295
  92.8 10.1 %shard_map.109 = (bf16[32,144,256]{2,1,0:T(8,128)(2,1)}, f32[64,128]{1,0:T(8,128)}) custom-call(s32[64]{0:T(128)} %select_reduce_fusion.6.perm_ref, s32[8]{0:T(128)} %get-tuple-element.12.start_ref, s32[8]{0:T(128)} %get-tuple-element.11.count_ref, s32[8]{0:T(128)} %dynamic_slice.15.nlen_ref, s32[1]{0:T(128)} %bitcast.1.total_ref, ...), custom_call_target="tpu_custom_call" | custom-call | flops 1073741824 | bytes 6291456 | tf_op jit(solution)/shard_map/pallas_call | solution.py:148
  102.9 0.8 reduce-precision_convert_fusion
  103.7 0.8 fusion.12
  104.4 10.5 %all-to-all-start.1 = ((bf16[32,144,256]{2,1,0:T(8,128)(2,1)}), bf16[32,144,256]{2,1,0:T(8,128)(2,1)}, u32[]{:S(2)}, u32[]{:S(2)}) async-start(bf16[32,144,256]{2,1,0:T(8,128)(2,1)} %fusion.12), calls=%async_computation.1 | async-start | bytes 4718592 | tf_op jit(solution)/shard_map/all_to_all | solution.py:334
  114.9 0.2 reduce-scatter.2.cloned.1.call-start
  115.4 0.1 concatenate.50
  115.5 3.2 %fusion.48 = f32[256,256]{0,1:T(8,128)S(1)} fusion(bf16[256,4096]{1,0:T(8,128)(2,1)} %all-gather.2.cloned.1.call-done, bf16[4096,256]{1,0:T(8,128)(2,1)} %param.13), kind=kOutput, calls=%fused_computation.124 | convolution fusion | flops 536870912 | bytes 4456448 | tf_op jit(solution)/shard_map/dot_general | solution.py:298
  118.8 0.1 copy.144
  119.0 0.1 concatenate.53
  119.1 0.1 copy.143
  119.2 0.1 copy.142
  119.4 0.1 copy.141
  119.5 2.9 %convolution_convert_fusion.1 = bf16[256,256]{1,0:T(8,128)(2,1)S(1)} fusion(bf16[256,4096]{1,0:T(8,128)(2,1)} %all-gather.2.cloned.1.call-done, bf16[4096,256]{1,0:T(8,128)(2,1)} %param.14), kind=kOutput, calls=%fused_computation.8 | convolution fusion | flops 536936448 | bytes 4325376 | tf_op jit(solution)/shard_map/dot_general | solution.py:298
  122.5 0.3 fusion.46
  122.9 0.2 fusion.2
  123.1 0.9 copy.151
  124.1 20.0 %all-to-all-done.1 = bf16[32,144,256]{2,1,0:T(8,128)(2,1)} async-done(((bf16[32,144,256]{2,1,0:T(8,128)(2,1)}), bf16[32,144,256]{2,1,0:T(8,128)(2,1)}, u32[]{:S(2)}, u32[]{:S(2)}) %all-to-all-start.1) | async-done | bytes 2359328 | tf_op jit(solution)/shard_map/all_to_all | solution.py:334
  144.1 2.3 %gather_fusion = bf16[12,144,256]{2,1,0:T(8,128)(2,1)S(1)} fusion(bf16[32,144,256]{2,1,0:T(8,128)(2,1)} %all-to-all-done.1, s32[1024]{0:T(1024)S(1)} %pad_clamp_fusion), kind=kCustom, calls=%fused_computation | custom fusion | bytes 1769520 | tf_op jit(solution)/shard_map/jit(_take)/gather | solution.py:335
  146.4 0.1 broadcast_select_fusion
  146.5 1.0 fusion.10
  147.6 1.5 reshape.468
  149.3 0.2 copy.148
  149.7 2.3 %fusion.3 = f32[4,64,2,128]{3,2,1,0:T(2,128)S(1)} fusion(f32[1,4,64,2,128]{4,3,2,1,0:T(2,128)} %copy.151, f32[3,4,64,2,128]{4,3,2,1,0:T(2,128)S(1)} %reshape.468, f32[4,4,64,2]{3,2,1,0:T(8,128)S(1)} %copy.148), kind=kLoop, calls=%fused_computation.10 | loop fusion | flops 720896 | bytes 1318912 | tf_op jit(solution)/shard_map/reduce_sum | solution.py:356
  152.0 0.3 divide_convert_fusion
  152.4 2.1 convolution_convert_fusion
  154.5 39.9 %reduce-scatter.2.cloned.1.call-done = bf16[256,512]{1,0:T(8,128)(2,1)} async-done(((bf16[256,4096]{1,0:T(8,128)(2,1)}), bf16[256,512]{1,0:T(8,128)(2,1)}) %reduce-scatter.2.cloned.1.call-update) | async-done | bytes 262160 | tf_op jit(solution)/shard_map/reduce_scatter | solution.py:359
  194.4 1.6 fusion.7
  196.0 8.9 %shard_map.110 = f32[1,256]{1,0:T(1,128)} custom-call(f32[1,256]{1,0:T(1,128)} %bitcast.75), custom_call_target="tpu_custom_call" | custom-call | tf_op jit(solution)/shard_map/pallas_call | solution.py:198
  205.0 0.7 add_rsqrt_fusion
  205.7 1.8 fusion.6
  (67 shorter events, 3.2 us)
Async XLA Ops:
  6.5 145.8 %copy-start = (bf16[256,4096]{1,0:T(8,128)(2,1)S(1)}, bf16[256,4096]{1,0:T(8,128)(2,1)}, u32[]{:S(2)}) copy-start(bf16[256,4096]{1,0:T(8,128)(2,1)} %param.15) | copy-start | bytes 6291460
  6.5 46.4 %all-gather.2.cloned.1.call-start = ((), (), s32[]{:S(2)}) async-start(), calls=%async_computation.3 | async-start | bytes 2359296 | tf_op jit(solution)/shard_map/all_gather | solution.py:254
  58.7 7.6 %copy-start.3 = (s32[256]{0:T(256)S(1)}, s32[256]{0:T(256)}, u32[]{:S(2)}) copy-start(s32[256]{0:T(256)} %param.20) | copy-start | bytes 3076
  58.7 34.0 %all-to-all-start = ((bf16[32,2,64,256]{3,2,1,0:T(8,128)(2,1)}), bf16[32,2,64,256]{3,2,1,0:T(8,128)(2,1)}, u32[]{:S(2)}, u32[]{:S(2)}) async-start(bf16[32,2,64,256]{3,2,1,0:T(8,128)(2,1)} %bitcast.65), calls=%async_computation | async-start | bytes 4194304 | tf_op jit(solution)/shard_map/all_to_all | solution.py:295
  104.4 39.7 %all-to-all-start.1 = ((bf16[32,144,256]{2,1,0:T(8,128)(2,1)}), bf16[32,144,256]{2,1,0:T(8,128)(2,1)}, u32[]{:S(2)}, u32[]{:S(2)}) async-start(bf16[32,144,256]{2,1,0:T(8,128)(2,1)} %fusion.12), calls=%async_computation.1 | async-start | bytes 4718592 | tf_op jit(solution)/shard_map/all_to_all | solution.py:334
  114.9 79.5 %reduce-scatter.2.cloned.1.call-start = ((), (), s32[]{:S(2)}) async-start(), calls=%async_computation.4 | async-start | bytes 2359296 | tf_op jit(solution)/shard_map/reduce_scatter | solution.py:359
  154.4 51.2 %copy-start.1 = (bf16[256,512]{1,0:T(8,128)(2,1)S(1)}, bf16[256,512]{1,0:T(8,128)(2,1)}, u32[]{:S(2)}) copy-start(bf16[256,512]{1,0:T(8,128)(2,1)} %param.11) | copy-start | bytes 786436
  154.4 51.2 %copy-start.2 = (f32[512]{0:T(512)S(1)}, f32[512]{0:T(512)}, u32[]{:S(2)}) copy-start(f32[512]{0:T(512)} %param.16) | copy-start | bytes 6148
Sparse Core Ops, SparseCore 0:
  9.1 43.7 all-gather.1
  154.6 39.7 reduce-scatter.1

commit v14 on v13

--- a/solution.py
+++ b/solution.py
@@ -336,7 +336,6 @@
     second = (my_ranks == 1)[:, None, None]
     got_out = (
         jnp.where(second, got[:, REQ_LEN : 2 * REQ_LEN], got[:, :REQ_LEN])
-        .astype(jnp.float32)
         .reshape(level_count, REQ_DEV, REQ_LEN, heads_local, HD)
     )
     lse_at = all_slots * REQ_LEN
@@ -349,11 +348,13 @@
         1,
         2,
     ).reshape(level_count, REQ_DEV, REQ_LEN, heads_local)
-    partial_out = jnp.concatenate([got_out, self_out[None]], axis=0)
     partial_lse = jnp.concatenate([got_lse, self_lse[None]], axis=0)
     highest = jnp.max(partial_lse, axis=0)
     factor = jnp.exp(partial_lse - highest[None])
-    merged = jnp.sum(factor[..., None] * partial_out, axis=0) / jnp.sum(factor, axis=0)[..., None]
+    weighted = factor[3][..., None] * self_out
+    for level in range(level_count):
+        weighted = weighted + factor[level][..., None] * got_out[level].astype(jnp.float32)
+    merged = weighted / jnp.sum(factor, axis=0)[..., None]
     attn = merged.astype(jnp.bfloat16).reshape(tok_rows, width_local)
     partial_value = jnp.dot(attn, w_out, preferred_element_type=jnp.float32)
     projected = lax.psum_scatter(

time: 215 us -> 211 us (0.981)
  starting transfers between devices: 18.4 us -> 13 us
  Pallas kernels: 19.1 us -> 23.7 us
  other arithmetic: 18 us -> 14.5 us
  local copies, waits for them, and re-layouts: 9.63 us -> 6.98 us
    all_to_all x1, starting transfers between devices: 10.5 us -> 5.28 us  [on_device(): lax.all_to_all(payload, 'leaf', split_axis=0, concat_axis=0, tiled=True)]
    pallas_call x1, Pallas kernels: 10.1 us -> 14.7 us  [node_attention(): pl.pallas_call(node_kernel, out_shape=(jax.ShapeDtypeStruct((slots // 2,...]
    reduce_sum x2 -> x1, other arithmetic: 2.32 us -> 0.04 us  [on_device(): merged = weighted / jnp.sum(factor, axis=0)[..., None]]
where the time goes in v14:
time: 211 us; the launch traced here: 209 us
  waiting for transfers between devices  125 us (59%)
  Pallas kernels  23.7 us (11%)
  other arithmetic  14.5 us (7%)
  between operations  13.8 us (7%)
  starting transfers between devices  13 us (6%)
  matrix products  12.2 us (6%)
  local copies, waits for them, and re-layouts  6.98 us (3%)
    reduce_scatter x1, waiting for transfers between devices, on_device(): lax.psum_scatter(partial_value.astype(jnp.bfloat16), 'mp', scatter_dimens...  39.9 us
    all_gather x1, waiting for transfers between devices, on_device(): columns = lax.all_gather(activations, 'mp', axis=1, tiled=True)  39.3 us
    all_to_all x1, waiting for transfers between devices, on_device(): lax.all_to_all(outgoing, 'leaf', split_axis=0, concat_axis=0, tiled=True)  23.6 us
    all_to_all x1, waiting for transfers between devices, on_device(): lax.all_to_all(payload, 'leaf', split_axis=0, concat_axis=0, tiled=True)  21.4 us
    pallas_call x1, Pallas kernels, node_attention(): pl.pallas_call(node_kernel, out_shape=(jax.ShapeDtypeStruct((slots // 2,...  14.7 us
    pallas_call x1, Pallas kernels, mp_sum(): pl.pallas_call(sum_kernel, out_shape=jax.ShapeDtypeStruct(x.shape, x.dtyp...  8.94 us
    all_to_all x1, starting transfers between devices, on_device(): lax.all_to_all(outgoing, 'leaf', split_axis=0, concat_axis=0, tiled=True)  7.64 us
    dot_general x2, matrix products, on_device(): jnp.dot(columns_late, matrix, preferred_element_type=jnp.float32)  6.08 us
  transfers between devices with their start and end apart: 4, of which 4 were waited for; matrix products, arithmetic and copies ran while one was open for 8% of the time, Pallas kernels for 0%

profile of v14, /device:TPU:6, one launch (start us, length us, event | category | flops | bytes accessed | tf_op | source)
XLA Modules:
  0.0 209.1 jit_solution(15392989134246031910)
XLA Ops:
  6.5 0.7 all-gather.2.cloned.1.call-update
  7.3 0.8 stack.14
  8.0 0.9 select_reduce_fusion.5
  9.0 0.9 select_reduce_fusion.4
  10.0 0.9 select_reduce_fusion.2
  11.4 0.2 dynamic-slice_reduce_fusion
  11.6 0.1 convert_reduce_fusion
  11.7 0.2 dynamic-slice_reduce_fusion.1
  12.3 0.1 and.121
  12.5 0.1 reshape.449
  13.3 0.3 multiply_cosine_fusion
  13.6 39.3 %all-gather.2.cloned.1.call-done = bf16[256,4096]{1,0:T(8,128)(2,1)} async-done(((bf16[256,512]{1,0:T(8,128)(2,1)}), bf16[256,4096]{1,0:T(8,128)(2,1)}) %all-gather.2.cloned.1.call-update) | async-done | bytes 2097168 | tf_op jit(solution)/shard_map/all_gather | solution.py:254
  52.9 3.1 %fusion.50 = f32[256,256]{0,1:T(8,128)S(1)} fusion(bf16[256,4096]{1,0:T(8,128)(2,1)} %all-gather.2.cloned.1.call-done, bf16[4096,256]{1,0:T(8,128)(2,1)} %param.12), kind=kOutput, calls=%fused_computation.134 | convolution fusion | flops 536870912 | bytes 4456448 | tf_op jit(solution)/shard_map/dot_general | solution.py:255
  56.2 0.1 copy.98
  56.4 2.4 %select_reduce_fusion = bf16[64,64,256]{2,1,0:T(8,128)(2,1)} fusion(pred[64,4]{1,0:T(8,128)(4,1)S(1)} %fusion.32, bf16[4,64,256]{2,1,0:T(8,128)(2,1)S(1)} %convert_element_type.94), kind=kLoop, calls=%fused_computation.1 | loop fusion | flops 7340032 | bytes 2228480 | tf_op jit(solution)/shard_map/reduce_sum | solution.py:287
  58.7 7.6 %all-to-all-start = ((bf16[32,2,64,256]{3,2,1,0:T(8,128)(2,1)}), bf16[32,2,64,256]{3,2,1,0:T(8,128)(2,1)}, u32[]{:S(2)}, u32[]{:S(2)}) async-start(bf16[32,2,64,256]{3,2,1,0:T(8,128)(2,1)} %bitcast.99), calls=%async_computation | async-start | bytes 4194304 | tf_op jit(solution)/shard_map/all_to_all | solution.py:295
  66.4 0.6 dynamic_slice.15.nlen_ref
  67.0 0.7 convert_reduce_fusion.4
  67.7 0.7 convert_reduce_fusion.2
  68.4 0.2 convert_reduce_fusion.1
  68.5 0.6 select_reduce_fusion.6.perm_ref
  69.2 23.6 %all-to-all-done = bf16[32,2,64,256]{3,2,1,0:T(8,128)(2,1)} async-done(((bf16[32,2,64,256]{3,2,1,0:T(8,128)(2,1)}), bf16[32,2,64,256]{3,2,1,0:T(8,128)(2,1)}, u32[]{:S(2)}, u32[]{:S(2)}) %all-to-all-start) | async-done | bytes 2097184 | tf_op jit(solution)/shard_map/all_to_all | solution.py:295
  92.8 14.7 %shard_map.109 = (bf16[32,144,256]{2,1,0:T(8,128)(2,1)}, f32[64,128]{1,0:T(8,128)}) custom-call(s32[64]{0:T(128)} %select_reduce_fusion.6.perm_ref, s32[8]{0:T(128)} %get-tuple-element.15.start_ref, s32[8]{0:T(128)} %get-tuple-element.14.count_ref, s32[8]{0:T(128)} %dynamic_slice.15.nlen_ref, s32[1]{0:T(128)} %bitcast.1.total_ref, ...), custom_call_target="tpu_custom_call" | custom-call | flops 1073741824 | bytes 6291456 | tf_op jit(solution)/shard_map/pallas_call | solution.py:148
  107.5 0.8 reduce-precision_convert_fusion
  108.3 0.8 fusion.15
  109.1 5.3 %all-to-all-start.1 = ((bf16[32,144,256]{2,1,0:T(8,128)(2,1)}), bf16[32,144,256]{2,1,0:T(8,128)(2,1)}, u32[]{:S(2)}, u32[]{:S(2)}) async-start(bf16[32,144,256]{2,1,0:T(8,128)(2,1)} %fusion.15), calls=%async_computation.1 | async-start | bytes 4718592 | tf_op jit(solution)/shard_map/all_to_all | solution.py:334
  114.5 0.1 concatenate.38
  114.6 0.1 concatenate.39
  114.7 0.1 copy.99
  114.9 0.1 copy.100
  115.0 2.9 %convolution_convert_fusion.1 = bf16[256,256]{1,0:T(8,128)(2,1)S(1)} fusion(bf16[256,4096]{1,0:T(8,128)(2,1)} %all-gather.2.cloned.1.call-done, bf16[4096,256]{1,0:T(8,128)(2,1)} %param.14), kind=kOutput, calls=%fused_computation.13 | convolution fusion | flops 536936448 | bytes 4325376 | tf_op jit(solution)/shard_map/dot_general | solution.py:298
  118.0 3.1 %fusion.51 = f32[256,256]{0,1:T(8,128)S(1)} fusion(bf16[256,4096]{1,0:T(8,128)(2,1)} %all-gather.2.cloned.1.call-done, bf16[4096,256]{1,0:T(8,128)(2,1)} %param.13), kind=kOutput, calls=%fused_computation.135 | convolution fusion | flops 536870912 | bytes 4456448 | tf_op jit(solution)/shard_map/dot_general | solution.py:298
  121.2 0.1 concatenate.41
  121.3 0.1 copy.101
  121.5 0.1 concatenate.42
  121.6 0.1 copy.102
  121.8 0.3 fusion.49
  122.1 21.4 %all-to-all-done.1 = bf16[32,144,256]{2,1,0:T(8,128)(2,1)} async-done(((bf16[32,144,256]{2,1,0:T(8,128)(2,1)}), bf16[32,144,256]{2,1,0:T(8,128)(2,1)}, u32[]{:S(2)}, u32[]{:S(2)}) %all-to-all-start.1) | async-done | bytes 2359328 | tf_op jit(solution)/shard_map/all_to_all | solution.py:334
  143.5 2.3 %gather_fusion = bf16[12,144,256]{2,1,0:T(8,128)(2,1)S(1)} fusion(bf16[32,144,256]{2,1,0:T(8,128)(2,1)} %all-to-all-done.1, s32[1024]{0:T(1024)S(1)} %pad_clamp_fusion), kind=kCustom, calls=%fused_computation | custom fusion | bytes 1769520 | tf_op jit(solution)/shard_map/jit(_take)/gather | solution.py:335
  145.8 0.1 broadcast_select_fusion
  146.4 0.6 fusion.7
  147.0 0.1 copy.108
  147.1 2.1 convolution_convert_fusion
  149.2 39.9 %reduce-scatter.2.cloned.1.call-done = bf16[256,512]{1,0:T(8,128)(2,1)} async-done(((bf16[256,4096]{1,0:T(8,128)(2,1)}), bf16[256,512]{1,0:T(8,128)(2,1)}) %reduce-scatter.2.cloned.1.call-update) | async-done | bytes 262160 | tf_op jit(solution)/shard_map/reduce_scatter | solution.py:360
  189.2 1.6 fusion.11
  190.8 8.9 %shard_map.110 = f32[1,256]{1,0:T(1,128)} custom-call(f32[1,256]{1,0:T(1,128)} %bitcast.109), custom_call_target="tpu_custom_call" | custom-call | tf_op jit(solution)/shard_map/pallas_call | solution.py:198
  199.8 0.7 add_rsqrt_fusion
  200.4 1.8 fusion.10
  (61 shorter events, 2.6 us)
Async XLA Ops:
  6.5 140.6 %copy-start = (bf16[256,4096]{1,0:T(8,128)(2,1)S(1)}, bf16[256,4096]{1,0:T(8,128)(2,1)}, u32[]{:S(2)}) copy-start(bf16[256,4096]{1,0:T(8,128)(2,1)} %param.15) | copy-start | bytes 6291460
  6.5 46.4 %all-gather.2.cloned.1.call-start = ((), (), s32[]{:S(2)}) async-start(), calls=%async_computation.3 | async-start | bytes 2359296 | tf_op jit(solution)/shard_map/all_gather | solution.py:254
  58.7 7.6 %copy-start.3 = (s32[256]{0:T(256)S(1)}, s32[256]{0:T(256)}, u32[]{:S(2)}) copy-start(s32[256]{0:T(256)} %param.20) | copy-start | bytes 3076
  58.7 34.0 %all-to-all-start = ((bf16[32,2,64,256]{3,2,1,0:T(8,128)(2,1)}), bf16[32,2,64,256]{3,2,1,0:T(8,128)(2,1)}, u32[]{:S(2)}, u32[]{:S(2)}) async-start(bf16[32,2,64,256]{3,2,1,0:T(8,128)(2,1)} %bitcast.99), calls=%async_computation | async-start | bytes 4194304 | tf_op jit(solution)/shard_map/all_to_all | solution.py:295
  109.1 34.4 %all-to-all-start.1 = ((bf16[32,144,256]{2,1,0:T(8,128)(2,1)}), bf16[32,144,256]{2,1,0:T(8,128)(2,1)}, u32[]{:S(2)}, u32[]{:S(2)}) async-start(bf16[32,144,256]{2,1,0:T(8,128)(2,1)} %fusion.15), calls=%async_computation.1 | async-start | bytes 4718592 | tf_op jit(solution)/shard_map/all_to_all | solution.py:334
  114.4 74.8 %reduce-scatter.2.cloned.1.call-start = ((), (), s32[]{:S(2)}) async-start(), calls=%async_computation.4 | async-start | bytes 2359296 | tf_op jit(solution)/shard_map/reduce_scatter | solution.py:360
  149.2 51.2 %copy-start.1 = (bf16[256,512]{1,0:T(8,128)(2,1)S(1)}, bf16[256,512]{1,0:T(8,128)(2,1)}, u32[]{:S(2)}) copy-start(bf16[256,512]{1,0:T(8,128)(2,1)} %param.11) | copy-start | bytes 786436
  149.2 51.2 %copy-start.2 = (f32[512]{0:T(512)S(1)}, f32[512]{0:T(512)}, u32[]{:S(2)}) copy-start(f32[512]{0:T(512)} %param.16) | copy-start | bytes 6148
Sparse Core Ops, SparseCore 0:
  9.1 43.7 all-gather.1
  149.3 39.7 reduce-scatter.1

commit v15 on v14

--- a/solution.py
+++ b/solution.py
@@ -334,10 +334,9 @@
     back = lax.all_to_all(payload, "leaf", split_axis=0, concat_axis=0, tiled=True)
     got = jnp.take(back, my_holders, axis=0)
     second = (my_ranks == 1)[:, None, None]
-    got_out = (
-        jnp.where(second, got[:, REQ_LEN : 2 * REQ_LEN], got[:, :REQ_LEN])
-        .reshape(level_count, REQ_DEV, REQ_LEN, heads_local, HD)
-    )
+    got_out = jax.vmap(
+        lambda h, r: lax.dynamic_slice(back, (h, r * REQ_LEN, 0), (1, REQ_LEN, width_local))[0]
+    )(my_holders, my_ranks).reshape(level_count, REQ_DEV, REQ_LEN, heads_local, HD)
     lse_at = all_slots * REQ_LEN
     got_pair = jnp.where(
         second[:, 0], got[:, lse_at + 1, :pair_width], got[:, lse_at, :pair_width]

time: 211 us -> 217 us (1.028)
  local copies, waits for them, and re-layouts: 6.98 us -> 13.5 us
  starting transfers between devices: 13 us -> 17.2 us
  Pallas kernels: 23.7 us -> 20.2 us
    all_to_all x1, starting transfers between devices: 5.28 us -> 9.38 us  [on_device(): lax.all_to_all(payload, 'leaf', split_axis=0, concat_axis=0, tiled=True)]
    all_to_all x0 -> x1, local copies, waits for them, and re-layouts: none -> 3.89 us  [on_device(): lax.all_to_all(payload, 'leaf', split_axis=0, concat_axis=0, tiled=True)]
    pallas_call x1, Pallas kernels: 14.7 us -> 11.2 us  [node_attention(): pl.pallas_call(node_kernel, out_shape=(jax.ShapeDtypeStruct((slots // 2,...]
    gather x0 -> x1, local copies, waits for them, and re-layouts: none -> 2.66 us  [on_device(): lax.dynamic_slice(back, (h, r * REQ_LEN, 0), (1, REQ_LEN, width_local))[0]]
where the time goes in v15:
time: 217 us; the launch traced here: 216 us
  waiting for transfers between devices  125 us (58%)
  Pallas kernels  20.2 us (9%)
  starting transfers between devices  17.2 us (8%)
  other arithmetic  14.5 us (7%)
  between operations  13.8 us (6%)
  local copies, waits for them, and re-layouts  13.5 us (6%)
  matrix products  12.2 us (6%)
    reduce_scatter x1, waiting for transfers between devices, on_device(): lax.psum_scatter(partial_value.astype(jnp.bfloat16), 'mp', scatter_dimens...  40 us
    all_gather x1, waiting for transfers between devices, on_device(): columns = lax.all_gather(activations, 'mp', axis=1, tiled=True)  39.3 us
    all_to_all x1, waiting for transfers between devices, on_device(): lax.all_to_all(outgoing, 'leaf', split_axis=0, concat_axis=0, tiled=True)  23.6 us
    all_to_all x1, waiting for transfers between devices, on_device(): lax.all_to_all(payload, 'leaf', split_axis=0, concat_axis=0, tiled=True)  21.2 us
    pallas_call x1, Pallas kernels, node_attention(): pl.pallas_call(node_kernel, out_shape=(jax.ShapeDtypeStruct((slots // 2,...  11.2 us
    all_to_all x1, starting transfers between devices, on_device(): lax.all_to_all(payload, 'leaf', split_axis=0, concat_axis=0, tiled=True)  9.38 us
    pallas_call x1, Pallas kernels, mp_sum(): pl.pallas_call(sum_kernel, out_shape=jax.ShapeDtypeStruct(x.shape, x.dtyp...  8.94 us
    all_to_all x1, starting transfers between devices, on_device(): lax.all_to_all(outgoing, 'leaf', split_axis=0, concat_axis=0, tiled=True)  7.64 us
  transfers between devices with their start and end apart: 4, of which 4 were waited for; matrix products, arithmetic and copies ran while one was open for 8% of the time, Pallas kernels for 0%

profile of v15, /device:TPU:6, one launch (start us, length us, event | category | flops | bytes accessed | tf_op | source)
XLA Modules:
  0.0 216.2 jit_solution(9822356547075923869)
XLA Ops:
  6.5 0.7 all-gather.2.cloned.1.call-update
  7.3 0.8 stack.14
  8.1 0.9 select_reduce_fusion.5
  9.2 0.9 select_reduce_fusion.4
  10.9 0.2 dynamic-slice_reduce_fusion
  11.1 0.2 multiply_reduce_fusion
  11.9 0.1 and.121
  12.0 0.9 select_reduce_fusion.2
  13.3 0.3 multiply_cosine_fusion
  13.6 39.3 %all-gather.2.cloned.1.call-done = bf16[256,4096]{1,0:T(8,128)(2,1)} async-done(((bf16[256,512]{1,0:T(8,128)(2,1)}), bf16[256,4096]{1,0:T(8,128)(2,1)}) %all-gather.2.cloned.1.call-update) | async-done | bytes 2097168 | tf_op jit(solution)/shard_map/all_gather | solution.py:254
  52.9 3.1 %fusion.55 = f32[256,256]{0,1:T(8,128)S(1)} fusion(bf16[256,4096]{1,0:T(8,128)(2,1)} %all-gather.2.cloned.1.call-done, bf16[4096,256]{1,0:T(8,128)(2,1)} %param.12), kind=kOutput, calls=%fused_computation.141 | convolution fusion | flops 536870912 | bytes 4456448 | tf_op jit(solution)/shard_map/dot_general | solution.py:255
  56.2 0.1 copy.136
  56.4 2.4 %select_reduce_fusion = bf16[64,64,256]{2,1,0:T(8,128)(2,1)} fusion(pred[64,4]{1,0:T(8,128)(4,1)S(1)} %fusion.32, bf16[4,64,256]{2,1,0:T(8,128)(2,1)S(1)} %convert_element_type.94), kind=kLoop, calls=%fused_computation.2 | loop fusion | flops 7340032 | bytes 2228480 | tf_op jit(solution)/shard_map/reduce_sum | solution.py:287
  58.7 7.6 %all-to-all-start = ((bf16[32,2,64,256]{3,2,1,0:T(8,128)(2,1)}), bf16[32,2,64,256]{3,2,1,0:T(8,128)(2,1)}, u32[]{:S(2)}, u32[]{:S(2)}) async-start(bf16[32,2,64,256]{3,2,1,0:T(8,128)(2,1)} %bitcast.112), calls=%async_computation | async-start | bytes 4194304 | tf_op jit(solution)/shard_map/all_to_all | solution.py:295
  66.4 0.6 dynamic_slice.15.nlen_ref
  67.0 0.7 convert_reduce_fusion.4
  67.7 0.7 convert_reduce_fusion.2
  68.4 0.2 convert_reduce_fusion.1
  68.5 0.6 select_reduce_fusion.6.perm_ref
  69.2 23.6 %all-to-all-done = bf16[32,2,64,256]{3,2,1,0:T(8,128)(2,1)} async-done(((bf16[32,2,64,256]{3,2,1,0:T(8,128)(2,1)}), bf16[32,2,64,256]{3,2,1,0:T(8,128)(2,1)}, u32[]{:S(2)}, u32[]{:S(2)}) %all-to-all-start) | async-done | bytes 2097184 | tf_op jit(solution)/shard_map/all_to_all | solution.py:295
  92.8 11.2 %shard_map.109 = (bf16[32,144,256]{2,1,0:T(8,128)(2,1)}, f32[64,128]{1,0:T(8,128)}) custom-call(s32[64]{0:T(128)} %select_reduce_fusion.6.perm_ref, s32[8]{0:T(128)} %get-tuple-element.17.start_ref, s32[8]{0:T(128)} %get-tuple-element.16.count_ref, s32[8]{0:T(128)} %dynamic_slice.15.nlen_ref, s32[1]{0:T(128)} %bitcast.1.total_ref, ...), custom_call_target="tpu_custom_call" | custom-call | flops 1073741824 | bytes 6291456 | tf_op jit(solution)/shard_map/pallas_call | solution.py:148
  104.0 0.8 reduce-precision_convert_fusion
  104.8 0.8 fusion.15
  105.5 9.4 %all-to-all-start.1 = ((bf16[32,144,256]{2,1,0:T(8,128)(2,1)}), bf16[32,144,256]{2,1,0:T(8,128)(2,1)}, u32[]{:S(2)}, u32[]{:S(2)}) async-start(bf16[32,144,256]{2,1,0:T(8,128)(2,1)} %fusion.15), calls=%async_computation.1 | async-start | bytes 4718592 | tf_op jit(solution)/shard_map/all_to_all | solution.py:334
  114.9 0.2 reduce-scatter.2.cloned.1.call-start
  115.4 0.1 concatenate.41
  115.5 3.2 %fusion.56 = f32[256,256]{0,1:T(8,128)S(1)} fusion(bf16[256,4096]{1,0:T(8,128)(2,1)} %all-gather.2.cloned.1.call-done, bf16[4096,256]{1,0:T(8,128)(2,1)} %param.13), kind=kOutput, calls=%fused_computation.142 | convolution fusion | flops 536870912 | bytes 4456448 | tf_op jit(solution)/shard_map/dot_general | solution.py:298
  118.8 0.1 copy.140
  119.0 0.1 concatenate.44
  119.1 0.1 copy.139
  119.2 0.1 copy.138
  119.4 0.1 copy.137
  119.5 2.9 %convolution_convert_fusion.1 = bf16[256,256]{1,0:T(8,128)(2,1)S(1)} fusion(bf16[256,4096]{1,0:T(8,128)(2,1)} %all-gather.2.cloned.1.call-done, bf16[4096,256]{1,0:T(8,128)(2,1)} %param.14), kind=kOutput, calls=%fused_computation.14 | convolution fusion | flops 536936448 | bytes 4325376 | tf_op jit(solution)/shard_map/dot_general | solution.py:298
  122.5 0.3 fusion.54
  122.9 21.2 %all-to-all-done.1 = bf16[32,144,256]{2,1,0:T(8,128)(2,1)} async-done(((bf16[32,144,256]{2,1,0:T(8,128)(2,1)}), bf16[32,144,256]{2,1,0:T(8,128)(2,1)}, u32[]{:S(2)}, u32[]{:S(2)}) %all-to-all-start.1) | async-done | bytes 2359328 | tf_op jit(solution)/shard_map/all_to_all | solution.py:334
  144.1 2.3 %gather_fusion = bf16[12,144,256]{2,1,0:T(8,128)(2,1)S(1)} fusion(bf16[32,144,256]{2,1,0:T(8,128)(2,1)} %all-to-all-done.1, s32[1024]{0:T(1024)S(1)} %pad_clamp_fusion), kind=kCustom, calls=%fused_computation | custom fusion | bytes 1769520 | tf_op jit(solution)/shard_map/jit(_take)/gather | solution.py:335
  146.4 0.1 broadcast_select_fusion
  146.8 3.9 %copy.143 = bf16[32,144,256]{2,0,1:T(8,128)(2,1)} copy(bf16[32,144,256]{2,1,0:T(8,128)(2,1)} %all-to-all-done.1) | data formatting | bytes 4718592 | tf_op jit(solution)/shard_map/all_to_all | solution.py:334
  150.7 2.7 %gather_fusion.1 = bf16[12,64,256]{2,0,1:T(8,128)(2,1)S(1)} fusion(bf16[32,144,256]{2,0,1:T(8,128)(2,1)} %copy.143, s32[12]{0:T(128)S(1)} %get-tuple-element.44), kind=kCustom, calls=%fused_computation.1 | custom fusion | bytes 786576 | tf_op jit(solution)/shard_map/vmap()/gather | solution.py:338
  153.3 0.1 fusion.53
  153.5 0.6 fusion.7
  154.0 0.1 copy.150
  154.2 2.1 convolution_convert_fusion
  156.3 40.0 %reduce-scatter.2.cloned.1.call-done = bf16[256,512]{1,0:T(8,128)(2,1)} async-done(((bf16[256,4096]{1,0:T(8,128)(2,1)}), bf16[256,512]{1,0:T(8,128)(2,1)}) %reduce-scatter.2.cloned.1.call-update) | async-done | bytes 262160 | tf_op jit(solution)/shard_map/reduce_scatter | solution.py:359
  196.3 1.6 fusion.11
  197.9 8.9 %shard_map.110 = f32[1,256]{1,0:T(1,128)} custom-call(f32[1,256]{1,0:T(1,128)} %bitcast.122), custom_call_target="tpu_custom_call" | custom-call | tf_op jit(solution)/shard_map/pallas_call | solution.py:198
  206.9 0.7 add_rsqrt_fusion
  207.6 1.8 fusion.10
  (62 shorter events, 2.9 us)
Async XLA Ops:
  6.5 147.7 %copy-start = (bf16[256,4096]{1,0:T(8,128)(2,1)S(1)}, bf16[256,4096]{1,0:T(8,128)(2,1)}, u32[]{:S(2)}) copy-start(bf16[256,4096]{1,0:T(8,128)(2,1)} %param.15) | copy-start | bytes 6291460
  6.5 46.4 %all-gather.2.cloned.1.call-start = ((), (), s32[]{:S(2)}) async-start(), calls=%async_computation.3 | async-start | bytes 2359296 | tf_op jit(solution)/shard_map/all_gather | solution.py:254
  58.7 7.6 %copy-start.3 = (s32[256]{0:T(256)S(1)}, s32[256]{0:T(256)}, u32[]{:S(2)}) copy-start(s32[256]{0:T(256)} %param.20) | copy-start | bytes 3076
  58.7 34.0 %all-to-all-start = ((bf16[32,2,64,256]{3,2,1,0:T(8,128)(2,1)}), bf16[32,2,64,256]{3,2,1,0:T(8,128)(2,1)}, u32[]{:S(2)}, u32[]{:S(2)}) async-start(bf16[32,2,64,256]{3,2,1,0:T(8,128)(2,1)} %bitcast.112), calls=%async_computation | async-start | bytes 4194304 | tf_op jit(solution)/shard_map/all_to_all | solution.py:295
  105.5 38.5 %all-to-all-start.1 = ((bf16[32,144,256]{2,1,0:T(8,128)(2,1)}), bf16[32,144,256]{2,1,0:T(8,128)(2,1)}, u32[]{:S(2)}, u32[]{:S(2)}) async-start(bf16[32,144,256]{2,1,0:T(8,128)(2,1)} %fusion.15), calls=%async_computation.1 | async-start | bytes 4718592 | tf_op jit(solution)/shard_map/all_to_all | solution.py:334
  114.9 81.4 %reduce-scatter.2.cloned.1.call-start = ((), (), s32[]{:S(2)}) async-start(), calls=%async_computation.4 | async-start | bytes 2359296 | tf_op jit(solution)/shard_map/reduce_scatter | solution.py:359
  156.3 51.3 %copy-start.1 = (bf16[256,512]{1,0:T(8,128)(2,1)S(1)}, bf16[256,512]{1,0:T(8,128)(2,1)}, u32[]{:S(2)}) copy-start(bf16[256,512]{1,0:T(8,128)(2,1)} %param.11) | copy-start | bytes 786436
  156.3 51.3 %copy-start.2 = (f32[512]{0:T(512)S(1)}, f32[512]{0:T(512)}, u32[]{:S(2)}) copy-start(f32[512]{0:T(512)} %param.16) | copy-start | bytes 6148
Sparse Core Ops, SparseCore 0:
  9.1 43.7 all-gather.1
  156.4 39.8 reduce-scatter.1
